TPU v7x, 32 devices: a whole 2x2x4 slice. The times are simulated.
32 devices in a mesh: grp: 4 (over x, core), row: 8 (over z, y).
Axes of the slice: x: 2, y: 2, z: 4, core: 2. Of those that a mesh axis runs over, the one named last changes fastest.
Arguments:
- signal: bfloat16 [128, 64, 128], P(('grp', 'row')), may hold values from -6 to 6
- leaf_basis: bfloat16 [128, 64, 128], P(('grp', 'row')), may hold values from -0.5 to 0.5
- near_blocks: bfloat16 [128, 3, 128, 128], P(('grp', 'row')), may hold values from -0.3125 to 0.3125
- coupling: bfloat16 [6144, 4096], P(('grp', 'row')), may hold values from -0.109375 to 0.109375
- block_cols: int32 [6144], P(('grp', 'row')), may hold values from 0 to 127, as said below
- block_rows: int32 [6144], P(('grp', 'row')), may hold values from 0 to 3
- block_live: int32 [6144], P(('grp', 'row')), may hold values 0 or 1
Outputs:
- product: bfloat16 [128, 64, 128], P(('grp', 'row'))
Inputs may be any that keep to these rules, and one draw needn't show every extreme that they name: `block_cols`: slot b of device d (d = b // 192, in group h = d // 8) names a column cluster of group (h + o) mod (4), where o = (b mod 192) // 64 - 1; a group's clusters are g * 32 to (g + 1) * 32 - 1.
All inputs are finite; a program needn't handle non-finite values. No bound on the sum of `block_live` on one device may be relied on, other than what follows from the above.
Results may differ from a plain program's by a relative error of at most 0.0039.
Values may be sent and summed in bfloat16 or wider, within the bound.
No kernel may reach another device: no remote copies, remote signals or barrier semaphores. Data moves between devices by JAX's collectives and lax.ppermute only.
A program may use at most 64 MiB of HBM per device.

v0:
```python
import functools

import jax
import jax.numpy as jnp
from jax import lax
from jax.experimental import pallas as pl
from jax.experimental.pallas import tpu as pltpu
from jax.sharding import PartitionSpec as P


K = 64
R = 64
LANES = 128
HALVES = LANES // K
TILES = K // HALVES
PAD = 4


F32 = jnp.float32
BF16 = jnp.bfloat16


def dot_nt(a, b):
    return lax.dot_general(a, b, (((1,), (1,)), ((), ())), preferred_element_type=F32)


def call(kernel, outs, *args, scratch=(), room=0):
    spec = pl.BlockSpec(memory_space=pltpu.VMEM)
    single = len(outs) == 1
    shapes = [pltpu.VMEM(s, d) for s, d in outs]
    return pl.pallas_call(
        kernel,
        out_shape=shapes[0] if single else shapes,
        in_specs=[spec] * len(args),
        out_specs=spec if single else [spec] * len(outs),
        scratch_shapes=scratch,
        compiler_params=pltpu.CompilerParams(vmem_limit_bytes=room + (2 << 20)),
    )(*args)


def skeleton_kernel(signal_ref, basis_ref, out_ref, across_ref, along_ref):
    last = signal_ref.shape[0] - 1
    for pair in range(signal_ref.shape[0] // 2):
        sides = [
            dot_nt(basis_ref[2 * pair + w], signal_ref[2 * pair + w]).astype(BF16) for w in range(2)
        ]
        out_ref[pl.ds(pair * K, K), :] = jnp.concatenate(sides, axis=1)
    odd = (lax.axis_index("row") & 1) == 1
    across_ref[...] = jnp.where(odd, signal_ref[0], signal_ref[last])
    along_ref[...] = jnp.where(odd, signal_ref[last], signal_ref[0])


def operator_kernel(n_grp, n_row, cl_dev, kinds, cols_ref, rows_ref, live_ref, *refs):
    coupling_ref, out_ref, wide_ref = refs
    gc = n_row * cl_dev
    shift = gc.bit_length() - 1
    local = cl_dev.bit_length() - 1
    n_slots = coupling_ref.shape[0]
    group = lax.axis_index("grp")
    row = lax.axis_index("row")
    cols = cols_ref[...]
    delta = (lax.shift_right_logical(cols, shift) - group + n_grp) & (n_grp - 1)
    partner = jnp.where((group & 1) == 0, 1, n_grp - 1)
    kind = jnp.where(delta == 0, 0, jnp.where(delta == partner, 1, 2)) - kinds[0]
    place = (cols & (gc - 1)) ^ lax.shift_left(row, local)
    code = kind * (cl_dev * gc) + rows_ref[...] * gc + place
    code = jnp.where(live_ref[...] > 0, code, -1)
    n_codes = len(kinds) * cl_dev * gc
    select = (lax.broadcasted_iota(jnp.int32, (n_codes, n_slots), 0) == code).astype(F32).astype(BF16)
    height = cl_dev * TILES
    tall = height + PAD

    def spread(step, _):
        lanes = pl.multiple_of(step * 2 * LANES, 2 * LANES)
        summed = jnp.dot(
            select, coupling_ref[:, pl.ds(lanes, 2 * LANES)], preferred_element_type=F32
        )
        for side in range(2):
            t = step * 2 + side
            for kind_row in range(len(kinds) * cl_dev):
                kind_here, cluster = divmod(kind_row, cl_dev)
                base = kind_here * gc * tall + cluster * TILES
                wide_ref[pl.ds(base + t, gc, stride=tall), :] = summed[
                    kind_row * gc : (kind_row + 1) * gc, side * LANES : (side + 1) * LANES
                ]
        return 0

    lax.fori_loop(0, TILES // 2, spread, 0)

    def narrow(pair, _):
        for which in range(2):
            start = (pair * 2 + which) * tall
            out_ref[pair, :, which * LANES : (which + 1) * LANES] = wide_ref[
                pl.ds(start, height), :
            ].astype(BF16)
        return 0

    lax.fori_loop(0, out_ref.shape[0], narrow, 0)


def far_pieces(total, pieces, pairs_piece):
    lane = lax.broadcasted_iota(jnp.int32, (K, LANES), 1)
    first = lane < K
    for operator_ref, base, piece_ref, places in pieces:
        for at, place in enumerate(places):
            for pair in range(pairs_piece):
                both = piece_ref[pl.ds((at * pairs_piece + pair) * K, K), :]
                swapped = jnp.concatenate([both[:, K:], both[:, :K]], axis=1)
                zero = jnp.zeros_like(both)
                weights = jnp.concatenate(
                    [
                        jnp.where(first, both, zero),
                        jnp.where(first, zero, swapped),
                        jnp.where(first, swapped, zero),
                        jnp.where(first, zero, both),
                    ],
                    axis=0,
                )
                index = base + place * pairs_piece + pair
                total = total + jnp.dot(
                    operator_ref[index], weights, preferred_element_type=F32
                )
    return total


def far_kernel(plan, pairs_piece, started, *refs):
    out_ref = refs[-1]
    total = refs[-2][...] if started else jnp.zeros(out_ref.shape, F32)
    pieces = [(refs[o], base, refs[p], places) for o, base, p, places in plan]
    out_ref[...] = far_pieces(total, pieces, pairs_piece)


def near_kernel(signal_ref, near_ref, basis_ref, total_ref, spread_ref):
    cl_dev = signal_ref.shape[0]
    for c in range(cl_dev):
        total = dot_nt(signal_ref[c], near_ref[c, 1])
        if c > 0:
            total = total + dot_nt(signal_ref[c - 1], near_ref[c, 0])
        if c < cl_dev - 1:
            total = total + dot_nt(signal_ref[c + 1], near_ref[c, 2])
        total_ref[:, c * LANES : (c + 1) * LANES] = total
    spread_ref[...] = jnp.zeros_like(spread_ref)
    for c in range(cl_dev):
        wide = basis_ref[c].astype(F32).reshape(TILES, HALVES, LANES)
        for parity in range(HALVES):
            start = parity * cl_dev * TILES + c * TILES
            spread_ref[start : start + TILES, c * LANES : (c + 1) * LANES] = wide[:, parity].astype(BF16)


def halo_kernel(n_dev, across_ref, along_ref, near_ref, so_far_ref, total_ref):
    cl_dev = near_ref.shape[0]
    row = lax.axis_index("row")
    me = lax.axis_index("grp") * lax.axis_size("row") + row
    odd = (row & 1) == 1
    across = across_ref[...]
    along = along_ref[...]
    zero = jnp.zeros_like(across)
    low = jnp.where(me == 0, zero, jnp.where(odd, across, along))
    high = jnp.where(me == n_dev - 1, zero, jnp.where(odd, along, across))
    total_ref[...] = so_far_ref[...]
    total_ref[:, :LANES] += dot_nt(low, near_ref[0, 0])
    total_ref[:, (cl_dev - 1) * LANES :] += dot_nt(high, near_ref[cl_dev - 1, 2])


def final_kernel(plan, pairs_piece, *refs):
    far_ref, near_total_ref, spread_ref, out_ref = refs[-4:]
    pieces = [(refs[o], base, refs[p], places) for o, base, p, places in plan]
    total = far_pieces(far_ref[...], pieces, pairs_piece)
    turned = total.T.astype(BF16)
    lhs = jnp.concatenate([turned[p * R : (p + 1) * R] for p in range(HALVES)], axis=1)
    res = near_total_ref[...] + jnp.dot(lhs, spread_ref[...], preferred_element_type=F32)
    for c in range(out_ref.shape[0]):
        out_ref[c] = res[:, c * LANES : (c + 1) * LANES].astype(BF16)


def held(*values):
    return [pltpu.with_memory_space_constraint(v, pltpu.VMEM) for v in values]


def after(value, *others):
    return lax.optimization_barrier((value, *others))[0]


def per_device(signal, leaf_basis, near_blocks, coupling, block_cols, block_rows, block_live):
    cl_dev = signal.shape[0]
    n_row = lax.axis_size("row")
    n_grp = lax.axis_size("grp")
    n_dev = n_row * n_grp
    gc = cl_dev * n_row
    pairs_piece = cl_dev // 2
    pairs_kind = gc // 2
    height = cl_dev * TILES

    def across_row(value, bit):
        return lax.ppermute(value, "row", [(i, i ^ bit) for i in range(n_row)])

    signal, leaf_basis, near_blocks, coupling, cols, rows, live = held(
        signal, leaf_basis, near_blocks, coupling, block_cols[None], block_rows[None], block_live[None]
    )
    partners = [(i, i ^ 1) for i in range(n_grp)]
    others = [(i, (i + 1) % n_grp if i % 2 else (i - 1) % n_grp) for i in range(n_grp)]

    mine, for_across, for_along = call(
        skeleton_kernel, [((cl_dev // 2 * K, LANES), BF16), ((R, LANES), BF16), ((R, LANES), BF16)], signal, leaf_basis
    )

    def operator(kinds):
        return call(
            functools.partial(operator_kernel, n_grp, n_row, cl_dev, kinds),
            [((len(kinds) * pairs_kind, height, 2 * LANES), BF16)],
            cols,
            rows,
            live,
            coupling,
            scratch=[pltpu.VMEM((len(kinds) * gc * (height + PAD), LANES), F32)],
            room=len(kinds) * gc * (height + PAD) * LANES * 4,
        )

    own_operator = operator((0,))
    side_operator = operator((1, 2))
    near_total, spread = call(
        near_kernel,
        [((R, cl_dev * LANES), F32), ((HALVES * height, cl_dev * LANES), BF16)],
        signal,
        near_blocks,
        leaf_basis,
    )

    places = [0]
    panel = mine
    bit = n_row // 2
    while bit > 1:
        got = across_row(panel, bit)
        panel = jnp.concatenate([panel, got], axis=0)
        places = places + [p ^ bit for p in places]
        bit //= 2
    over_y = across_row(panel, 1)
    places_y = [p ^ 1 for p in places]
    other_a = lax.ppermute(panel, "grp", others)
    across = across_row(after(for_across, panel), 1)
    pairs = [(i, i + 1) for i in range(1, n_dev - 1, 2)]
    along = lax.ppermute(after(for_along, panel), ("grp", "row"), pairs + [(b, a) for a, b in pairs])
    own_far = call(
        functools.partial(far_kernel, [(0, 0, 1, places)], pairs_piece, False),
        [((height, LANES), F32)],
        own_operator,
        *held(panel),
    )
    other_b = lax.ppermute(over_y, "grp", others)
    partner = lax.ppermute(jnp.concatenate([panel, over_y], axis=0), "grp", partners)

    with_halo = call(
        functools.partial(halo_kernel, n_dev),
        [((R, cl_dev * LANES), F32)],
        *held(across, along),
        near_blocks,
        near_total,
    )
    plan = [(0, 0, 2, places_y), (1, pairs_kind, 3, places), (1, 0, 4, places + places_y)]
    far = call(
        functools.partial(far_kernel, plan, pairs_piece, True),
        [((height, LANES), F32)],
        own_operator,
        side_operator,
        *held(over_y, other_a, partner),
        own_far,
    )
    return pl.pallas_call(
        functools.partial(final_kernel, [(0, pairs_kind, 1, places_y)], pairs_piece),
        out_shape=jax.ShapeDtypeStruct(signal.shape, BF16),
        in_specs=[pl.BlockSpec(memory_space=pltpu.VMEM)] * 5,
        out_specs=pl.BlockSpec(memory_space=pltpu.VMEM),
        compiler_params=pltpu.CompilerParams(vmem_limit_bytes=4 << 20),
        name="final",
    )(side_operator, *held(other_b), far, with_halo, spread)


def solution(mesh):
    in_specs = (
        P(("grp", "row"), None, None),
        P(("grp", "row"), None, None),
        P(("grp", "row"), None, None, None),
        P(("grp", "row"), None),
        P(("grp", "row")),
        P(("grp", "row")),
        P(("grp", "row")),
    )
    out_specs = P(("grp", "row"), None, None)

    return jax.shard_map(per_device, mesh=mesh, in_specs=in_specs, out_specs=out_specs, check_vma=False)
```

profile of v0, /device:TPU:1, one launch (start us, length us, event | category | flops | bytes accessed | tf_op | source)
XLA Modules:
  0.0 39.0 jit_solution(303990593091119724)
XLA Ops:
  0.0 0.8 %copy-done.3 = bf16[4,64,128]{2,1,0:T(8,128)(2,1)S(1)} copy-done((bf16[4,64,128]{2,1,0:T(8,128)(2,1)S(1)}, bf16[4,64,128]{2,1,0:T(8,128)(2,1)}, u32[]{:S(2)}) %copy-start.3) | copy-done | bytes 65560
  0.8 0.8 %copy-done.5 = bf16[4,64,128]{2,1,0:T(8,128)(2,1)S(1)} copy-done((bf16[4,64,128]{2,1,0:T(8,128)(2,1)S(1)}, bf16[4,64,128]{2,1,0:T(8,128)(2,1)}, u32[]{:S(2)}) %copy-start.5) | copy-done | bytes 65560
  1.7 0.2 shard_map.74
  1.9 3.2 %collective-permute-start = (bf16[128,128]{1,0:T(8,128)(2,1)S(1)}, bf16[128,128]{1,0:T(8,128)(2,1)S(1)}, u32[]{:S(2)}, u32[]{:S(2)}) collective-permute-start(bf16[128,128]{1,0:T(8,128)(2,1)S(1)} %get-tuple-element.12), channel_id=1, source_target_pairs={{0,4},{1,5},{2,6},{3,7},{4,0},{5,1},{6,2},{7,3},{8,12},{9,13},{10,... | collective-permute-start | bytes 98312 | tf_op jit(solution)/shard_map/ppermute | solution.py:195
  5.1 1.3 %collective-permute-done = bf16[128,128]{1,0:T(8,128)(2,1)S(1)} collective-permute-done((bf16[128,128]{1,0:T(8,128)(2,1)S(1)}, bf16[128,128]{1,0:T(8,128)(2,1)S(1)}, u32[]{:S(2)}, u32[]{:S(2)}) %collective-permute-start) | collective-permute-done | bytes 32800 | tf_op jit(solution)/shard_map/ppermute | solution.py:195
  6.4 1.4 %collective-permute-start.1 = (bf16[256,128]{1,0:T(8,128)(2,1)S(1)}, bf16[256,128]{1,0:T(8,128)(2,1)S(1)}, u32[]{:S(2)}, u32[]{:S(2)}) collective-permute-start(bf16[256,128]{1,0:T(8,128)(2,1)S(1)} %pad_maximum_fusion.1), channel_id=1, source_target_pairs={{0,2},{1,3},{2,0},{3,1},{4,6},{5,7},{6,4},{7,5},{8,10},{9,11},{10,... | collective-permute-start | bytes 196616 | tf_op jit(solution)/shard_map/ppermute | solution.py:195
  7.9 1.7 %collective-permute-done.1 = bf16[256,128]{1,0:T(8,128)(2,1)S(1)} collective-permute-done((bf16[256,128]{1,0:T(8,128)(2,1)S(1)}, bf16[256,128]{1,0:T(8,128)(2,1)S(1)}, u32[]{:S(2)}, u32[]{:S(2)}) %collective-permute-start.1) | collective-permute-done | bytes 65568 | tf_op jit(solution)/shard_map/ppermute | solution.py:195
  9.5 1.4 %collective-permute-start.2 = (bf16[512,128]{1,0:T(8,128)(2,1)S(1)}, bf16[512,128]{1,0:T(8,128)(2,1)S(1)}, u32[]{:S(2)}, u32[]{:S(2)}) collective-permute-start(bf16[512,128]{1,0:T(8,128)(2,1)S(1)} %constant_dynamic-update-slice_fusion.refs_1_), channel_id=1, source_target_pairs={{0,1},{1,0},{2,3},{3,2},{4,5},{5,4},{6,7},{7,6},{8,9},{9,8},{10,11... | collective-permute-start | bytes 393224 | tf_op jit(solution)/shard_map/ppermute | solution.py:195
  10.9 2.5 %collective-permute-done.2.refs_2_ = bf16[512,128]{1,0:T(8,128)(2,1)S(1)} collective-permute-done((bf16[512,128]{1,0:T(8,128)(2,1)S(1)}, bf16[512,128]{1,0:T(8,128)(2,1)S(1)}, u32[]{:S(2)}, u32[]{:S(2)}) %collective-permute-start.2) | collective-permute-done | bytes 131104 | tf_op jit(solution)/shard_map/ppermute | solution.py:195
  13.4 4.3 %collective-permute-start.5 = (bf16[1024,128]{1,0:T(8,128)(2,1)S(1)}, bf16[1024,128]{1,0:T(8,128)(2,1)S(1)}, u32[]{:S(2)}, u32[]{:S(2)}) collective-permute-start(bf16[1024,128]{1,0:T(8,128)(2,1)S(1)} %pad_maximum_fusion), channel_id=1, source_target_pairs={{0,8},{8,0},{16,24},{24,16},{1,9},{9,1},{17,25},{25,17},{2,10},{10... | collective-permute-start | bytes 786440 | tf_op jit(solution)/shard_map/ppermute | solution.py:250
  17.7 1.4 %collective-permute-start.4 = (bf16[512,128]{1,0:T(8,128)(2,1)S(1)}, bf16[512,128]{1,0:T(8,128)(2,1)S(1)}, u32[]{:S(2)}, u32[]{:S(2)}) collective-permute-start(bf16[512,128]{1,0:T(8,128)(2,1)S(1)} %constant_dynamic-update-slice_fusion.refs_1_), channel_id=1, source_target_pairs={{0,24},{8,16},{16,8},{24,0},{1,25},{9,17},{17,9},{25,1},{2,26},{10... | collective-permute-start | bytes 393224 | tf_op jit(solution)/shard_map/ppermute | solution.py:239
  19.1 0.4 collective-permute-start.3
  19.5 1.4 %collective-permute-start.6 = (bf16[64,128]{1,0:T(8,128)(2,1)S(1)}, bf16[64,128]{1,0:T(8,128)(2,1)S(1)}, u32[]{:S(2)}, u32[]{:S(2)}) collective-permute-start(bf16[64,128]{1,0:T(8,128)(2,1)S(1)} %get-tuple-element.14), channel_id=1, source_target_pairs={{0,1},{1,0},{2,3},{3,2},{4,5},{5,4},{6,7},{7,6},{8,9},{9,8},{10,11... | collective-permute-start | bytes 49160 | tf_op jit(solution)/shard_map/ppermute | solution.py:195
  20.9 5.4 %collective-permute-start.7 = (bf16[64,128]{1,0:T(8,128)(2,1)S(1)}, bf16[64,128]{1,0:T(8,128)(2,1)S(1)}, u32[]{:S(2)}, u32[]{:S(2)}) collective-permute-start(bf16[64,128]{1,0:T(8,128)(2,1)S(1)} %get-tuple-element.16), channel_id=1, source_target_pairs={{1,2},{3,4},{5,6},{7,8},{9,10},{11,12},{13,14},{15,16},{17,18},{19... | collective-permute-start | bytes 49160 | tf_op jit(solution)/shard_map/ppermute | solution.py:242
  26.3 0.0 copy-start
  26.3 1.4 %copy-done = bf16[192,4096]{1,0:T(8,128)(2,1)S(1)} copy-done((bf16[192,4096]{1,0:T(8,128)(2,1)S(1)}, bf16[192,4096]{1,0:T(8,128)(2,1)}, u32[]{:S(2)}) %copy-start) | copy-done | bytes 1572888
  27.7 0.7 %copy-done.7 = s32[192]{0:T(256)S(1)} copy-done((s32[192]{0:T(256)S(1)}, s32[192]{0:T(256)}, u32[]{:S(2)}) %copy-start.7) | copy-done | bytes 792
  28.4 0.7 %copy-done.9 = s32[192]{0:T(256)S(1)} copy-done((s32[192]{0:T(256)S(1)}, s32[192]{0:T(256)}, u32[]{:S(2)}) %copy-start.9) | copy-done | bytes 792
  29.1 0.7 %copy-done.11 = s32[192]{0:T(256)S(1)} copy-done((s32[192]{0:T(256)S(1)}, s32[192]{0:T(256)}, u32[]{:S(2)}) %copy-start.11) | copy-done | bytes 792
  29.8 2.8 %shard_map.75.refs_0_ = bf16[16,128,256]{2,1,0:T(8,128)(2,1)S(1)} custom-call(s32[1,192]{1,0:T(1,128)S(1)} %bitcast.3, s32[1,192]{1,0:T(1,128)S(1)} %bitcast.5, s32[1,192]{1,0:T(1,128)S(1)} %bitcast.7, bf16[192,4096]{1,0:T(8,128)(2,1)S(1)} %copy-done), custom_call_target="tpu_custom_call" | custom-call | tf_op jit(solution)/shard_map/pallas_call | solution.py:31
  32.6 0.0 copy-start.2
  32.6 0.0 copy-start.4
  32.6 0.0 copy-start.6
  32.6 3.4 %shard_map.73.refs_1_.refs_0_ = bf16[32,128,256]{2,1,0:T(8,128)(2,1)S(1)} custom-call(s32[1,192]{1,0:T(1,128)S(1)} %bitcast.4, s32[1,192]{1,0:T(1,128)S(1)} %bitcast.6, s32[1,192]{1,0:T(1,128)S(1)} %bitcast.8, bf16[192,4096]{1,0:T(8,128)(2,1)S(1)} %copy-done.1), custom_call_target="tpu_custom_call" | custom-call | tf_op jit(solution)/shard_map/pallas_call | solution.py:31
  36.1 0.4 shard_map.78
  36.5 0.4 shard_map.76.refs_5_
  36.8 0.0 collective-permute-done.7.along_ref
  36.9 0.1 shard_map.79.refs_3_
  37.0 0.0 collective-permute-done.4.refs_3_
  37.0 0.0 collective-permute-done.5.refs_4_
  37.0 0.8 %shard_map.77.refs_2_ = f32[128,128]{1,0:T(8,128)S(1)} custom-call(bf16[16,128,256]{2,1,0:T(8,128)(2,1)S(1)} %shard_map.75.refs_0_, bf16[32,128,256]{2,1,0:T(8,128)(2,1)S(1)} %shard_map.73.refs_1_.refs_0_, bf16[512,128]{1,0:T(8,128)(2,1)S(1)} %collective-permute-done.2.refs_2_, bf16[512,128]{1,0:T(8,128)(2,1)S(1)} %collective-permute-done.4.refs_3_, ...), custom_call_target="tpu_custom_call" | custom-call | tf_op jit(solution)/shard_map/pallas_call | solution.py:31
  37.8 1.2 %final.1 = bf16[4,64,128]{2,1,0:T(8,128)(2,1)} custom-call(bf16[32,128,256]{2,1,0:T(8,128)(2,1)S(1)} %shard_map.73.refs_1_.refs_0_, bf16[512,128]{1,0:T(8,128)(2,1)S(1)} %collective-permute-done.3.refs_1_, f32[128,128]{1,0:T(8,128)S(1)} %shard_map.77.refs_2_, f32[64,512]{1,0:T(8,128)S(1)} %shard_map.79.refs_3_, bf16[256,512]{1,0:T(8,128)(2,1)S(1)} %get-tuple-element.18.refs_4_), custom_call_target="tpu_custom_call" | custom-call | tf_op jit(solution)/shard_map/final/pallas_call | solution.py:268
  (23 shorter events, 0.1 us)
Async XLA Ops:
  0.0 0.8 %copy-start.3 = (bf16[4,64,128]{2,1,0:T(8,128)(2,1)S(1)}, bf16[4,64,128]{2,1,0:T(8,128)(2,1)}, u32[]{:S(2)}) copy-start(bf16[4,64,128]{2,1,0:T(8,128)(2,1)} %signal_ref.3) | copy-start | bytes 196612
  0.8 0.8 %copy-start.5 = (bf16[4,64,128]{2,1,0:T(8,128)(2,1)S(1)}, bf16[4,64,128]{2,1,0:T(8,128)(2,1)}, u32[]{:S(2)}) copy-start(bf16[4,64,128]{2,1,0:T(8,128)(2,1)} %basis_ref.3) | copy-start | bytes 196612
  1.7 30.9 %copy-start.8 = (s32[192]{0:T(256)S(1)}, s32[192]{0:T(256)}, u32[]{:S(2)}) copy-start(s32[192]{0:T(256)} %param.11) | copy-start | bytes 2308
  1.7 30.9 %copy-start.10 = (s32[192]{0:T(256)S(1)}, s32[192]{0:T(256)}, u32[]{:S(2)}) copy-start(s32[192]{0:T(256)} %param.12) | copy-start | bytes 2308
  1.7 30.9 %copy-start.12 = (s32[192]{0:T(256)S(1)}, s32[192]{0:T(256)}, u32[]{:S(2)}) copy-start(s32[192]{0:T(256)} %param.13) | copy-start | bytes 2308
  1.9 4.5 %collective-permute-start = (bf16[128,128]{1,0:T(8,128)(2,1)S(1)}, bf16[128,128]{1,0:T(8,128)(2,1)S(1)}, u32[]{:S(2)}, u32[]{:S(2)}) collective-permute-start(bf16[128,128]{1,0:T(8,128)(2,1)S(1)} %get-tuple-element.12), channel_id=1, source_target_pairs={{0,4},{1,5},{2,6},{3,7},{4,0},{5,1},{6,2},{7,3},{8,12},{9,13},{10,... | collective-permute-start | bytes 98312 | tf_op jit(solution)/shard_map/ppermute | solution.py:195
  6.4 3.1 %collective-permute-start.1 = (bf16[256,128]{1,0:T(8,128)(2,1)S(1)}, bf16[256,128]{1,0:T(8,128)(2,1)S(1)}, u32[]{:S(2)}, u32[]{:S(2)}) collective-permute-start(bf16[256,128]{1,0:T(8,128)(2,1)S(1)} %pad_maximum_fusion.1), channel_id=1, source_target_pairs={{0,2},{1,3},{2,0},{3,1},{4,6},{5,7},{6,4},{7,5},{8,10},{9,11},{10,... | collective-permute-start | bytes 196616 | tf_op jit(solution)/shard_map/ppermute | solution.py:195
  9.5 3.9 %collective-permute-start.2 = (bf16[512,128]{1,0:T(8,128)(2,1)S(1)}, bf16[512,128]{1,0:T(8,128)(2,1)S(1)}, u32[]{:S(2)}, u32[]{:S(2)}) collective-permute-start(bf16[512,128]{1,0:T(8,128)(2,1)S(1)} %constant_dynamic-update-slice_fusion.refs_1_), channel_id=1, source_target_pairs={{0,1},{1,0},{2,3},{3,2},{4,5},{5,4},{6,7},{7,6},{8,9},{9,8},{10,11... | collective-permute-start | bytes 393224 | tf_op jit(solution)/shard_map/ppermute | solution.py:195
  13.4 23.6 %collective-permute-start.5 = (bf16[1024,128]{1,0:T(8,128)(2,1)S(1)}, bf16[1024,128]{1,0:T(8,128)(2,1)S(1)}, u32[]{:S(2)}, u32[]{:S(2)}) collective-permute-start(bf16[1024,128]{1,0:T(8,128)(2,1)S(1)} %pad_maximum_fusion), channel_id=1, source_target_pairs={{0,8},{8,0},{16,24},{24,16},{1,9},{9,1},{17,25},{25,17},{2,10},{10... | collective-permute-start | bytes 786440 | tf_op jit(solution)/shard_map/ppermute | solution.py:250
  17.7 19.3 %collective-permute-start.4 = (bf16[512,128]{1,0:T(8,128)(2,1)S(1)}, bf16[512,128]{1,0:T(8,128)(2,1)S(1)}, u32[]{:S(2)}, u32[]{:S(2)}) collective-permute-start(bf16[512,128]{1,0:T(8,128)(2,1)S(1)} %constant_dynamic-update-slice_fusion.refs_1_), channel_id=1, source_target_pairs={{0,24},{8,16},{16,8},{24,0},{1,25},{9,17},{17,9},{25,1},{2,26},{10... | collective-permute-start | bytes 393224 | tf_op jit(solution)/shard_map/ppermute | solution.py:239
  19.1 18.7 %collective-permute-start.3 = (bf16[512,128]{1,0:T(8,128)(2,1)S(1)}, bf16[512,128]{1,0:T(8,128)(2,1)S(1)}, u32[]{:S(2)}, u32[]{:S(2)}) collective-permute-start(bf16[512,128]{1,0:T(8,128)(2,1)S(1)} %collective-permute-done.2.refs_2_), channel_id=1, source_target_pairs={{0,24},{8,16},{16,8},{24,0},{1,25},{9,17},{17,9},{25,1},{2,26},{10... | collective-permute-start | bytes 393224 | tf_op jit(solution)/shard_map/ppermute | solution.py:249
  19.5 17.4 %collective-permute-start.6 = (bf16[64,128]{1,0:T(8,128)(2,1)S(1)}, bf16[64,128]{1,0:T(8,128)(2,1)S(1)}, u32[]{:S(2)}, u32[]{:S(2)}) collective-permute-start(bf16[64,128]{1,0:T(8,128)(2,1)S(1)} %get-tuple-element.14), channel_id=1, source_target_pairs={{0,1},{1,0},{2,3},{3,2},{4,5},{5,4},{6,7},{7,6},{8,9},{9,8},{10,11... | collective-permute-start | bytes 49160 | tf_op jit(solution)/shard_map/ppermute | solution.py:195
  20.9 15.9 %collective-permute-start.7 = (bf16[64,128]{1,0:T(8,128)(2,1)S(1)}, bf16[64,128]{1,0:T(8,128)(2,1)S(1)}, u32[]{:S(2)}, u32[]{:S(2)}) collective-permute-start(bf16[64,128]{1,0:T(8,128)(2,1)S(1)} %get-tuple-element.16), channel_id=1, source_target_pairs={{1,2},{3,4},{5,6},{7,8},{9,10},{11,12},{13,14},{15,16},{17,18},{19... | collective-permute-start | bytes 49160 | tf_op jit(solution)/shard_map/ppermute | solution.py:242
  26.3 1.4 %copy-start = (bf16[192,4096]{1,0:T(8,128)(2,1)S(1)}, bf16[192,4096]{1,0:T(8,128)(2,1)}, u32[]{:S(2)}) copy-start(bf16[192,4096]{1,0:T(8,128)(2,1)} %refs_0_.3) | copy-start | bytes 4718596
  27.7 0.7 %copy-start.7 = (s32[192]{0:T(256)S(1)}, s32[192]{0:T(256)}, u32[]{:S(2)}) copy-start(s32[192]{0:T(256)} %param.11) | copy-start | bytes 2308
  28.4 0.7 %copy-start.9 = (s32[192]{0:T(256)S(1)}, s32[192]{0:T(256)}, u32[]{:S(2)}) copy-start(s32[192]{0:T(256)} %param.12) | copy-start | bytes 2308
  29.1 0.7 %copy-start.11 = (s32[192]{0:T(256)S(1)}, s32[192]{0:T(256)}, u32[]{:S(2)}) copy-start(s32[192]{0:T(256)} %param.13) | copy-start | bytes 2308
  29.8 2.8 %copy-start.1 = (bf16[192,4096]{1,0:T(8,128)(2,1)S(1)}, bf16[192,4096]{1,0:T(8,128)(2,1)}, u32[]{:S(2)}) copy-start(bf16[192,4096]{1,0:T(8,128)(2,1)} %refs_0_.3) | copy-start | bytes 4718596
  32.6 3.5 %copy-start.2 = (bf16[4,3,128,128]{3,2,1,0:T(8,128)(2,1)S(1)}, bf16[4,3,128,128]{3,2,1,0:T(8,128)(2,1)}, u32[]{:S(2)}) copy-start(bf16[4,3,128,128]{3,2,1,0:T(8,128)(2,1)} %near_ref.3) | copy-start | bytes 1179652
  32.6 3.5 %copy-start.4 = (bf16[4,64,128]{2,1,0:T(8,128)(2,1)S(1)}, bf16[4,64,128]{2,1,0:T(8,128)(2,1)}, u32[]{:S(2)}) copy-start(bf16[4,64,128]{2,1,0:T(8,128)(2,1)} %signal_ref.3) | copy-start | bytes 196612
  32.6 3.5 %copy-start.6 = (bf16[4,64,128]{2,1,0:T(8,128)(2,1)S(1)}, bf16[4,64,128]{2,1,0:T(8,128)(2,1)}, u32[]{:S(2)}) copy-start(bf16[4,64,128]{2,1,0:T(8,128)(2,1)} %basis_ref.3) | copy-start | bytes 196612
where the time goes:
time: 39.3 us; the launch traced here: 39 us
  starting transfers between devices  18.9 us (48%)
  Pallas kernels  9.25 us (24%)
  waiting for transfers between devices  5.51 us (14%)
  local copies, waits for them, and re-layouts  5.17 us (13%)
    pallas_call x7, Pallas kernels, call(): pl.pallas_call(kernel, out_shape=shapes[0] if single else shapes, in_spec...  8.07 us
    ppermute x4, starting transfers between devices, across_row(): return lax.ppermute(value, 'row', [(i, i ^ bit) for i in range(n_row)])  7.44 us
    ppermute x4, waiting for transfers between devices, across_row(): return lax.ppermute(value, 'row', [(i, i ^ bit) for i in range(n_row)])  5.49 us
    ppermute x1, starting transfers between devices, per_device(): lax.ppermute(after(for_along, panel), ('grp', 'row'), pairs + [(b, a) for...  5.41 us
    unnamed x28, local copies, waits for them, and re-layouts  5.16 us
    ppermute x1, starting transfers between devices, per_device(): lax.ppermute(jnp.concatenate([panel, over_y], axis=0), 'grp', partners)  4.26 us
    ppermute x1, starting transfers between devices, per_device(): other_a = lax.ppermute(panel, 'grp', others)  1.38 us
    pallas_call x1, Pallas kernels, per_device(): pl.pallas_call(functools.partial(final_kernel, [(0, pairs_kind, 1, places...  1.19 us
  transfers between devices with their start and end apart: 8, of which 3 were waited for; matrix products, arithmetic and copies ran while one was open for 0% of the time, Pallas kernels for 20%

commit v1 on v0

--- a/solution.py
+++ b/solution.py
@@ -24,21 +24,33 @@
     return lax.dot_general(a, b, (((1,), (1,)), ((), ())), preferred_element_type=F32)
 
 
-def call(kernel, outs, *args, scratch=(), room=0):
+def call(kernel, outs, *args, scratch=(), room=0, in_hbm=()):
     spec = pl.BlockSpec(memory_space=pltpu.VMEM)
+    far_spec = pl.BlockSpec(memory_space=pltpu.HBM)
     single = len(outs) == 1
     shapes = [pltpu.VMEM(s, d) for s, d in outs]
+    args = [
+        pltpu.with_memory_space_constraint(a, pltpu.HBM) if i in in_hbm else a
+        for i, a in enumerate(args)
+    ]
     return pl.pallas_call(
         kernel,
         out_shape=shapes[0] if single else shapes,
-        in_specs=[spec] * len(args),
+        in_specs=[far_spec if i in in_hbm else spec for i in range(len(args))],
         out_specs=spec if single else [spec] * len(outs),
         scratch_shapes=scratch,
         compiler_params=pltpu.CompilerParams(vmem_limit_bytes=room + (2 << 20)),
     )(*args)
 
 
-def skeleton_kernel(signal_ref, basis_ref, out_ref, across_ref, along_ref):
+def skeleton_kernel(*refs):
+    sources, here, (out_ref, across_ref, along_ref, sems) = refs[:5], refs[5:10], refs[10:]
+    copies = [pltpu.make_async_copy(a, b, sems.at[n]) for n, (a, b) in enumerate(zip(sources, here))]
+    for copy in copies:
+        copy.start()
+    signal_ref, basis_ref = here[:2]
+    copies[0].wait()
+    copies[1].wait()
     last = signal_ref.shape[0] - 1
     for pair in range(signal_ref.shape[0] // 2):
         sides = [
@@ -48,44 +60,39 @@
     odd = (lax.axis_index("row") & 1) == 1
     across_ref[...] = jnp.where(odd, signal_ref[0], signal_ref[last])
     along_ref[...] = jnp.where(odd, signal_ref[last], signal_ref[0])
-
-
-def operator_kernel(n_grp, n_row, cl_dev, kinds, cols_ref, rows_ref, live_ref, *refs):
-    coupling_ref, out_ref, wide_ref = refs
+    for copy in copies[2:]:
+        copy.wait()
+
+
+def slot_codes(n_grp, n_row, cl_dev, first_kind, cols, rows, live):
     gc = n_row * cl_dev
     shift = gc.bit_length() - 1
     local = cl_dev.bit_length() - 1
-    n_slots = coupling_ref.shape[0]
     group = lax.axis_index("grp")
     row = lax.axis_index("row")
-    cols = cols_ref[...]
     delta = (lax.shift_right_logical(cols, shift) - group + n_grp) & (n_grp - 1)
     partner = jnp.where((group & 1) == 0, 1, n_grp - 1)
-    kind = jnp.where(delta == 0, 0, jnp.where(delta == partner, 1, 2)) - kinds[0]
+    kind = jnp.where(delta == 0, 0, jnp.where(delta == partner, 1, 2)) - first_kind
     place = (cols & (gc - 1)) ^ lax.shift_left(row, local)
-    code = kind * (cl_dev * gc) + rows_ref[...] * gc + place
-    code = jnp.where(live_ref[...] > 0, code, -1)
-    n_codes = len(kinds) * cl_dev * gc
-    select = (lax.broadcasted_iota(jnp.int32, (n_codes, n_slots), 0) == code).astype(F32).astype(BF16)
+    return jnp.where(live > 0, kind * (cl_dev * gc) + rows * gc + place, -1)
+
+
+def sum_slots(n_kinds, gc, cl_dev, code, coupling_of, out_ref, wide_ref):
+    n_codes = n_kinds * cl_dev * gc
+    shape = (n_codes, code.shape[1])
+    select = (lax.broadcasted_iota(jnp.int32, shape, 0) == code).astype(F32).astype(BF16)
     height = cl_dev * TILES
     tall = height + PAD
-
-    def spread(step, _):
-        lanes = pl.multiple_of(step * 2 * LANES, 2 * LANES)
-        summed = jnp.dot(
-            select, coupling_ref[:, pl.ds(lanes, 2 * LANES)], preferred_element_type=F32
-        )
+    for step in range(TILES // 2):
+        summed = jnp.dot(select, coupling_of(step), preferred_element_type=F32)
         for side in range(2):
             t = step * 2 + side
-            for kind_row in range(len(kinds) * cl_dev):
+            for kind_row in range(n_kinds * cl_dev):
                 kind_here, cluster = divmod(kind_row, cl_dev)
                 base = kind_here * gc * tall + cluster * TILES
                 wide_ref[pl.ds(base + t, gc, stride=tall), :] = summed[
                     kind_row * gc : (kind_row + 1) * gc, side * LANES : (side + 1) * LANES
                 ]
-        return 0
-
-    lax.fori_loop(0, TILES // 2, spread, 0)
 
     def narrow(pair, _):
         for which in range(2):
@@ -95,7 +102,61 @@
             ].astype(BF16)
         return 0
 
-    lax.fori_loop(0, out_ref.shape[0], narrow, 0)
+    lax.fori_loop(0, out_ref.shape[0], narrow, 0, unroll=4)
+
+
+def own_operator_kernel(n_grp, n_row, cl_dev, cols_ref, rows_ref, live_ref, coupling_ref, *refs):
+    out_ref, rest_ref, mine_ref, wide_ref, sems = refs
+    per = coupling_ref.shape[0] // 3
+    half = coupling_ref.shape[1] // 2
+    copies = [
+        pltpu.make_async_copy(
+            coupling_ref.at[per : 2 * per, n * half : (n + 1) * half],
+            mine_ref.at[:, n * half : (n + 1) * half],
+            sems.at[n],
+        )
+        for n in range(2)
+    ]
+    others = [
+        pltpu.make_async_copy(
+            coupling_ref.at[2 * per * n : 2 * per * n + per],
+            rest_ref.at[per * n : per * n + per],
+            sems.at[2 + n],
+        )
+        for n in range(2)
+    ]
+    for copy in copies + others:
+        copy.start()
+    cut = slice(per, 2 * per)
+    code = slot_codes(
+        n_grp, n_row, cl_dev, 0, cols_ref[:, cut], rows_ref[:, cut], live_ref[:, cut]
+    )
+
+    def coupling_of(step):
+        if step % (TILES // 4) == 0:
+            copies[step // (TILES // 4)].wait()
+        return mine_ref[:, step * 2 * LANES : (step + 1) * 2 * LANES]
+
+    sum_slots(1, n_row * cl_dev, cl_dev, code, coupling_of, out_ref, wide_ref)
+    for copy in others:
+        copy.wait()
+
+
+def side_operator_kernel(n_grp, n_row, cl_dev, cols_ref, rows_ref, live_ref, rest_ref, *refs):
+    out_ref, wide_ref = refs
+    per = rest_ref.shape[0] // 2
+
+    def outer(ref):
+        return jnp.concatenate([ref[:, :per], ref[:, 2 * per :]], axis=1)
+
+    code = slot_codes(
+        n_grp, n_row, cl_dev, 1, outer(cols_ref), outer(rows_ref), outer(live_ref)
+    )
+
+    def coupling_of(step):
+        return rest_ref[:, step * 2 * LANES : (step + 1) * 2 * LANES]
+
+    sum_slots(2, n_row * cl_dev, cl_dev, code, coupling_of, out_ref, wide_ref)
 
 
 def far_pieces(total, pieces, pairs_piece):
@@ -177,10 +238,6 @@
     return [pltpu.with_memory_space_constraint(v, pltpu.VMEM) for v in values]
 
 
-def after(value, *others):
-    return lax.optimization_barrier((value, *others))[0]
-
-
 def per_device(signal, leaf_basis, near_blocks, coupling, block_cols, block_rows, block_live):
     cl_dev = signal.shape[0]
     n_row = lax.axis_size("row")
@@ -194,30 +251,56 @@
     def across_row(value, bit):
         return lax.ppermute(value, "row", [(i, i ^ bit) for i in range(n_row)])
 
-    signal, leaf_basis, near_blocks, coupling, cols, rows, live = held(
-        signal, leaf_basis, near_blocks, coupling, block_cols[None], block_rows[None], block_live[None]
-    )
     partners = [(i, i ^ 1) for i in range(n_grp)]
     others = [(i, (i + 1) % n_grp if i % 2 else (i - 1) % n_grp) for i in range(n_grp)]
-
-    mine, for_across, for_along = call(
-        skeleton_kernel, [((cl_dev // 2 * K, LANES), BF16), ((R, LANES), BF16), ((R, LANES), BF16)], signal, leaf_basis
-    )
-
-    def operator(kinds):
-        return call(
-            functools.partial(operator_kernel, n_grp, n_row, cl_dev, kinds),
-            [((len(kinds) * pairs_kind, height, 2 * LANES), BF16)],
-            cols,
-            rows,
-            live,
-            coupling,
-            scratch=[pltpu.VMEM((len(kinds) * gc * (height + PAD), LANES), F32)],
-            room=len(kinds) * gc * (height + PAD) * LANES * 4,
-        )
-
-    own_operator = operator((0,))
-    side_operator = operator((1, 2))
+    n_slots = coupling.shape[0]
+
+    signal, leaf_basis, cols, rows, live, mine, for_across, for_along = call(
+        skeleton_kernel,
+        [(signal.shape, BF16), (leaf_basis.shape, BF16)]
+        + [((1, n_slots), jnp.int32)] * 3
+        + [((cl_dev // 2 * K, LANES), BF16), ((R, LANES), BF16), ((R, LANES), BF16)],
+        signal,
+        leaf_basis,
+        block_cols[None],
+        block_rows[None],
+        block_live[None],
+        in_hbm=range(5),
+        scratch=[pltpu.SemaphoreType.DMA((5,))],
+    )
+
+    def wide(n_kinds):
+        return (n_kinds * gc * (height + PAD), LANES)
+
+    own_operator, rest = call(
+        functools.partial(own_operator_kernel, n_grp, n_row, cl_dev),
+        [
+            ((pairs_kind, height, 2 * LANES), BF16),
+            ((n_slots // 3 * 2, coupling.shape[1]), BF16),
+        ],
+        cols,
+        rows,
+        live,
+        coupling,
+        in_hbm=(3,),
+        scratch=[
+            pltpu.VMEM((n_slots // 3, coupling.shape[1]), BF16),
+            pltpu.VMEM(wide(1), F32),
+            pltpu.SemaphoreType.DMA((4,)),
+        ],
+        room=wide(1)[0] * LANES * 4 + n_slots // 3 * coupling.shape[1] * 2,
+    )
+    side_operator = call(
+        functools.partial(side_operator_kernel, n_grp, n_row, cl_dev),
+        [((2 * pairs_kind, height, 2 * LANES), BF16)],
+        cols,
+        rows,
+        live,
+        rest,
+        scratch=[pltpu.VMEM(wide(2), F32)],
+        room=wide(2)[0] * LANES * 4,
+    )
+    (near_blocks,) = held(near_blocks)
     near_total, spread = call(
         near_kernel,
         [((R, cl_dev * LANES), F32), ((HALVES * height, cl_dev * LANES), BF16)],
@@ -237,9 +320,9 @@
     over_y = across_row(panel, 1)
     places_y = [p ^ 1 for p in places]
     other_a = lax.ppermute(panel, "grp", others)
-    across = across_row(after(for_across, panel), 1)
+    across = across_row(for_across, 1)
     pairs = [(i, i + 1) for i in range(1, n_dev - 1, 2)]
-    along = lax.ppermute(after(for_along, panel), ("grp", "row"), pairs + [(b, a) for a, b in pairs])
+    along = lax.ppermute(for_along, ("grp", "row"), pairs + [(b, a) for a, b in pairs])
     own_far = call(
         functools.partial(far_kernel, [(0, 0, 1, places)], pairs_piece, False),
         [((height, LANES), F32)],
@@ -287,4 +370,6 @@
     )
     out_specs = P(("grp", "row"), None, None)
 
-    return jax.shard_map(per_device, mesh=mesh, in_specs=in_specs, out_specs=out_specs, check_vma=False)
+    return jax.shard_map(
+        per_device, mesh=mesh, in_specs=in_specs, out_specs=out_specs, check_vma=False
+    )

time: 39.3 us -> 31.6 us (0.80)
  local copies, waits for them, and re-layouts: 5.17 us -> 0.03 us
  Pallas kernels: 9.25 us -> 6.85 us
    unnamed x28 -> x4, local copies, waits for them, and re-layouts: 5.16 us -> 0.02 us
    pallas_call x7, Pallas kernels: 8.07 us -> 5.66 us  [call(): pl.pallas_call(kernel, out_shape=shapes[0] if single else shapes, in_spec...]
  transfers between devices with their start and end apart: 8 -> 8, of which waited for: 3 -> 3; matrix products, arithmetic and copies ran while one was open for 0% -> 0% of each run, Pallas kernels for 20% -> 14%
where the time goes in v1:
time: 31.6 us; the launch traced here: 31.4 us
  starting transfers between devices  18.9 us (60%)
  Pallas kernels  6.85 us (22%)
  waiting for transfers between devices  5.5 us (17%)
    ppermute x4, starting transfers between devices, across_row(): return lax.ppermute(value, 'row', [(i, i ^ bit) for i in range(n_row)])  7.44 us
    pallas_call x7, Pallas kernels, call(): pl.pallas_call(kernel, out_shape=shapes[0] if single else shapes, in_spec...  5.66 us
    ppermute x4, waiting for transfers between devices, across_row(): return lax.ppermute(value, 'row', [(i, i ^ bit) for i in range(n_row)])  5.49 us
    ppermute x1, starting transfers between devices, per_device(): lax.ppermute(for_along, ('grp', 'row'), pairs + [(b, a) for a, b in pairs])  5.41 us
    ppermute x1, starting transfers between devices, per_device(): lax.ppermute(jnp.concatenate([panel, over_y], axis=0), 'grp', partners)  4.26 us
    ppermute x1, starting transfers between devices, per_device(): other_a = lax.ppermute(panel, 'grp', others)  1.38 us
    pallas_call x1, Pallas kernels, per_device(): pl.pallas_call(functools.partial(final_kernel, [(0, pairs_kind, 1, places...  1.19 us
  transfers between devices with their start and end apart: 8, of which 3 were waited for; matrix products, arithmetic and copies ran while one was open for 0% of the time, Pallas kernels for 14%

profile of v1, /device:TPU:1, one launch (start us, length us, event | category | flops | bytes accessed | tf_op | source)
XLA Modules:
  0.0 31.4 jit_solution(13679923445222701390)
XLA Ops:
  0.0 1.1 %shard_map.73 = (bf16[4,64,128]{2,1,0:T(8,128)(2,1)S(1)}, bf16[4,64,128]{2,1,0:T(8,128)(2,1)S(1)}, s32[1,192]{1,0:T(1,128)S(1)}, s32[1,192]{1,0:T(1,128)S(1)}, s...) custom-call(bf16[4,64,128]{2,1,0:T(8,128)(2,1)} %refs_0_.1, ...), custom_call_target="tpu_custom_call" | custom-call | tf_op jit(solution)/shard_map/pallas_call | solution.py:36
  1.2 3.2 %collective-permute-start = (bf16[128,128]{1,0:T(8,128)(2,1)S(1)}, bf16[128,128]{1,0:T(8,128)(2,1)S(1)}, u32[]{:S(2)}, u32[]{:S(2)}) collective-permute-start(bf16[128,128]{1,0:T(8,128)(2,1)S(1)} %get-tuple-element.21), channel_id=1, source_target_pairs={{0,4},{1,5},{2,6},{3,7},{4,0},{5,1},{6,2},{7,3},{8,12},{9,13},{10,... | collective-permute-start | bytes 98312 | tf_op jit(solution)/shard_map/ppermute | solution.py:252
  4.4 1.3 %collective-permute-done = bf16[128,128]{1,0:T(8,128)(2,1)S(1)} collective-permute-done((bf16[128,128]{1,0:T(8,128)(2,1)S(1)}, bf16[128,128]{1,0:T(8,128)(2,1)S(1)}, u32[]{:S(2)}, u32[]{:S(2)}) %collective-permute-start) | collective-permute-done | bytes 32800 | tf_op jit(solution)/shard_map/ppermute | solution.py:252
  5.7 1.4 %collective-permute-start.1 = (bf16[256,128]{1,0:T(8,128)(2,1)S(1)}, bf16[256,128]{1,0:T(8,128)(2,1)S(1)}, u32[]{:S(2)}, u32[]{:S(2)}) collective-permute-start(bf16[256,128]{1,0:T(8,128)(2,1)S(1)} %pad_maximum_fusion.1), channel_id=1, source_target_pairs={{0,2},{1,3},{2,0},{3,1},{4,6},{5,7},{6,4},{7,5},{8,10},{9,11},{10,... | collective-permute-start | bytes 196616 | tf_op jit(solution)/shard_map/ppermute | solution.py:252
  7.1 1.7 %collective-permute-done.1 = bf16[256,128]{1,0:T(8,128)(2,1)S(1)} collective-permute-done((bf16[256,128]{1,0:T(8,128)(2,1)S(1)}, bf16[256,128]{1,0:T(8,128)(2,1)S(1)}, u32[]{:S(2)}, u32[]{:S(2)}) %collective-permute-start.1) | collective-permute-done | bytes 65568 | tf_op jit(solution)/shard_map/ppermute | solution.py:252
  8.8 1.4 %collective-permute-start.2 = (bf16[512,128]{1,0:T(8,128)(2,1)S(1)}, bf16[512,128]{1,0:T(8,128)(2,1)S(1)}, u32[]{:S(2)}, u32[]{:S(2)}) collective-permute-start(bf16[512,128]{1,0:T(8,128)(2,1)S(1)} %constant_dynamic-update-slice_fusion.refs_1_), channel_id=1, source_target_pairs={{0,1},{1,0},{2,3},{3,2},{4,5},{5,4},{6,7},{7,6},{8,9},{9,8},{10,11... | collective-permute-start | bytes 393224 | tf_op jit(solution)/shard_map/ppermute | solution.py:252
  10.2 2.5 %collective-permute-done.2.refs_2_ = bf16[512,128]{1,0:T(8,128)(2,1)S(1)} collective-permute-done((bf16[512,128]{1,0:T(8,128)(2,1)S(1)}, bf16[512,128]{1,0:T(8,128)(2,1)S(1)}, u32[]{:S(2)}, u32[]{:S(2)}) %collective-permute-start.2) | collective-permute-done | bytes 131104 | tf_op jit(solution)/shard_map/ppermute | solution.py:252
  12.7 4.3 %collective-permute-start.5 = (bf16[1024,128]{1,0:T(8,128)(2,1)S(1)}, bf16[1024,128]{1,0:T(8,128)(2,1)S(1)}, u32[]{:S(2)}, u32[]{:S(2)}) collective-permute-start(bf16[1024,128]{1,0:T(8,128)(2,1)S(1)} %pad_maximum_fusion), channel_id=1, source_target_pairs={{0,8},{8,0},{16,24},{24,16},{1,9},{9,1},{17,25},{25,17},{2,10},{10... | collective-permute-start | bytes 786440 | tf_op jit(solution)/shard_map/ppermute | solution.py:333
  17.0 1.4 %collective-permute-start.4 = (bf16[512,128]{1,0:T(8,128)(2,1)S(1)}, bf16[512,128]{1,0:T(8,128)(2,1)S(1)}, u32[]{:S(2)}, u32[]{:S(2)}) collective-permute-start(bf16[512,128]{1,0:T(8,128)(2,1)S(1)} %constant_dynamic-update-slice_fusion.refs_1_), channel_id=1, source_target_pairs={{0,24},{8,16},{16,8},{24,0},{1,25},{9,17},{17,9},{25,1},{2,26},{10... | collective-permute-start | bytes 393224 | tf_op jit(solution)/shard_map/ppermute | solution.py:322
  18.3 0.4 %collective-permute-start.3 = (bf16[512,128]{1,0:T(8,128)(2,1)S(1)}, bf16[512,128]{1,0:T(8,128)(2,1)S(1)}, u32[]{:S(2)}, u32[]{:S(2)}) collective-permute-start(bf16[512,128]{1,0:T(8,128)(2,1)S(1)} %collective-permute-done.2.refs_2_), channel_id=1, source_target_pairs={{0,24},{8,16},{16,8},{24,0},{1,25},{9,17},{17,9},{25,1},{2,26},{10... | collective-permute-start | bytes 393224 | tf_op jit(solution)/shard_map/ppermute | solution.py:332
  18.7 1.4 %collective-permute-start.6 = (bf16[64,128]{1,0:T(8,128)(2,1)S(1)}, bf16[64,128]{1,0:T(8,128)(2,1)S(1)}, u32[]{:S(2)}, u32[]{:S(2)}) collective-permute-start(bf16[64,128]{1,0:T(8,128)(2,1)S(1)} %get-tuple-element.23), channel_id=1, source_target_pairs={{0,1},{1,0},{2,3},{3,2},{4,5},{5,4},{6,7},{7,6},{8,9},{9,8},{10,11... | collective-permute-start | bytes 49160 | tf_op jit(solution)/shard_map/ppermute | solution.py:252
  20.2 5.4 %collective-permute-start.7 = (bf16[64,128]{1,0:T(8,128)(2,1)S(1)}, bf16[64,128]{1,0:T(8,128)(2,1)S(1)}, u32[]{:S(2)}, u32[]{:S(2)}) collective-permute-start(bf16[64,128]{1,0:T(8,128)(2,1)S(1)} %get-tuple-element.24), channel_id=1, source_target_pairs={{1,2},{3,4},{5,6},{7,8},{9,10},{11,12},{13,14},{15,16},{17,18},{19... | collective-permute-start | bytes 49160 | tf_op jit(solution)/shard_map/ppermute | solution.py:325
  25.6 0.0 copy-start
  25.6 1.8 %shard_map.74 = (bf16[16,128,256]{2,1,0:T(8,128)(2,1)S(1)}, bf16[128,4096]{1,0:T(8,128)(2,1)S(1)}) custom-call(s32[1,192]{1,0:T(1,128)S(1)} %get-tuple-element.17.cols_ref, s32[1,192]{1,0:T(1,128)S(1)} %get-tuple-element.18.rows_ref, s32[1,192]{1,0:T(1,128)S(1)} %get-tuple-element.19.live_ref, bf16[192,4096]{1,0:T(8,128)(2,1)} %coupling_ref.1), custom_call_target="tpu_custom_call" | custom-call | tf_op jit(solution)/shard_map/pallas_call | solution.py:36
  27.4 1.1 %shard_map.75.refs_1_.refs_0_ = bf16[32,128,256]{2,1,0:T(8,128)(2,1)S(1)} custom-call(s32[1,192]{1,0:T(1,128)S(1)} %get-tuple-element.17.cols_ref, s32[1,192]{1,0:T(1,128)S(1)} %get-tuple-element.18.rows_ref, s32[1,192]{1,0:T(1,128)S(1)} %get-tuple-element.19.live_ref, bf16[128,4096]{1,0:T(8,128)(2,1)S(1)} %get-tuple-element.20.rest_ref), custom_call_target="tpu_custom_call" | custom-call | tf_op jit(solution)/shard_map/pallas_call | solution.py:36
  28.4 0.0 copy-done
  28.5 0.4 %shard_map.78 = (f32[64,512]{1,0:T(8,128)S(1)}, bf16[256,512]{1,0:T(8,128)(2,1)S(1)}) custom-call(bf16[4,64,128]{2,1,0:T(8,128)(2,1)S(1)} %get-tuple-element.25.signal_ref, bf16[4,3,128,128]{3,2,1,0:T(8,128)(2,1)S(1)} %copy-done, bf16[4,64,128]{2,1,0:T(8,128)(2,1)S(1)} %get-tuple-element.26.basis_ref), custom_call_target="tpu_custom_call" | custom-call | tf_op jit(solution)/shard_map/pallas_call | solution.py:36
  28.8 0.0 collective-permute-done.6.across_ref
  28.9 0.0 collective-permute-done.7.along_ref
  28.9 0.1 shard_map.79.refs_3_
  29.0 0.4 %shard_map.76.refs_5_ = f32[128,128]{1,0:T(8,128)S(1)} custom-call(bf16[16,128,256]{2,1,0:T(8,128)(2,1)S(1)} %get-tuple-element.22.refs_0_, bf16[512,128]{1,0:T(8,128)(2,1)S(1)} %constant_dynamic-update-slice_fusion.refs_1_), custom_call_target="tpu_custom_call" | custom-call | tf_op jit(solution)/shard_map/pallas_call | solution.py:36
  29.4 0.0 collective-permute-done.4.refs_3_
  29.4 0.0 collective-permute-done.5.refs_4_
  29.4 0.8 %shard_map.77.refs_2_ = f32[128,128]{1,0:T(8,128)S(1)} custom-call(bf16[16,128,256]{2,1,0:T(8,128)(2,1)S(1)} %get-tuple-element.22.refs_0_, bf16[32,128,256]{2,1,0:T(8,128)(2,1)S(1)} %shard_map.75.refs_1_.refs_0_, bf16[512,128]{1,0:T(8,128)(2,1)S(1)} %collective-permute-done.2.refs_2_, bf16[512,128]{1,0:T(8,128)(2,1)S(1)} %collective-permute-done.4.refs_3_, ...), custom_call_target="tpu_custom_call" | custom-call | tf_op jit(solution)/shard_map/pallas_call | solution.py:36
  30.2 0.0 collective-permute-done.3.refs_1_
  30.2 1.2 %final.1 = bf16[4,64,128]{2,1,0:T(8,128)(2,1)} custom-call(bf16[32,128,256]{2,1,0:T(8,128)(2,1)S(1)} %shard_map.75.refs_1_.refs_0_, bf16[512,128]{1,0:T(8,128)(2,1)S(1)} %collective-permute-done.3.refs_1_, f32[128,128]{1,0:T(8,128)S(1)} %shard_map.77.refs_2_, f32[64,512]{1,0:T(8,128)S(1)} %shard_map.79.refs_3_, bf16[256,512]{1,0:T(8,128)(2,1)S(1)} %get-tuple-element.28.refs_4_), custom_call_target="tpu_custom_call" | custom-call | tf_op jit(solution)/shard_map/final/pallas_call | solution.py:351
  (5 shorter events, 0.0 us)
Async XLA Ops:
  1.2 4.5 %collective-permute-start = (bf16[128,128]{1,0:T(8,128)(2,1)S(1)}, bf16[128,128]{1,0:T(8,128)(2,1)S(1)}, u32[]{:S(2)}, u32[]{:S(2)}) collective-permute-start(bf16[128,128]{1,0:T(8,128)(2,1)S(1)} %get-tuple-element.21), channel_id=1, source_target_pairs={{0,4},{1,5},{2,6},{3,7},{4,0},{5,1},{6,2},{7,3},{8,12},{9,13},{10,... | collective-permute-start | bytes 98312 | tf_op jit(solution)/shard_map/ppermute | solution.py:252
  5.7 3.1 %collective-permute-start.1 = (bf16[256,128]{1,0:T(8,128)(2,1)S(1)}, bf16[256,128]{1,0:T(8,128)(2,1)S(1)}, u32[]{:S(2)}, u32[]{:S(2)}) collective-permute-start(bf16[256,128]{1,0:T(8,128)(2,1)S(1)} %pad_maximum_fusion.1), channel_id=1, source_target_pairs={{0,2},{1,3},{2,0},{3,1},{4,6},{5,7},{6,4},{7,5},{8,10},{9,11},{10,... | collective-permute-start | bytes 196616 | tf_op jit(solution)/shard_map/ppermute | solution.py:252
  8.8 3.9 %collective-permute-start.2 = (bf16[512,128]{1,0:T(8,128)(2,1)S(1)}, bf16[512,128]{1,0:T(8,128)(2,1)S(1)}, u32[]{:S(2)}, u32[]{:S(2)}) collective-permute-start(bf16[512,128]{1,0:T(8,128)(2,1)S(1)} %constant_dynamic-update-slice_fusion.refs_1_), channel_id=1, source_target_pairs={{0,1},{1,0},{2,3},{3,2},{4,5},{5,4},{6,7},{7,6},{8,9},{9,8},{10,11... | collective-permute-start | bytes 393224 | tf_op jit(solution)/shard_map/ppermute | solution.py:252
  12.7 16.7 %collective-permute-start.5 = (bf16[1024,128]{1,0:T(8,128)(2,1)S(1)}, bf16[1024,128]{1,0:T(8,128)(2,1)S(1)}, u32[]{:S(2)}, u32[]{:S(2)}) collective-permute-start(bf16[1024,128]{1,0:T(8,128)(2,1)S(1)} %pad_maximum_fusion), channel_id=1, source_target_pairs={{0,8},{8,0},{16,24},{24,16},{1,9},{9,1},{17,25},{25,17},{2,10},{10... | collective-permute-start | bytes 786440 | tf_op jit(solution)/shard_map/ppermute | solution.py:333
  17.0 12.4 %collective-permute-start.4 = (bf16[512,128]{1,0:T(8,128)(2,1)S(1)}, bf16[512,128]{1,0:T(8,128)(2,1)S(1)}, u32[]{:S(2)}, u32[]{:S(2)}) collective-permute-start(bf16[512,128]{1,0:T(8,128)(2,1)S(1)} %constant_dynamic-update-slice_fusion.refs_1_), channel_id=1, source_target_pairs={{0,24},{8,16},{16,8},{24,0},{1,25},{9,17},{17,9},{25,1},{2,26},{10... | collective-permute-start | bytes 393224 | tf_op jit(solution)/shard_map/ppermute | solution.py:322
  18.3 11.8 %collective-permute-start.3 = (bf16[512,128]{1,0:T(8,128)(2,1)S(1)}, bf16[512,128]{1,0:T(8,128)(2,1)S(1)}, u32[]{:S(2)}, u32[]{:S(2)}) collective-permute-start(bf16[512,128]{1,0:T(8,128)(2,1)S(1)} %collective-permute-done.2.refs_2_), channel_id=1, source_target_pairs={{0,24},{8,16},{16,8},{24,0},{1,25},{9,17},{17,9},{25,1},{2,26},{10... | collective-permute-start | bytes 393224 | tf_op jit(solution)/shard_map/ppermute | solution.py:332
  18.7 10.1 %collective-permute-start.6 = (bf16[64,128]{1,0:T(8,128)(2,1)S(1)}, bf16[64,128]{1,0:T(8,128)(2,1)S(1)}, u32[]{:S(2)}, u32[]{:S(2)}) collective-permute-start(bf16[64,128]{1,0:T(8,128)(2,1)S(1)} %get-tuple-element.23), channel_id=1, source_target_pairs={{0,1},{1,0},{2,3},{3,2},{4,5},{5,4},{6,7},{7,6},{8,9},{9,8},{10,11... | collective-permute-start | bytes 49160 | tf_op jit(solution)/shard_map/ppermute | solution.py:252
  20.2 8.7 %collective-permute-start.7 = (bf16[64,128]{1,0:T(8,128)(2,1)S(1)}, bf16[64,128]{1,0:T(8,128)(2,1)S(1)}, u32[]{:S(2)}, u32[]{:S(2)}) collective-permute-start(bf16[64,128]{1,0:T(8,128)(2,1)S(1)} %get-tuple-element.24), channel_id=1, source_target_pairs={{1,2},{3,4},{5,6},{7,8},{9,10},{11,12},{13,14},{15,16},{17,18},{19... | collective-permute-start | bytes 49160 | tf_op jit(solution)/shard_map/ppermute | solution.py:325
  25.6 2.9 %copy-start = (bf16[4,3,128,128]{3,2,1,0:T(8,128)(2,1)S(1)}, bf16[4,3,128,128]{3,2,1,0:T(8,128)(2,1)}, u32[]{:S(2)}) copy-start(bf16[4,3,128,128]{3,2,1,0:T(8,128)(2,1)} %near_ref.3) | copy-start | bytes 1179652

commit v2 on v1

--- a/solution.py
+++ b/solution.py
@@ -208,30 +208,38 @@
             spread_ref[start : start + TILES, c * LANES : (c + 1) * LANES] = wide[:, parity].astype(BF16)
 
 
-def halo_kernel(n_dev, across_ref, along_ref, near_ref, so_far_ref, total_ref):
-    cl_dev = near_ref.shape[0]
+def final_kernel(plan, pairs_piece, n_row, n_grp, *refs):
+    other_ref, partner_ref, along_ref, across_ref, near_ref = refs[1:6]
+    far_ref, near_total_ref, spread_ref, out_ref = refs[-4:]
+    cl_dev = out_ref.shape[0]
     row = lax.axis_index("row")
-    me = lax.axis_index("grp") * lax.axis_size("row") + row
+    group = lax.axis_index("grp")
     odd = (row & 1) == 1
+    odd_group = (group & 1) == 1
+    from_other = other_ref[other_ref.shape[0] - R :]
+    from_partner = partner_ref[partner_ref.shape[0] - R :]
+    before = jnp.where(odd_group, from_partner, from_other)
+    behind = jnp.where(odd_group, from_other, from_partner)
+    along = jnp.where(row == 0, before, jnp.where(row == n_row - 1, behind, along_ref[...]))
     across = across_ref[...]
-    along = along_ref[...]
     zero = jnp.zeros_like(across)
-    low = jnp.where(me == 0, zero, jnp.where(odd, across, along))
-    high = jnp.where(me == n_dev - 1, zero, jnp.where(odd, along, across))
-    total_ref[...] = so_far_ref[...]
-    total_ref[:, :LANES] += dot_nt(low, near_ref[0, 0])
-    total_ref[:, (cl_dev - 1) * LANES :] += dot_nt(high, near_ref[cl_dev - 1, 2])
-
-
-def final_kernel(plan, pairs_piece, *refs):
-    far_ref, near_total_ref, spread_ref, out_ref = refs[-4:]
+    is_first = (row == 0) & (group == 0)
+    is_last = (row == n_row - 1) & (group == n_grp - 1)
+    low = jnp.where(is_first, zero, jnp.where(odd, across, along))
+    high = jnp.where(is_last, zero, jnp.where(odd, along, across))
+    sides = {0: dot_nt(low, near_ref[0, 0])}
+    last = cl_dev - 1
+    sides[last] = dot_nt(high, near_ref[last, 2])
     pieces = [(refs[o], base, refs[p], places) for o, base, p, places in plan]
     total = far_pieces(far_ref[...], pieces, pairs_piece)
     turned = total.T.astype(BF16)
     lhs = jnp.concatenate([turned[p * R : (p + 1) * R] for p in range(HALVES)], axis=1)
     res = near_total_ref[...] + jnp.dot(lhs, spread_ref[...], preferred_element_type=F32)
-    for c in range(out_ref.shape[0]):
-        out_ref[c] = res[:, c * LANES : (c + 1) * LANES].astype(BF16)
+    for c in range(cl_dev):
+        here = res[:, c * LANES : (c + 1) * LANES]
+        if c in sides:
+            here = here + sides[c]
+        out_ref[c] = here.astype(BF16)
 
 
 def held(*values):
@@ -242,7 +250,6 @@
     cl_dev = signal.shape[0]
     n_row = lax.axis_size("row")
     n_grp = lax.axis_size("grp")
-    n_dev = n_row * n_grp
     gc = cl_dev * n_row
     pairs_piece = cl_dev // 2
     pairs_kind = gc // 2
@@ -309,36 +316,37 @@
         leaf_basis,
     )
 
+    row = lax.axis_index("row")
+
+    def packed(*values):
+        return jnp.concatenate(values, axis=0)
+
     places = [0]
     panel = mine
+    along = for_along
     bit = n_row // 2
     while bit > 1:
-        got = across_row(panel, bit)
-        panel = jnp.concatenate([panel, got], axis=0)
+        size = panel.shape[0]
+        got = across_row(packed(panel, along), bit)
+        panel = packed(panel, got[:size])
+        crosses = (row % bit == 0) | (row % bit == bit - 1)
+        along = jnp.where(crosses, got[size:], along)
         places = places + [p ^ bit for p in places]
         bit //= 2
-    over_y = across_row(panel, 1)
+    size = panel.shape[0]
+    got = across_row(packed(panel, along, for_across), 1)
+    over_y, along, across = got[:size], got[size : size + R], got[size + R :]
     places_y = [p ^ 1 for p in places]
     other_a = lax.ppermute(panel, "grp", others)
-    across = across_row(for_across, 1)
-    pairs = [(i, i + 1) for i in range(1, n_dev - 1, 2)]
-    along = lax.ppermute(for_along, ("grp", "row"), pairs + [(b, a) for a, b in pairs])
     own_far = call(
         functools.partial(far_kernel, [(0, 0, 1, places)], pairs_piece, False),
         [((height, LANES), F32)],
         own_operator,
         *held(panel),
     )
-    other_b = lax.ppermute(over_y, "grp", others)
-    partner = lax.ppermute(jnp.concatenate([panel, over_y], axis=0), "grp", partners)
-
-    with_halo = call(
-        functools.partial(halo_kernel, n_dev),
-        [((R, cl_dev * LANES), F32)],
-        *held(across, along),
-        near_blocks,
-        near_total,
-    )
+    other_b = lax.ppermute(packed(over_y, along), "grp", others)
+    partner = lax.ppermute(packed(panel, over_y, along), "grp", partners)
+
     plan = [(0, 0, 2, places_y), (1, pairs_kind, 3, places), (1, 0, 4, places + places_y)]
     far = call(
         functools.partial(far_kernel, plan, pairs_piece, True),
@@ -349,13 +357,22 @@
         own_far,
     )
     return pl.pallas_call(
-        functools.partial(final_kernel, [(0, pairs_kind, 1, places_y)], pairs_piece),
+        functools.partial(
+            final_kernel, [(0, pairs_kind, 1, places_y)], pairs_piece, n_row, n_grp
+        ),
         out_shape=jax.ShapeDtypeStruct(signal.shape, BF16),
-        in_specs=[pl.BlockSpec(memory_space=pltpu.VMEM)] * 5,
+        in_specs=[pl.BlockSpec(memory_space=pltpu.VMEM)] * 9,
         out_specs=pl.BlockSpec(memory_space=pltpu.VMEM),
         compiler_params=pltpu.CompilerParams(vmem_limit_bytes=4 << 20),
         name="final",
-    )(side_operator, *held(other_b), far, with_halo, spread)
+    )(
+        side_operator,
+        *held(other_b, partner, along, across),
+        near_blocks,
+        far,
+        near_total,
+        spread,
+    )
 
 
 def solution(mesh):

time: 31.6 us -> 27.9 us (0.88)
  starting transfers between devices: 18.9 us -> 12 us
  waiting for transfers between devices: 5.5 us -> 8.68 us
    ppermute x3 -> x2, starting transfers between devices: 10 us -> 4.52 us  [the longest x1 4.03 us: per_device(): partner = lax.ppermute(packed(panel, over_y, along), 'grp', partners)]
    ppermute x1, waiting for transfers between devices: 0.01 us -> 3.89 us  [per_device(): other_a = lax.ppermute(panel, 'grp', others)]
    ppermute x4 -> x3, waiting for transfers between devices: 5.49 us -> 3.32 us  [across_row(): return lax.ppermute(value, 'row', [(i, i ^ bit) for i in range(n_row)])]
    ppermute x3 -> x2, waiting for transfers between devices: 0.01 us -> 1.47 us  [the longest x1 1.46 us: per_device(): other_b = lax.ppermute(packed(over_y, along), 'grp', others)]
    ppermute x4 -> x3, starting transfers between devices: 7.44 us -> 6.06 us  [across_row(): return lax.ppermute(value, 'row', [(i, i ^ bit) for i in range(n_row)])]
    pallas_call x7 -> x6, Pallas kernels: 5.66 us -> 5.51 us  [call(): pl.pallas_call(kernel, out_shape=shapes[0] if single else shapes, in_spec...]
  transfers between devices with their start and end apart: 8 -> 6, of which waited for: 3 -> 4; matrix products, arithmetic and copies ran while one was open for 0% -> 0% of each run, Pallas kernels for 14% -> 16%
where the time goes in v2:
time: 27.9 us; the launch traced here: 27.6 us
  starting transfers between devices  12 us (43%)
  waiting for transfers between devices  8.68 us (31%)
  Pallas kernels  6.71 us (24%)
    ppermute x3, starting transfers between devices, across_row(): return lax.ppermute(value, 'row', [(i, i ^ bit) for i in range(n_row)])  6.06 us
    pallas_call x6, Pallas kernels, call(): pl.pallas_call(kernel, out_shape=shapes[0] if single else shapes, in_spec...  5.51 us
    ppermute x1, starting transfers between devices, per_device(): partner = lax.ppermute(packed(panel, over_y, along), 'grp', partners)  4.03 us
    ppermute x1, waiting for transfers between devices, per_device(): other_a = lax.ppermute(panel, 'grp', others)  3.89 us
    ppermute x3, waiting for transfers between devices, across_row(): return lax.ppermute(value, 'row', [(i, i ^ bit) for i in range(n_row)])  3.32 us
    ppermute x1, waiting for transfers between devices, per_device(): other_b = lax.ppermute(packed(over_y, along), 'grp', others)  1.46 us
    ppermute x1, starting transfers between devices, per_device(): other_a = lax.ppermute(panel, 'grp', others)  1.39 us
    pallas_call x1, Pallas kernels, per_device(): pl.pallas_call(functools.partial(final_kernel, [(0, pairs_kind, 1, places...  1.19 us
  transfers between devices with their start and end apart: 6, of which 4 were waited for; matrix products, arithmetic and copies ran while one was open for 0% of the time, Pallas kernels for 16%

profile of v2, /device:TPU:1, one launch (start us, length us, event | category | flops | bytes accessed | tf_op | source)
XLA Modules:
  0.0 27.6 jit_solution(15504395457769163636)
XLA Ops:
  0.0 1.1 %shard_map.73 = (bf16[4,64,128]{2,1,0:T(8,128)(2,1)S(1)}, bf16[4,64,128]{2,1,0:T(8,128)(2,1)S(1)}, s32[1,192]{1,0:T(1,128)S(1)}, s32[1,192]{1,0:T(1,128)S(1)}, s...) custom-call(bf16[4,64,128]{2,1,0:T(8,128)(2,1)} %refs_0_.1, ...), custom_call_target="tpu_custom_call" | custom-call | tf_op jit(solution)/shard_map/pallas_call | solution.py:36
  1.2 3.2 %collective-permute-start = (bf16[192,128]{1,0:T(8,128)(2,1)S(1)}, bf16[192,128]{1,0:T(8,128)(2,1)S(1)}, u32[]{:S(2)}, u32[]{:S(2)}) collective-permute-start(bf16[192,128]{1,0:T(8,128)(2,1)S(1)} %pad_maximum_fusion.3), channel_id=1, source_target_pairs={{0,4},{1,5},{2,6},{3,7},{4,0},{5,1},{6,2},{7,3},{8,12},{9,13},{10,... | collective-permute-start | bytes 147464 | tf_op jit(solution)/shard_map/ppermute | solution.py:259
  4.4 1.5 %collective-permute-done = bf16[192,128]{1,0:T(8,128)(2,1)S(1)} collective-permute-done((bf16[192,128]{1,0:T(8,128)(2,1)S(1)}, bf16[192,128]{1,0:T(8,128)(2,1)S(1)}, u32[]{:S(2)}, u32[]{:S(2)}) %collective-permute-start) | collective-permute-done | bytes 49184 | tf_op jit(solution)/shard_map/ppermute | solution.py:259
  5.9 1.5 %collective-permute-start.1 = (bf16[320,128]{1,0:T(8,128)(2,1)S(1)}, bf16[320,128]{1,0:T(8,128)(2,1)S(1)}, u32[]{:S(2)}, u32[]{:S(2)}) collective-permute-start(bf16[320,128]{1,0:T(8,128)(2,1)S(1)} %pad_maximum_fusion.2), channel_id=1, source_target_pairs={{0,2},{1,3},{2,0},{3,1},{4,6},{5,7},{6,4},{7,5},{8,10},{9,11},{10,... | collective-permute-start | bytes 245768 | tf_op jit(solution)/shard_map/ppermute | solution.py:259
  7.4 1.8 %collective-permute-done.1 = bf16[320,128]{1,0:T(8,128)(2,1)S(1)} collective-permute-done((bf16[320,128]{1,0:T(8,128)(2,1)S(1)}, bf16[320,128]{1,0:T(8,128)(2,1)S(1)}, u32[]{:S(2)}, u32[]{:S(2)}) %collective-permute-start.1) | collective-permute-done | bytes 81952 | tf_op jit(solution)/shard_map/ppermute | solution.py:259
  9.3 1.4 %collective-permute-start.2 = (bf16[640,128]{1,0:T(8,128)(2,1)S(1)}, bf16[640,128]{1,0:T(8,128)(2,1)S(1)}, u32[]{:S(2)}, u32[]{:S(2)}) collective-permute-start(bf16[640,128]{1,0:T(8,128)(2,1)S(1)} %constant_dynamic-update-slice_fusion), channel_id=1, source_target_pairs={{0,1},{1,0},{2,3},{3,2},{4,5},{5,4},{6,7},{7,6},{8,9},{9,8},{10,11... | collective-permute-start | bytes 491528 | tf_op jit(solution)/shard_map/ppermute | solution.py:259
  10.7 0.0 copy-start
  10.7 1.8 %shard_map.74 = (bf16[16,128,256]{2,1,0:T(8,128)(2,1)S(1)}, bf16[128,4096]{1,0:T(8,128)(2,1)S(1)}) custom-call(s32[1,192]{1,0:T(1,128)S(1)} %get-tuple-element.17.cols_ref, s32[1,192]{1,0:T(1,128)S(1)} %get-tuple-element.18.rows_ref, s32[1,192]{1,0:T(1,128)S(1)} %get-tuple-element.19.live_ref, bf16[192,4096]{1,0:T(8,128)(2,1)} %coupling_ref.1), custom_call_target="tpu_custom_call" | custom-call | tf_op jit(solution)/shard_map/pallas_call | solution.py:36
  12.5 1.1 %shard_map.75.refs_1_.refs_0_ = bf16[32,128,256]{2,1,0:T(8,128)(2,1)S(1)} custom-call(s32[1,192]{1,0:T(1,128)S(1)} %get-tuple-element.17.cols_ref, s32[1,192]{1,0:T(1,128)S(1)} %get-tuple-element.18.rows_ref, s32[1,192]{1,0:T(1,128)S(1)} %get-tuple-element.19.live_ref, bf16[128,4096]{1,0:T(8,128)(2,1)S(1)} %get-tuple-element.20.rest_ref), custom_call_target="tpu_custom_call" | custom-call | tf_op jit(solution)/shard_map/pallas_call | solution.py:36
  13.5 0.0 copy-done
  13.5 0.4 %shard_map.78 = (f32[64,512]{1,0:T(8,128)S(1)}, bf16[256,512]{1,0:T(8,128)(2,1)S(1)}) custom-call(bf16[4,64,128]{2,1,0:T(8,128)(2,1)S(1)} %get-tuple-element.25.signal_ref, bf16[4,3,128,128]{3,2,1,0:T(8,128)(2,1)S(1)} %copy-done, bf16[4,64,128]{2,1,0:T(8,128)(2,1)S(1)} %get-tuple-element.26.basis_ref), custom_call_target="tpu_custom_call" | custom-call | tf_op jit(solution)/shard_map/pallas_call | solution.py:36
  13.9 0.0 collective-permute-done.2
  14.0 4.0 %collective-permute-start.4 = (bf16[1088,128]{1,0:T(8,128)(2,1)S(1)}, bf16[1088,128]{1,0:T(8,128)(2,1)S(1)}, u32[]{:S(2)}, u32[]{:S(2)}) collective-permute-start(bf16[1088,128]{1,0:T(8,128)(2,1)S(1)} %pad_maximum_fusion), channel_id=1, source_target_pairs={{0,8},{8,0},{16,24},{24,16},{1,9},{9,1},{17,25},{25,17},{2,10},{10... | collective-permute-start | bytes 835592 | tf_op jit(solution)/shard_map/ppermute | solution.py:348
  18.0 1.4 %collective-permute-start.5 = (bf16[512,128]{1,0:T(8,128)(2,1)S(1)}, bf16[512,128]{1,0:T(8,128)(2,1)S(1)}, u32[]{:S(2)}, u32[]{:S(2)}) collective-permute-start(bf16[512,128]{1,0:T(8,128)(2,1)S(1)} %pad_maximum_fusion.1.refs_1_), channel_id=1, source_target_pairs={{0,24},{8,16},{16,8},{24,0},{1,25},{9,17},{17,9},{25,1},{2,26},{10... | collective-permute-start | bytes 393224 | tf_op jit(solution)/shard_map/ppermute | solution.py:340
  19.4 0.4 %shard_map.76.refs_5_ = f32[128,128]{1,0:T(8,128)S(1)} custom-call(bf16[16,128,256]{2,1,0:T(8,128)(2,1)S(1)} %get-tuple-element.24.refs_0_, bf16[512,128]{1,0:T(8,128)(2,1)S(1)} %pad_maximum_fusion.1.refs_1_), custom_call_target="tpu_custom_call" | custom-call | tf_op jit(solution)/shard_map/pallas_call | solution.py:36
  19.8 0.5 %collective-permute-start.3 = (bf16[576,128]{1,0:T(8,128)(2,1)S(1)}, bf16[576,128]{1,0:T(8,128)(2,1)S(1)}, u32[]{:S(2)}, u32[]{:S(2)}) collective-permute-start(bf16[576,128]{1,0:T(8,128)(2,1)S(1)} %concatenate.30), channel_id=1, source_target_pairs={{0,24},{8,16},{16,8},{24,0},{1,25},{9,17},{17,9},{25,1},{2,26},{10... | collective-permute-start | bytes 442376 | tf_op jit(solution)/shard_map/ppermute | solution.py:347
  20.3 3.9 %collective-permute-done.5.refs_3_ = bf16[512,128]{1,0:T(8,128)(2,1)S(1)} collective-permute-done((bf16[512,128]{1,0:T(8,128)(2,1)S(1)}, bf16[512,128]{1,0:T(8,128)(2,1)S(1)}, u32[]{:S(2)}, u32[]{:S(2)}) %collective-permute-start.5) | collective-permute-done | bytes 131104 | tf_op jit(solution)/shard_map/ppermute | solution.py:340
  24.2 0.0 collective-permute-done.4.refs_4_.refs_2_
  24.2 0.8 %shard_map.77.refs_6_ = f32[128,128]{1,0:T(8,128)S(1)} custom-call(bf16[16,128,256]{2,1,0:T(8,128)(2,1)S(1)} %get-tuple-element.24.refs_0_, bf16[32,128,256]{2,1,0:T(8,128)(2,1)S(1)} %shard_map.75.refs_1_.refs_0_, bf16[512,128]{1,0:T(8,128)(2,1)S(1)} %slice.36.refs_2_, bf16[512,128]{1,0:T(8,128)(2,1)S(1)} %collective-permute-done.5.refs_3_, ...), custom_call_target="tpu_custom_call" | custom-call | tf_op jit(solution)/shard_map/pallas_call | solution.py:36
  25.0 1.5 %collective-permute-done.3.refs_1_ = bf16[576,128]{1,0:T(8,128)(2,1)S(1)} collective-permute-done((bf16[576,128]{1,0:T(8,128)(2,1)S(1)}, bf16[576,128]{1,0:T(8,128)(2,1)S(1)}, u32[]{:S(2)}, u32[]{:S(2)}) %collective-permute-start.3) | collective-permute-done | bytes 147488 | tf_op jit(solution)/shard_map/ppermute | solution.py:347
  26.4 1.2 %final.1 = bf16[4,64,128]{2,1,0:T(8,128)(2,1)} custom-call(bf16[32,128,256]{2,1,0:T(8,128)(2,1)S(1)} %shard_map.75.refs_1_.refs_0_, bf16[576,128]{1,0:T(8,128)(2,1)S(1)} %collective-permute-done.3.refs_1_, bf16[1088,128]{1,0:T(8,128)(2,1)S(1)} %collective-permute-done.4.refs_4_.refs_2_, bf16[64,128]{1,0:T(8,128)(2,1)S(1)} %get-tuple-element.30.refs_3_, ...), custom_call_target="tpu_custom_call" | custom-call | tf_op jit(solution)/shard_map/final/pallas_call | solution.py:359
  (13 shorter events, 0.1 us)
Async XLA Ops:
  1.2 4.7 %collective-permute-start = (bf16[192,128]{1,0:T(8,128)(2,1)S(1)}, bf16[192,128]{1,0:T(8,128)(2,1)S(1)}, u32[]{:S(2)}, u32[]{:S(2)}) collective-permute-start(bf16[192,128]{1,0:T(8,128)(2,1)S(1)} %pad_maximum_fusion.3), channel_id=1, source_target_pairs={{0,4},{1,5},{2,6},{3,7},{4,0},{5,1},{6,2},{7,3},{8,12},{9,13},{10,... | collective-permute-start | bytes 147464 | tf_op jit(solution)/shard_map/ppermute | solution.py:259
  5.9 3.4 %collective-permute-start.1 = (bf16[320,128]{1,0:T(8,128)(2,1)S(1)}, bf16[320,128]{1,0:T(8,128)(2,1)S(1)}, u32[]{:S(2)}, u32[]{:S(2)}) collective-permute-start(bf16[320,128]{1,0:T(8,128)(2,1)S(1)} %pad_maximum_fusion.2), channel_id=1, source_target_pairs={{0,2},{1,3},{2,0},{3,1},{4,6},{5,7},{6,4},{7,5},{8,10},{9,11},{10,... | collective-permute-start | bytes 245768 | tf_op jit(solution)/shard_map/ppermute | solution.py:259
  9.3 4.6 %collective-permute-start.2 = (bf16[640,128]{1,0:T(8,128)(2,1)S(1)}, bf16[640,128]{1,0:T(8,128)(2,1)S(1)}, u32[]{:S(2)}, u32[]{:S(2)}) collective-permute-start(bf16[640,128]{1,0:T(8,128)(2,1)S(1)} %constant_dynamic-update-slice_fusion), channel_id=1, source_target_pairs={{0,1},{1,0},{2,3},{3,2},{4,5},{5,4},{6,7},{7,6},{8,9},{9,8},{10,11... | collective-permute-start | bytes 491528 | tf_op jit(solution)/shard_map/ppermute | solution.py:259
  10.7 2.9 %copy-start = (bf16[4,3,128,128]{3,2,1,0:T(8,128)(2,1)S(1)}, bf16[4,3,128,128]{3,2,1,0:T(8,128)(2,1)}, u32[]{:S(2)}) copy-start(bf16[4,3,128,128]{3,2,1,0:T(8,128)(2,1)} %refs_5_.1) | copy-start | bytes 1179652
  14.0 10.2 %collective-permute-start.4 = (bf16[1088,128]{1,0:T(8,128)(2,1)S(1)}, bf16[1088,128]{1,0:T(8,128)(2,1)S(1)}, u32[]{:S(2)}, u32[]{:S(2)}) collective-permute-start(bf16[1088,128]{1,0:T(8,128)(2,1)S(1)} %pad_maximum_fusion), channel_id=1, source_target_pairs={{0,8},{8,0},{16,24},{24,16},{1,9},{9,1},{17,25},{25,17},{2,10},{10... | collective-permute-start | bytes 835592 | tf_op jit(solution)/shard_map/ppermute | solution.py:348
  18.0 6.2 %collective-permute-start.5 = (bf16[512,128]{1,0:T(8,128)(2,1)S(1)}, bf16[512,128]{1,0:T(8,128)(2,1)S(1)}, u32[]{:S(2)}, u32[]{:S(2)}) collective-permute-start(bf16[512,128]{1,0:T(8,128)(2,1)S(1)} %pad_maximum_fusion.1.refs_1_), channel_id=1, source_target_pairs={{0,24},{8,16},{16,8},{24,0},{1,25},{9,17},{17,9},{25,1},{2,26},{10... | collective-permute-start | bytes 393224 | tf_op jit(solution)/shard_map/ppermute | solution.py:340
  19.8 6.7 %collective-permute-start.3 = (bf16[576,128]{1,0:T(8,128)(2,1)S(1)}, bf16[576,128]{1,0:T(8,128)(2,1)S(1)}, u32[]{:S(2)}, u32[]{:S(2)}) collective-permute-start(bf16[576,128]{1,0:T(8,128)(2,1)S(1)} %concatenate.30), channel_id=1, source_target_pairs={{0,24},{8,16},{16,8},{24,0},{1,25},{9,17},{17,9},{25,1},{2,26},{10... | collective-permute-start | bytes 442376 | tf_op jit(solution)/shard_map/ppermute | solution.py:347

commit v3 on v2

--- a/solution.py
+++ b/solution.py
@@ -321,44 +321,65 @@
     def packed(*values):
         return jnp.concatenate(values, axis=0)
 
+    row = lax.axis_index("row")
+
+    def packed(*values):
+        return jnp.concatenate(values, axis=0)
+
     places = [0]
     panel = mine
     along = for_along
     bit = n_row // 2
+    over_ya = None
     while bit > 1:
         size = panel.shape[0]
         got = across_row(packed(panel, along), bit)
+        if bit == 2:
+            over_ya = across_row(panel, 1)
+            other_a = lax.ppermute(panel, "grp", others)
         panel = packed(panel, got[:size])
         crosses = (row % bit == 0) | (row % bit == bit - 1)
         along = jnp.where(crosses, got[size:], along)
         places = places + [p ^ bit for p in places]
         bit //= 2
-    size = panel.shape[0]
-    got = across_row(packed(panel, along, for_across), 1)
-    over_y, along, across = got[:size], got[size : size + R], got[size + R :]
+    size = panel.shape[0] // 2
     places_y = [p ^ 1 for p in places]
-    other_a = lax.ppermute(panel, "grp", others)
+    half = len(places) // 2
+    got = across_row(packed(panel[size:], along, for_across), 1)
+    leaps = [
+        (g * n_row + r, h * n_row + (r ^ 1)) for g, h in others for r in range(n_row)
+    ]
+    other_b = lax.ppermute(packed(panel[size:], along), ("grp", "row"), leaps)
+    over_yb, along, across = got[:size], got[size : size + R], got[size + R :]
+    early_part = packed(panel, over_ya)
+    early_places = places + places_y[:half]
+    late_places = places_y[half:]
+    other_c = lax.ppermute(packed(panel[size:], over_ya), "grp", others)
     own_far = call(
-        functools.partial(far_kernel, [(0, 0, 1, places)], pairs_piece, False),
+        functools.partial(far_kernel, [(0, 0, 1, early_places)], pairs_piece, False),
         [((height, LANES), F32)],
         own_operator,
-        *held(panel),
-    )
-    other_b = lax.ppermute(packed(over_y, along), "grp", others)
-    partner = lax.ppermute(packed(panel, over_y, along), "grp", partners)
-
-    plan = [(0, 0, 2, places_y), (1, pairs_kind, 3, places), (1, 0, 4, places + places_y)]
+        *held(early_part),
+    )
+    partner = lax.ppermute(packed(early_part, over_yb, along), "grp", partners)
+
+    plan = [
+        (0, 0, 2, late_places),
+        (1, pairs_kind, 3, places[:half]),
+        (1, 0, 4, early_places + late_places),
+        (1, pairs_kind, 5, places[half:] + places_y[:half]),
+    ]
     far = call(
         functools.partial(far_kernel, plan, pairs_piece, True),
         [((height, LANES), F32)],
         own_operator,
         side_operator,
-        *held(over_y, other_a, partner),
+        *held(over_yb, other_a, partner, other_c),
         own_far,
     )
     return pl.pallas_call(
         functools.partial(
-            final_kernel, [(0, pairs_kind, 1, places_y)], pairs_piece, n_row, n_grp
+            final_kernel, [(0, pairs_kind, 1, late_places)], pairs_piece, n_row, n_grp
         ),
         out_shape=jax.ShapeDtypeStruct(signal.shape, BF16),
         in_specs=[pl.BlockSpec(memory_space=pltpu.VMEM)] * 9,

time: 27.9 us -> 36.2 us (1.30)
  the two profiles are of different devices: /device:TPU:1 before, /device:TPU:0 now
where the time goes in v3:
time: 36.2 us; the launch traced here: 35.6 us
  starting transfers between devices  10.4 us (29%)
  local copies, waits for them, and re-layouts  9.36 us (26%)
  Pallas kernels  6.68 us (18%)
  waiting for transfers between devices  5.29 us (15%)
  other arithmetic  3.64 us (10%)
    unnamed x32, local copies, waits for them, and re-layouts  8.72 us
    ppermute x4, starting transfers between devices, across_row(): return lax.ppermute(value, 'row', [(i, i ^ bit) for i in range(n_row)])  8.67 us
    pallas_call x6, Pallas kernels, call(): pl.pallas_call(kernel, out_shape=shapes[0] if single else shapes, in_spec...  5.56 us
    ppermute x4, waiting for transfers between devices, across_row(): return lax.ppermute(value, 'row', [(i, i ^ bit) for i in range(n_row)])  4.17 us
    concatenate x7, other arithmetic, packed(): return jnp.concatenate(values, axis=0)  2.91 us
    ppermute x1, starting transfers between devices, per_device(): other_b = lax.ppermute(packed(panel[size:], along), ('grp', 'row'), leaps)  1.12 us
    pallas_call x1, Pallas kernels, per_device(): pl.pallas_call(functools.partial(final_kernel, [(0, pairs_kind, 1, late_p...  1.12 us
    ppermute x1, waiting for transfers between devices, per_device(): partner = lax.ppermute(packed(early_part, over_yb, along), 'grp', partners)  1.11 us
  transfers between devices with their start and end apart: 8, of which 3 were waited for; matrix products, arithmetic and copies ran while one was open for 11% of the time, Pallas kernels for 12%

profile of v3, /device:TPU:0, one launch (start us, length us, event | category | flops | bytes accessed | tf_op | source)
XLA Modules:
  0.0 35.6 jit_solution(1809890147980324267)
XLA Ops:
  0.0 1.2 %shard_map.73 = (bf16[4,64,128]{2,1,0:T(8,128)(2,1)S(1)}, bf16[4,64,128]{2,1,0:T(8,128)(2,1)S(1)}, s32[1,192]{1,0:T(1,128)S(1)}, s32[1,192]{1,0:T(1,128)S(1)}, s...) custom-call(bf16[4,64,128]{2,1,0:T(8,128)(2,1)} %refs_0_.1, ...), custom_call_target="tpu_custom_call" | custom-call | tf_op jit(solution)/shard_map/pallas_call | solution.py:36
  1.2 0.6 %copy-done.3 = bf16[4,64,128]{2,1,0:T(8,128)(2,1)} copy-done((bf16[4,64,128]{2,1,0:T(8,128)(2,1)}, bf16[4,64,128]{2,1,0:T(8,128)(2,1)S(1)}, u32[]{:S(2)}) %copy-start.3) | copy-done | bytes 65560
  1.8 0.6 %copy-done.5 = bf16[4,64,128]{2,1,0:T(8,128)(2,1)} copy-done((bf16[4,64,128]{2,1,0:T(8,128)(2,1)}, bf16[4,64,128]{2,1,0:T(8,128)(2,1)S(1)}, u32[]{:S(2)}) %copy-start.5) | copy-done | bytes 65560
  2.4 0.6 %copy-done.7 = bf16[64,128]{1,0:T(8,128)(2,1)} copy-done((bf16[64,128]{1,0:T(8,128)(2,1)}, bf16[64,128]{1,0:T(8,128)(2,1)S(1)}, u32[]{:S(2)}) %copy-start.7) | copy-done | bytes 16408
  3.0 0.6 %pad_maximum_fusion.6 = bf16[192,128]{1,0:T(8,128)(2,1)} fusion(bf16[64,128]{1,0:T(8,128)(2,1)S(1)} %get-tuple-element.22, bf16[128,128]{1,0:T(8,128)(2,1)S(1)} %get-tuple-element.21), kind=kLoop, calls=%fused_computation.7 | loop fusion | flops 98304 | bytes 98304 | tf_op jit(solution)/shard_map/concatenate | solution.py:327
  3.7 4.1 %collective-permute-start = (bf16[192,128]{1,0:T(8,128)(2,1)}, bf16[192,128]{1,0:T(8,128)(2,1)}, u32[]{:S(2)}, u32[]{:S(2)}) collective-permute-start(bf16[192,128]{1,0:T(8,128)(2,1)} %pad_maximum_fusion.6), channel_id=1, source_target_pairs={{0,4},{1,5},{2,6},{3,7},{4,0},{5,1},{6,2},{7,3},{8,12},{9,13},{10,... | collective-permute-start | bytes 147464 | tf_op jit(solution)/shard_map/ppermute | solution.py:259
  7.7 0.6 %constant_dynamic-update-slice_fusion.3 = bf16[1088,128]{1,0:T(8,128)(2,1)} fusion(bf16[128,128]{1,0:T(8,128)(2,1)S(1)} %get-tuple-element.21), kind=kLoop, calls=%fused_computation.13 | loop fusion | bytes 65536
  8.3 1.8 %shard_map.74 = (bf16[16,128,256]{2,1,0:T(8,128)(2,1)S(1)}, bf16[128,4096]{1,0:T(8,128)(2,1)S(1)}) custom-call(s32[1,192]{1,0:T(1,128)S(1)} %get-tuple-element.17.cols_ref, s32[1,192]{1,0:T(1,128)S(1)} %get-tuple-element.18.rows_ref, s32[1,192]{1,0:T(1,128)S(1)} %get-tuple-element.19.live_ref, bf16[192,4096]{1,0:T(8,128)(2,1)} %coupling_ref.1), custom_call_target="tpu_custom_call" | custom-call | tf_op jit(solution)/shard_map/pallas_call | solution.py:36
  10.2 0.7 %copy-done.9 = s32[1,192]{1,0:T(1,128)S(1)} copy-done((s32[1,192]{1,0:T(1,128)S(1)}, s32[1,192]{1,0:T(1,128)}, u32[]{:S(2)}) %copy-start.9) | copy-done | bytes 792
  10.8 0.6 %copy-done.11 = s32[1,192]{1,0:T(1,128)S(1)} copy-done((s32[1,192]{1,0:T(1,128)S(1)}, s32[1,192]{1,0:T(1,128)}, u32[]{:S(2)}) %copy-start.11) | copy-done | bytes 792
  11.5 0.7 %copy-done.13 = s32[1,192]{1,0:T(1,128)S(1)} copy-done((s32[1,192]{1,0:T(1,128)S(1)}, s32[1,192]{1,0:T(1,128)}, u32[]{:S(2)}) %copy-start.13) | copy-done | bytes 792
  12.1 1.1 %shard_map.75.refs_1_.refs_0_ = bf16[32,128,256]{2,1,0:T(8,128)(2,1)S(1)} custom-call(s32[1,192]{1,0:T(1,128)S(1)} %copy-done.9, s32[1,192]{1,0:T(1,128)S(1)} %copy-done.11, s32[1,192]{1,0:T(1,128)S(1)} %copy-done.13, bf16[128,4096]{1,0:T(8,128)(2,1)S(1)} %get-tuple-element.20.rest_ref), custom_call_target="tpu_custom_call" | custom-call | tf_op jit(solution)/shard_map/pallas_call | solution.py:36
  13.2 0.8 %copy-done.4 = bf16[4,64,128]{2,1,0:T(8,128)(2,1)S(1)} copy-done((bf16[4,64,128]{2,1,0:T(8,128)(2,1)S(1)}, bf16[4,64,128]{2,1,0:T(8,128)(2,1)}, u32[]{:S(2)}) %copy-start.4) | copy-done | bytes 65560
  14.1 0.8 %copy-done.6 = bf16[4,64,128]{2,1,0:T(8,128)(2,1)S(1)} copy-done((bf16[4,64,128]{2,1,0:T(8,128)(2,1)S(1)}, bf16[4,64,128]{2,1,0:T(8,128)(2,1)}, u32[]{:S(2)}) %copy-start.6) | copy-done | bytes 65560
  15.3 0.7 %slice_select_fusion.1 = bf16[64,128]{1,0:T(8,128)(2,1)S(1)} fusion(bf16[64,128]{1,0:T(8,128)(2,1)S(1)} %get-tuple-element.22, bf16[192,128]{1,0:T(8,128)(2,1)} %collective-permute-done, pred[]{:T(512)S(6)} %or.6), kind=kLoop, calls=%fused_computation.9 | loop fusion | flops 8192 | bytes 49153 | tf_op jit(solution)/shard_map/jit(_where)/select_n | solution.py:342
  16.0 1.4 %constant_dynamic-update-slice_fusion.2 = (bf16[1088,128]{1,0:T(8,128)(2,1)}, bf16[128,128]{1,0:T(8,128)(2,1)S(1)}) fusion(bf16[1088,128]{1,0:T(8,128)(2,1)} %constant_dynamic-update-slice_fusion.3, bf16[192,128]{1,0:T(8,128)(2,1)} %collective-permute-done), kind=kLoop, calls=%fused_computation.12 | loop fusion | bytes 98304
  17.4 0.8 %pad_maximum_fusion.3 = bf16[320,128]{1,0:T(8,128)(2,1)S(1)} fusion(bf16[64,128]{1,0:T(8,128)(2,1)S(1)} %slice_select_fusion.1, bf16[128,128]{1,0:T(8,128)(2,1)S(1)} %get-tuple-element.34, bf16[128,128]{1,0:T(8,128)(2,1)} %copy-done.1), kind=kLoop, calls=%fused_computation.4 | loop fusion | flops 245760 | bytes 163840 | tf_op jit(solution)/shard_map/concatenate | solution.py:327
  18.1 1.6 %collective-permute-start.1 = (bf16[320,128]{1,0:T(8,128)(2,1)S(1)}, bf16[320,128]{1,0:T(8,128)(2,1)S(1)}, u32[]{:S(2)}, u32[]{:S(2)}) collective-permute-start(bf16[320,128]{1,0:T(8,128)(2,1)S(1)} %pad_maximum_fusion.3), channel_id=1, source_target_pairs={{0,2},{1,3},{2,0},{3,1},{4,6},{5,7},{6,4},{7,5},{8,10},{9,11},{10,... | collective-permute-start | bytes 245768 | tf_op jit(solution)/shard_map/ppermute | solution.py:259
  19.7 0.8 %pad_maximum_fusion.5 = bf16[256,128]{1,0:T(8,128)(2,1)S(1)} fusion(bf16[128,128]{1,0:T(8,128)(2,1)S(1)} %get-tuple-element.34, bf16[128,128]{1,0:T(8,128)(2,1)} %copy-done.1), kind=kLoop, calls=%fused_computation.6 | loop fusion | flops 131072 | bytes 131072 | tf_op jit(solution)/shard_map/concatenate | solution.py:327
  20.5 1.5 %collective-permute-start.3 = (bf16[256,128]{1,0:T(8,128)(2,1)S(1)}, bf16[256,128]{1,0:T(8,128)(2,1)S(1)}, u32[]{:S(2)}, u32[]{:S(2)}) collective-permute-start(bf16[256,128]{1,0:T(8,128)(2,1)S(1)} %pad_maximum_fusion.5), channel_id=1, source_target_pairs={{0,1},{1,0},{2,3},{3,2},{4,5},{5,4},{6,7},{7,6},{8,9},{9,8},{10,11... | collective-permute-start | bytes 196616 | tf_op jit(solution)/shard_map/ppermute | solution.py:259
  22.1 0.5 %collective-permute-done.1 = bf16[320,128]{1,0:T(8,128)(2,1)S(1)} collective-permute-done((bf16[320,128]{1,0:T(8,128)(2,1)S(1)}, bf16[320,128]{1,0:T(8,128)(2,1)S(1)}, u32[]{:S(2)}, u32[]{:S(2)}) %collective-permute-start.1) | collective-permute-done | bytes 81952 | tf_op jit(solution)/shard_map/ppermute | solution.py:259
  22.6 0.6 %constant_dynamic-update-slice_fusion.1 = (bf16[1088,128]{1,0:T(8,128)(2,1)}, bf16[256,128]{1,0:T(8,128)(2,1)S(1)}) fusion(bf16[1088,128]{1,0:T(8,128)(2,1)} %get-tuple-element.33, bf16[320,128]{1,0:T(8,128)(2,1)S(1)} %collective-permute-done.1), kind=kLoop, calls=%fused_computation.11 | loop fusion | bytes 196608
  23.2 1.1 %collective-permute-start.2 = (bf16[320,128]{1,0:T(8,128)(2,1)S(1)}, bf16[320,128]{1,0:T(8,128)(2,1)S(1)}, u32[]{:S(2)}, u32[]{:S(2)}) collective-permute-start(bf16[320,128]{1,0:T(8,128)(2,1)S(1)} %pad_maximum_fusion.4), channel_id=1, source_target_pairs={{0,25},{1,24},{2,27},{3,26},{4,29},{5,28},{6,31},{7,30},{8,17},{9,... | collective-permute-start | bytes 245768 | tf_op jit(solution)/shard_map/ppermute | solution.py:352
  24.4 0.7 %pad_maximum_fusion.2 = bf16[384,128]{1,0:T(8,128)(2,1)S(1)} fusion(bf16[64,128]{1,0:T(8,128)(2,1)} %copy-done.7, bf16[64,128]{1,0:T(8,128)(2,1)S(1)} %slice_select_fusion, bf16[256,128]{1,0:T(8,128)(2,1)S(1)} %get-tuple-element.32), kind=kLoop, calls=%fused_computation.2 | loop fusion | flops 294912 | bytes 196608 | tf_op jit(solution)/shard_map/concatenate | solution.py:327
  25.1 1.5 %collective-permute-start.4 = (bf16[384,128]{1,0:T(8,128)(2,1)S(1)}, bf16[384,128]{1,0:T(8,128)(2,1)S(1)}, u32[]{:S(2)}, u32[]{:S(2)}) collective-permute-start(bf16[384,128]{1,0:T(8,128)(2,1)S(1)} %pad_maximum_fusion.2), channel_id=1, source_target_pairs={{0,1},{1,0},{2,3},{3,2},{4,5},{5,4},{6,7},{7,6},{8,9},{9,8},{10,11... | collective-permute-start | bytes 294920 | tf_op jit(solution)/shard_map/ppermute | solution.py:259
  27.0 0.6 %constant_dynamic-update-slice_fusion = bf16[1088,128]{1,0:T(8,128)(2,1)} fusion(bf16[1088,128]{1,0:T(8,128)(2,1)} %get-tuple-element.31, bf16[256,128]{1,0:T(8,128)(2,1)S(1)} %collective-permute-done.3), kind=kLoop, calls=%fused_computation.10 | loop fusion | bytes 131072
  27.6 3.7 %collective-permute-done.4 = bf16[384,128]{1,0:T(8,128)(2,1)S(1)} collective-permute-done((bf16[384,128]{1,0:T(8,128)(2,1)S(1)}, bf16[384,128]{1,0:T(8,128)(2,1)S(1)}, u32[]{:S(2)}, u32[]{:S(2)}) %collective-permute-start.4) | collective-permute-done | bytes 98336 | tf_op jit(solution)/shard_map/ppermute | solution.py:259
  31.3 0.6 %slice_dynamic-update-slice_fusion = bf16[1088,128]{1,0:T(8,128)(2,1)} fusion(bf16[1088,128]{1,0:T(8,128)(2,1)} %constant_dynamic-update-slice_fusion, bf16[384,128]{1,0:T(8,128)(2,1)S(1)} %collective-permute-done.4), kind=kLoop, calls=%fused_computation.3 | loop fusion | bytes 163840 | tf_op jit(solution)/shard_map/concatenate | solution.py:327
  32.1 0.4 %shard_map.76.refs_6_ = f32[128,128]{1,0:T(8,128)S(1)} custom-call(bf16[16,128,256]{2,1,0:T(8,128)(2,1)S(1)} %get-tuple-element.24.refs_0_, bf16[768,128]{1,0:T(8,128)(2,1)S(1)} %pad_maximum_fusion.refs_1_), custom_call_target="tpu_custom_call" | custom-call | tf_op jit(solution)/shard_map/pallas_call | solution.py:36
  32.6 1.1 %collective-permute-done.5.refs_4_.refs_2_ = bf16[1088,128]{1,0:T(8,128)(2,1)S(1)} collective-permute-done((bf16[1088,128]{1,0:T(8,128)(2,1)}, bf16[1088,128]{1,0:T(8,128)(2,1)S(1)}, u32[]{:S(2)}, u32[]{:S(2)}) %collective-permute-start.5) | collective-permute-done | bytes 278560 | tf_op jit(solution)/shard_map/ppermute | solution.py:364
  33.7 0.8 %shard_map.77.refs_6_ = f32[128,128]{1,0:T(8,128)S(1)} custom-call(bf16[16,128,256]{2,1,0:T(8,128)(2,1)S(1)} %get-tuple-element.24.refs_0_, bf16[32,128,256]{2,1,0:T(8,128)(2,1)S(1)} %shard_map.75.refs_1_.refs_0_, bf16[256,128]{1,0:T(8,128)(2,1)S(1)} %slice.39.refs_2_, bf16[256,128]{1,0:T(8,128)(2,1)S(1)} %collective-permute-done.6.refs_3_, ...), custom_call_target="tpu_custom_call" | custom-call | tf_op jit(solution)/shard_map/pallas_call | solution.py:36
  34.5 1.1 %final.1 = bf16[4,64,128]{2,1,0:T(8,128)(2,1)} custom-call(bf16[32,128,256]{2,1,0:T(8,128)(2,1)S(1)} %shard_map.75.refs_1_.refs_0_, bf16[320,128]{1,0:T(8,128)(2,1)S(1)} %collective-permute-done.2.refs_1_, bf16[1088,128]{1,0:T(8,128)(2,1)S(1)} %collective-permute-done.5.refs_4_.refs_2_, bf16[64,128]{1,0:T(8,128)(2,1)S(1)} %get-tuple-element.30.refs_3_, ...), custom_call_target="tpu_custom_call" | custom-call | tf_op jit(solution)/shard_map/final/pallas_call | solution.py:380
  (35 shorter events, 1.1 us)
Async XLA Ops:
  1.2 0.6 %copy-start.3 = (bf16[4,64,128]{2,1,0:T(8,128)(2,1)}, bf16[4,64,128]{2,1,0:T(8,128)(2,1)S(1)}, u32[]{:S(2)}) copy-start(bf16[4,64,128]{2,1,0:T(8,128)(2,1)S(1)} %get-tuple-element.25.signal_ref) | copy-start | bytes 196612
  1.8 0.6 %copy-start.5 = (bf16[4,64,128]{2,1,0:T(8,128)(2,1)}, bf16[4,64,128]{2,1,0:T(8,128)(2,1)S(1)}, u32[]{:S(2)}) copy-start(bf16[4,64,128]{2,1,0:T(8,128)(2,1)S(1)} %get-tuple-element.26.basis_ref) | copy-start | bytes 196612
  2.4 0.6 %copy-start.7 = (bf16[64,128]{1,0:T(8,128)(2,1)}, bf16[64,128]{1,0:T(8,128)(2,1)S(1)}, u32[]{:S(2)}) copy-start(bf16[64,128]{1,0:T(8,128)(2,1)S(1)} %get-tuple-element.23) | copy-start | bytes 49156
  3.0 4.7 %copy-start.1 = (bf16[128,128]{1,0:T(8,128)(2,1)}, bf16[128,128]{1,0:T(8,128)(2,1)S(1)}, u32[]{:S(2)}) copy-start(bf16[128,128]{1,0:T(8,128)(2,1)S(1)} %get-tuple-element.21) | copy-start | bytes 98308
  3.0 7.1 %copy-start.8 = (s32[1,192]{1,0:T(1,128)}, s32[1,192]{1,0:T(1,128)S(1)}, u32[]{:S(2)}) copy-start(s32[1,192]{1,0:T(1,128)S(1)} %get-tuple-element.17.cols_ref) | copy-start | bytes 2308
  3.0 7.1 %copy-start.10 = (s32[1,192]{1,0:T(1,128)}, s32[1,192]{1,0:T(1,128)S(1)}, u32[]{:S(2)}) copy-start(s32[1,192]{1,0:T(1,128)S(1)} %get-tuple-element.18.rows_ref) | copy-start | bytes 2308
  3.0 7.1 %copy-start.12 = (s32[1,192]{1,0:T(1,128)}, s32[1,192]{1,0:T(1,128)S(1)}, u32[]{:S(2)}) copy-start(s32[1,192]{1,0:T(1,128)S(1)} %get-tuple-element.19.live_ref) | copy-start | bytes 2308
  3.7 11.6 %collective-permute-start = (bf16[192,128]{1,0:T(8,128)(2,1)}, bf16[192,128]{1,0:T(8,128)(2,1)}, u32[]{:S(2)}, u32[]{:S(2)}) collective-permute-start(bf16[192,128]{1,0:T(8,128)(2,1)} %pad_maximum_fusion.6), channel_id=1, source_target_pairs={{0,4},{1,5},{2,6},{3,7},{4,0},{5,1},{6,2},{7,3},{8,12},{9,13},{10,... | collective-permute-start | bytes 147464 | tf_op jit(solution)/shard_map/ppermute | solution.py:259
  8.3 4.9 %copy-start = (bf16[4,3,128,128]{3,2,1,0:T(8,128)(2,1)S(1)}, bf16[4,3,128,128]{3,2,1,0:T(8,128)(2,1)}, u32[]{:S(2)}) copy-start(bf16[4,3,128,128]{3,2,1,0:T(8,128)(2,1)} %refs_5_.1) | copy-start | bytes 1179652
  10.2 0.7 %copy-start.9 = (s32[1,192]{1,0:T(1,128)S(1)}, s32[1,192]{1,0:T(1,128)}, u32[]{:S(2)}) copy-start(s32[1,192]{1,0:T(1,128)} %copy-done.8) | copy-start | bytes 2308
  10.8 0.6 %copy-start.11 = (s32[1,192]{1,0:T(1,128)S(1)}, s32[1,192]{1,0:T(1,128)}, u32[]{:S(2)}) copy-start(s32[1,192]{1,0:T(1,128)} %copy-done.10) | copy-start | bytes 2308
  11.5 0.7 %copy-start.13 = (s32[1,192]{1,0:T(1,128)S(1)}, s32[1,192]{1,0:T(1,128)}, u32[]{:S(2)}) copy-start(s32[1,192]{1,0:T(1,128)} %copy-done.12) | copy-start | bytes 2308
  13.2 18.9 %copy-start.2 = (bf16[128,128]{1,0:T(8,128)(2,1)S(1)}, bf16[128,128]{1,0:T(8,128)(2,1)}, u32[]{:S(2)}) copy-start(bf16[128,128]{1,0:T(8,128)(2,1)} %copy-done.1) | copy-start | bytes 98308
  13.2 0.8 %copy-start.4 = (bf16[4,64,128]{2,1,0:T(8,128)(2,1)S(1)}, bf16[4,64,128]{2,1,0:T(8,128)(2,1)}, u32[]{:S(2)}) copy-start(bf16[4,64,128]{2,1,0:T(8,128)(2,1)} %copy-done.3) | copy-start | bytes 196612
  14.1 0.8 %copy-start.6 = (bf16[4,64,128]{2,1,0:T(8,128)(2,1)S(1)}, bf16[4,64,128]{2,1,0:T(8,128)(2,1)}, u32[]{:S(2)}) copy-start(bf16[4,64,128]{2,1,0:T(8,128)(2,1)} %copy-done.5) | copy-start | bytes 196612
  18.1 4.4 %collective-permute-start.1 = (bf16[320,128]{1,0:T(8,128)(2,1)S(1)}, bf16[320,128]{1,0:T(8,128)(2,1)S(1)}, u32[]{:S(2)}, u32[]{:S(2)}) collective-permute-start(bf16[320,128]{1,0:T(8,128)(2,1)S(1)} %pad_maximum_fusion.3), channel_id=1, source_target_pairs={{0,2},{1,3},{2,0},{3,1},{4,6},{5,7},{6,4},{7,5},{8,10},{9,11},{10,... | collective-permute-start | bytes 245768 | tf_op jit(solution)/shard_map/ppermute | solution.py:259
  20.5 6.1 %collective-permute-start.3 = (bf16[256,128]{1,0:T(8,128)(2,1)S(1)}, bf16[256,128]{1,0:T(8,128)(2,1)S(1)}, u32[]{:S(2)}, u32[]{:S(2)}) collective-permute-start(bf16[256,128]{1,0:T(8,128)(2,1)S(1)} %pad_maximum_fusion.5), channel_id=1, source_target_pairs={{0,1},{1,0},{2,3},{3,2},{4,5},{5,4},{6,7},{7,6},{8,9},{9,8},{10,11... | collective-permute-start | bytes 196616 | tf_op jit(solution)/shard_map/ppermute | solution.py:259
  22.0 10.5 %collective-permute-start.6 = (bf16[256,128]{1,0:T(8,128)(2,1)S(1)}, bf16[256,128]{1,0:T(8,128)(2,1)S(1)}, u32[]{:S(2)}, u32[]{:S(2)}) collective-permute-start(bf16[256,128]{1,0:T(8,128)(2,1)S(1)} %pad_maximum_fusion.5), channel_id=1, source_target_pairs={{0,24},{8,16},{16,8},{24,0},{1,25},{9,17},{17,9},{25,1},{2,26},{10... | collective-permute-start | bytes 196616 | tf_op jit(solution)/shard_map/ppermute | solution.py:339
  23.2 11.2 %collective-permute-start.2 = (bf16[320,128]{1,0:T(8,128)(2,1)S(1)}, bf16[320,128]{1,0:T(8,128)(2,1)S(1)}, u32[]{:S(2)}, u32[]{:S(2)}) collective-permute-start(bf16[320,128]{1,0:T(8,128)(2,1)S(1)} %pad_maximum_fusion.4), channel_id=1, source_target_pairs={{0,25},{1,24},{2,27},{3,26},{4,29},{5,28},{6,31},{7,30},{8,17},{9,... | collective-permute-start | bytes 245768 | tf_op jit(solution)/shard_map/ppermute | solution.py:352
  25.1 6.2 %collective-permute-start.4 = (bf16[384,128]{1,0:T(8,128)(2,1)S(1)}, bf16[384,128]{1,0:T(8,128)(2,1)S(1)}, u32[]{:S(2)}, u32[]{:S(2)}) collective-permute-start(bf16[384,128]{1,0:T(8,128)(2,1)S(1)} %pad_maximum_fusion.2), channel_id=1, source_target_pairs={{0,1},{1,0},{2,3},{3,2},{4,5},{5,4},{6,7},{7,6},{8,9},{9,8},{10,11... | collective-permute-start | bytes 294920 | tf_op jit(solution)/shard_map/ppermute | solution.py:259
  26.6 5.9 %collective-permute-start.7 = (bf16[512,128]{1,0:T(8,128)(2,1)S(1)}, bf16[512,128]{1,0:T(8,128)(2,1)S(1)}, u32[]{:S(2)}, u32[]{:S(2)}) collective-permute-start(bf16[512,128]{1,0:T(8,128)(2,1)S(1)} %pad_maximum_fusion.1), channel_id=1, source_target_pairs={{0,24},{8,16},{16,8},{24,0},{1,25},{9,17},{17,9},{25,1},{2,26},{10... | collective-permute-start | bytes 393224 | tf_op jit(solution)/shard_map/ppermute | solution.py:357
  31.9 1.8 %collective-permute-start.5 = (bf16[1088,128]{1,0:T(8,128)(2,1)}, bf16[1088,128]{1,0:T(8,128)(2,1)S(1)}, u32[]{:S(2)}, u32[]{:S(2)}) collective-permute-start(bf16[1088,128]{1,0:T(8,128)(2,1)} %slice_dynamic-update-slice_fusion), channel_id=1, source_target_pairs={{0,8},{8,0},{16,24},{24,16},{1,9},{9,1},{17,25},{25,17},{2,10},{10... | collective-permute-start | bytes 835592 | tf_op jit(solution)/shard_map/ppermute | solution.py:364

commit v4 on v3

--- a/solution.py
+++ b/solution.py
@@ -330,18 +330,26 @@
     panel = mine
     along = for_along
     bit = n_row // 2
-    over_ya = None
-    while bit > 1:
+    while bit > 4:
         size = panel.shape[0]
         got = across_row(packed(panel, along), bit)
-        if bit == 2:
-            over_ya = across_row(panel, 1)
-            other_a = lax.ppermute(panel, "grp", others)
         panel = packed(panel, got[:size])
         crosses = (row % bit == 0) | (row % bit == bit - 1)
         along = jnp.where(crosses, got[size:], along)
         places = places + [p ^ bit for p in places]
         bit //= 2
+    size = panel.shape[0]
+    got = across_row(panel, 4)
+    with_along = packed(panel, along)
+    near_z = across_row(with_along, 2)
+    far_z = across_row(with_along, 6)
+    places = places + [p ^ 4 for p in places]
+    places = places + [p ^ 2 for p in places]
+    first_half = packed(panel, got)
+    over_ya = across_row(first_half, 1)
+    other_a = lax.ppermute(first_half, "grp", others)
+    panel = packed(first_half, near_z[:size], far_z[:size])
+    along = jnp.where((row % 4 == 1) | (row % 4 == 2), far_z[size:], near_z[size:])
     size = panel.shape[0] // 2
     places_y = [p ^ 1 for p in places]
     half = len(places) // 2
@@ -354,7 +362,8 @@
     early_part = packed(panel, over_ya)
     early_places = places + places_y[:half]
     late_places = places_y[half:]
-    other_c = lax.ppermute(packed(panel[size:], over_ya), "grp", others)
+    other_c = lax.ppermute(over_ya, "grp", others)
+    other_e = across_row(other_a, 2)
     own_far = call(
         functools.partial(far_kernel, [(0, 0, 1, early_places)], pairs_piece, False),
         [((height, LANES), F32)],
@@ -367,14 +376,15 @@
         (0, 0, 2, late_places),
         (1, pairs_kind, 3, places[:half]),
         (1, 0, 4, early_places + late_places),
-        (1, pairs_kind, 5, places[half:] + places_y[:half]),
+        (1, pairs_kind, 5, places_y[:half]),
+        (1, pairs_kind, 6, places[half:]),
     ]
     far = call(
         functools.partial(far_kernel, plan, pairs_piece, True),
         [((height, LANES), F32)],
         own_operator,
         side_operator,
-        *held(over_yb, other_a, partner, other_c),
+        *held(over_yb, other_a, partner, other_c, other_e),
         own_far,
     )
     return pl.pallas_call(

time: 36.2 us -> 39.3 us (1.086)
  other arithmetic: 3.64 us -> 0.76 us
  local copies, waits for them, and re-layouts: 9.36 us -> 12.1 us
  waiting for transfers between devices: 5.29 us -> 7.45 us
  Pallas kernels: 6.68 us -> 7.31 us
  starting transfers between devices: 10.4 us -> 10.8 us
    ppermute x2, waiting for transfers between devices: 0.01 us -> 2.95 us  [the longest x1 2.95 us: per_device(): other_c = lax.ppermute(over_ya, 'grp', others)]
    concatenate x7 -> x2, other arithmetic: 2.91 us -> 0.01 us  [packed(): return jnp.concatenate(values, axis=0)]
    unnamed x32 -> x28, local copies, waits for them, and re-layouts: 8.72 us -> 10.3 us
    concatenate x1 -> x3, local copies, waits for them, and re-layouts: 0.63 us -> 1.89 us  [packed(): return jnp.concatenate(values, axis=0)]
    ppermute x1, waiting for transfers between devices: 1.11 us -> 0.01 us  [per_device(): partner = lax.ppermute(packed(early_part, over_yb, along), 'grp', partners)]
    pallas_call x6, Pallas kernels: 5.56 us -> 6.19 us  [call(): pl.pallas_call(kernel, out_shape=shapes[0] if single else shapes, in_spec...]
    ppermute x4 -> x6, waiting for transfers between devices: 4.17 us -> 4.49 us  [across_row(): return lax.ppermute(value, 'row', [(i, i ^ bit) for i in range(n_row)])]
    ppermute x4 -> x6, starting transfers between devices: 8.67 us -> 8.68 us  [across_row(): return lax.ppermute(value, 'row', [(i, i ^ bit) for i in range(n_row)])]
  transfers between devices with their start and end apart: 8 -> 10, of which waited for: 3 -> 3; matrix products, arithmetic and copies ran while one was open for 11% -> 22% of each run, Pallas kernels for 12% -> 11%
where the time goes in v4:
time: 39.3 us; the launch traced here: 38.7 us
  local copies, waits for them, and re-layouts  12.1 us (31%)
  starting transfers between devices  10.8 us (27%)
  waiting for transfers between devices  7.45 us (19%)
  Pallas kernels  7.31 us (19%)
  other arithmetic  0.76 us (2%)
    unnamed x28, local copies, waits for them, and re-layouts  10.3 us
    ppermute x6, starting transfers between devices, across_row(): return lax.ppermute(value, 'row', [(i, i ^ bit) for i in range(n_row)])  8.68 us
    pallas_call x6, Pallas kernels, call(): pl.pallas_call(kernel, out_shape=shapes[0] if single else shapes, in_spec...  6.19 us
    ppermute x6, waiting for transfers between devices, across_row(): return lax.ppermute(value, 'row', [(i, i ^ bit) for i in range(n_row)])  4.49 us
    ppermute x1, waiting for transfers between devices, per_device(): other_c = lax.ppermute(over_ya, 'grp', others)  2.95 us
    concatenate x3, local copies, waits for them, and re-layouts, packed(): return jnp.concatenate(values, axis=0)  1.89 us
    ppermute x1, starting transfers between devices, per_device(): other_b = lax.ppermute(packed(panel[size:], along), ('grp', 'row'), leaps)  1.2 us
    pallas_call x1, Pallas kernels, per_device(): pl.pallas_call(functools.partial(final_kernel, [(0, pairs_kind, 1, late_p...  1.12 us
  transfers between devices with their start and end apart: 10, of which 3 were waited for; matrix products, arithmetic and copies ran while one was open for 22% of the time, Pallas kernels for 11%

profile of v4, /device:TPU:0, one launch (start us, length us, event | category | flops | bytes accessed | tf_op | source)
XLA Modules:
  0.0 38.7 jit_solution(8875740247684550728)
XLA Ops:
  0.0 1.8 %shard_map.73 = (bf16[4,64,128]{2,1,0:T(8,128)(2,1)S(1)}, bf16[4,64,128]{2,1,0:T(8,128)(2,1)S(1)}, s32[1,192]{1,0:T(1,128)S(1)}, s32[1,192]{1,0:T(1,128)S(1)}, s...) custom-call(bf16[4,64,128]{2,1,0:T(8,128)(2,1)} %refs_0_.1, ...), custom_call_target="tpu_custom_call" | custom-call | tf_op jit(solution)/shard_map/pallas_call | solution.py:36
  1.8 4.1 %collective-permute-start.3 = (bf16[128,128]{1,0:T(8,128)(2,1)}, bf16[128,128]{1,0:T(8,128)(2,1)}, u32[]{:S(2)}, u32[]{:S(2)}) collective-permute-start(bf16[128,128]{1,0:T(8,128)(2,1)} %get-tuple-element.21), channel_id=1, source_target_pairs={{0,4},{1,5},{2,6},{3,7},{4,0},{5,1},{6,2},{7,3},{8,12},{9,13},{10,... | collective-permute-start | bytes 98312 | tf_op jit(solution)/shard_map/ppermute | solution.py:259
  6.0 1.4 %constant_dynamic-update-slice_fusion.13 = (bf16[768,128]{1,0:T(8,128)(2,1)}, bf16[1088,128]{1,0:T(8,128)(2,1)}, bf16[256,128]{1,0:T(8,128)(2,1)}, bf16[192,128]{1,0:T(8,128)(2,1)}) fusion(bf16[128,128]{1,0:T(8,128)(2,1)} %get-tuple-element.21), kind=kLoop, calls=%fused_computation.16 | loop fusion | bytes 163840
  7.4 0.6 %constant_dynamic-update-slice_fusion = bf16[192,128]{1,0:T(8,128)(2,1)} fusion(bf16[192,128]{1,0:T(8,128)(2,1)} %get-tuple-element.45, bf16[64,128]{1,0:T(8,128)(2,1)S(1)} %get-tuple-element.22), kind=kLoop, calls=%fused_computation.3 | loop fusion | bytes 32768 | tf_op jit(solution)/shard_map/concatenate | solution.py:327
  8.0 1.6 %collective-permute-start = (bf16[192,128]{1,0:T(8,128)(2,1)}, bf16[192,128]{1,0:T(8,128)(2,1)}, u32[]{:S(2)}, u32[]{:S(2)}) collective-permute-start(bf16[192,128]{1,0:T(8,128)(2,1)} %constant_dynamic-update-slice_fusion), channel_id=1, source_target_pairs={{0,2},{1,3},{2,0},{3,1},{4,6},{5,7},{6,4},{7,5},{8,10},{9,11},{10,... | collective-permute-start | bytes 147464 | tf_op jit(solution)/shard_map/ppermute | solution.py:259
  9.6 1.8 %shard_map.74 = (bf16[16,128,256]{2,1,0:T(8,128)(2,1)S(1)}, bf16[128,4096]{1,0:T(8,128)(2,1)S(1)}) custom-call(s32[1,192]{1,0:T(1,128)S(1)} %get-tuple-element.17.cols_ref, s32[1,192]{1,0:T(1,128)S(1)} %get-tuple-element.18.rows_ref, s32[1,192]{1,0:T(1,128)S(1)} %get-tuple-element.19.live_ref, bf16[192,4096]{1,0:T(8,128)(2,1)} %coupling_ref.1), custom_call_target="tpu_custom_call" | custom-call | tf_op jit(solution)/shard_map/pallas_call | solution.py:36
  11.4 0.6 %copy-done.7 = s32[1,192]{1,0:T(1,128)S(1)} copy-done((s32[1,192]{1,0:T(1,128)S(1)}, s32[1,192]{1,0:T(1,128)}, u32[]{:S(2)}) %copy-start.7) | copy-done | bytes 792
  12.1 0.7 %copy-done.9 = s32[1,192]{1,0:T(1,128)S(1)} copy-done((s32[1,192]{1,0:T(1,128)S(1)}, s32[1,192]{1,0:T(1,128)}, u32[]{:S(2)}) %copy-start.9) | copy-done | bytes 792
  12.7 0.7 %copy-done.11 = s32[1,192]{1,0:T(1,128)S(1)} copy-done((s32[1,192]{1,0:T(1,128)S(1)}, s32[1,192]{1,0:T(1,128)}, u32[]{:S(2)}) %copy-start.11) | copy-done | bytes 792
  13.4 1.1 %shard_map.75.refs_1_.refs_0_ = bf16[32,128,256]{2,1,0:T(8,128)(2,1)S(1)} custom-call(s32[1,192]{1,0:T(1,128)S(1)} %copy-done.7, s32[1,192]{1,0:T(1,128)S(1)} %copy-done.9, s32[1,192]{1,0:T(1,128)S(1)} %copy-done.11, bf16[128,4096]{1,0:T(8,128)(2,1)S(1)} %get-tuple-element.20.rest_ref), custom_call_target="tpu_custom_call" | custom-call | tf_op jit(solution)/shard_map/pallas_call | solution.py:36
  14.5 0.8 %copy-done.3 = bf16[4,64,128]{2,1,0:T(8,128)(2,1)S(1)} copy-done((bf16[4,64,128]{2,1,0:T(8,128)(2,1)S(1)}, bf16[4,64,128]{2,1,0:T(8,128)(2,1)}, u32[]{:S(2)}) %copy-start.3) | copy-done | bytes 65560
  15.3 0.8 %copy-done.5 = bf16[4,64,128]{2,1,0:T(8,128)(2,1)S(1)} copy-done((bf16[4,64,128]{2,1,0:T(8,128)(2,1)S(1)}, bf16[4,64,128]{2,1,0:T(8,128)(2,1)}, u32[]{:S(2)}) %copy-start.5) | copy-done | bytes 65560
  16.2 0.4 shard_map.78
  16.6 1.4 %constant_dynamic-update-slice_fusion.12 = (bf16[768,128]{1,0:T(8,128)(2,1)}, bf16[1088,128]{1,0:T(8,128)(2,1)}, bf16[256,128]{1,0:T(8,128)(2,1)}) fusion(bf16[768,128]{1,0:T(8,128)(2,1)} %get-tuple-element.42, bf16[128,128]{1,0:T(8,128)(2,1)} %collective-permute-done.3, bf16[1088,128]{1,0:T(8,128)(2,1)} %get-tuple-element.43, ...), kind=kLoop, calls=%fused_computation.15 | loop fusion | bytes 131072
  18.0 1.7 %collective-permute-start.4 = (bf16[256,128]{1,0:T(8,128)(2,1)}, bf16[256,128]{1,0:T(8,128)(2,1)S(1)}, u32[]{:S(2)}, u32[]{:S(2)}) collective-permute-start(bf16[256,128]{1,0:T(8,128)(2,1)} %get-tuple-element.41), channel_id=1, source_target_pairs={{0,1},{1,0},{2,3},{3,2},{4,5},{5,4},{6,7},{7,6},{8,9},{9,8},{10,11... | collective-permute-start | bytes 196616 | tf_op jit(solution)/shard_map/ppermute | solution.py:259
  19.7 0.7 %slice_select_fusion = bf16[64,128]{1,0:T(8,128)(2,1)S(1)} fusion(bf16[192,128]{1,0:T(8,128)(2,1)} %collective-permute-done, bf16[192,128]{1,0:T(8,128)(2,1)} %collective-permute-done.1, pred[]{:T(512)S(6)} %or.3), kind=kLoop, calls=%fused_computation.17 | loop fusion | flops 8192 | bytes 49153 | tf_op jit(solution)/shard_map/jit(_where)/select_n | solution.py:352
  20.4 1.4 %constant_dynamic-update-slice_fusion.11 = (bf16[768,128]{1,0:T(8,128)(2,1)}, bf16[1088,128]{1,0:T(8,128)(2,1)}, bf16[128,128]{1,0:T(8,128)(2,1)S(1)}) fusion(bf16[768,128]{1,0:T(8,128)(2,1)} %get-tuple-element.39, bf16[192,128]{1,0:T(8,128)(2,1)} %collective-permute-done, bf16[1088,128]{1,0:T(8,128)(2,1)} %get-tuple-element.40), kind=kLoop, calls=%fused_computation.14 | loop fusion | bytes 131072
  21.9 1.4 %constant_dynamic-update-slice_fusion.10 = (bf16[768,128]{1,0:T(8,128)(2,1)}, bf16[1088,128]{1,0:T(8,128)(2,1)}, bf16[128,128]{1,0:T(8,128)(2,1)S(1)}) fusion(bf16[768,128]{1,0:T(8,128)(2,1)} %get-tuple-element.36, bf16[192,128]{1,0:T(8,128)(2,1)} %collective-permute-done.1, bf16[1088,128]{1,0:T(8,128)(2,1)} %get-tuple-element.37), kind=kLoop, calls=%fused_computation.13 | loop fusion | bytes 131072
  23.3 0.5 %collective-permute-start.5 = (bf16[384,128]{1,0:T(8,128)(2,1)S(1)}, bf16[384,128]{1,0:T(8,128)(2,1)S(1)}, u32[]{:S(2)}, u32[]{:S(2)}) collective-permute-start(bf16[384,128]{1,0:T(8,128)(2,1)S(1)} %pad_maximum_fusion), channel_id=1, source_target_pairs={{0,1},{1,0},{2,3},{3,2},{4,5},{5,4},{6,7},{7,6},{8,9},{9,8},{10,11... | collective-permute-start | bytes 294920 | tf_op jit(solution)/shard_map/ppermute | solution.py:259
  23.7 0.7 %constant_dynamic-update-slice_fusion.9 = (bf16[768,128]{1,0:T(8,128)(2,1)}, bf16[1088,128]{1,0:T(8,128)(2,1)}) fusion(bf16[768,128]{1,0:T(8,128)(2,1)} %get-tuple-element.33, bf16[256,128]{1,0:T(8,128)(2,1)S(1)} %collective-permute-done.4, bf16[1088,128]{1,0:T(8,128)(2,1)} %get-tuple-element.34), kind=kLoop, calls=%fused_computation.12 | loop fusion | bytes 196608 | tf_op jit(solution)/shard_map/concatenate | solution.py:327
  24.4 4.0 %collective-permute-done.5 = bf16[384,128]{1,0:T(8,128)(2,1)S(1)} collective-permute-done((bf16[384,128]{1,0:T(8,128)(2,1)S(1)}, bf16[384,128]{1,0:T(8,128)(2,1)S(1)}, u32[]{:S(2)}, u32[]{:S(2)}) %collective-permute-start.5) | collective-permute-done | bytes 98336 | tf_op jit(solution)/shard_map/ppermute | solution.py:259
  28.4 0.6 %slice_dynamic-update-slice_fusion = bf16[1088,128]{1,0:T(8,128)(2,1)} fusion(bf16[1088,128]{1,0:T(8,128)(2,1)} %get-tuple-element.32, bf16[384,128]{1,0:T(8,128)(2,1)S(1)} %collective-permute-done.5), kind=kLoop, calls=%fused_computation.1 | loop fusion | bytes 163840 | tf_op jit(solution)/shard_map/concatenate | solution.py:327
  29.0 0.5 %collective-permute-start.6 = (bf16[1088,128]{1,0:T(8,128)(2,1)}, bf16[1088,128]{1,0:T(8,128)(2,1)S(1)}, u32[]{:S(2)}, u32[]{:S(2)}) collective-permute-start(bf16[1088,128]{1,0:T(8,128)(2,1)} %slice_dynamic-update-slice_fusion), channel_id=1, source_target_pairs={{0,8},{8,0},{16,24},{24,16},{1,9},{9,1},{17,25},{25,17},{2,10},{10... | collective-permute-start | bytes 835592 | tf_op jit(solution)/shard_map/ppermute | solution.py:373
  29.5 1.2 %collective-permute-start.2 = (bf16[320,128]{1,0:T(8,128)(2,1)S(1)}, bf16[320,128]{1,0:T(8,128)(2,1)S(1)}, u32[]{:S(2)}, u32[]{:S(2)}) collective-permute-start(bf16[320,128]{1,0:T(8,128)(2,1)S(1)} %pad_maximum_fusion.1), channel_id=1, source_target_pairs={{0,25},{1,24},{2,27},{3,26},{4,29},{5,28},{6,31},{7,30},{8,17},{9,... | collective-permute-start | bytes 245768 | tf_op jit(solution)/shard_map/ppermute | solution.py:360
  30.7 0.9 %copy-done.1 = bf16[768,128]{1,0:T(8,128)(2,1)S(1)} copy-done((bf16[768,128]{1,0:T(8,128)(2,1)S(1)}, bf16[768,128]{1,0:T(8,128)(2,1)}, u32[]{:S(2)}) %copy-start.1) | copy-done | bytes 196632
  31.6 0.4 %shard_map.76.refs_7_ = f32[128,128]{1,0:T(8,128)S(1)} custom-call(bf16[16,128,256]{2,1,0:T(8,128)(2,1)S(1)} %get-tuple-element.24.refs_0_, bf16[768,128]{1,0:T(8,128)(2,1)S(1)} %copy-done.1), custom_call_target="tpu_custom_call" | custom-call | tf_op jit(solution)/shard_map/pallas_call | solution.py:36
  32.0 0.4 %collective-permute-start.8 = (bf16[256,128]{1,0:T(8,128)(2,1)S(1)}, bf16[256,128]{1,0:T(8,128)(2,1)S(1)}, u32[]{:S(2)}, u32[]{:S(2)}) collective-permute-start(bf16[256,128]{1,0:T(8,128)(2,1)S(1)} %collective-permute-done.4), channel_id=1, source_target_pairs={{0,24},{8,16},{16,8},{24,0},{1,25},{9,17},{17,9},{25,1},{2,26},{10... | collective-permute-start | bytes 196616 | tf_op jit(solution)/shard_map/ppermute | solution.py:365
  32.5 0.8 %collective-permute-start.9 = (bf16[256,128]{1,0:T(8,128)(2,1)S(1)}, bf16[256,128]{1,0:T(8,128)(2,1)S(1)}, u32[]{:S(2)}, u32[]{:S(2)}) collective-permute-start(bf16[256,128]{1,0:T(8,128)(2,1)S(1)} %collective-permute-done.7.refs_3_), channel_id=1, source_target_pairs={{0,2},{1,3},{2,0},{3,1},{4,6},{5,7},{6,4},{7,5},{8,10},{9,11},{10,... | collective-permute-start | bytes 196616 | tf_op jit(solution)/shard_map/ppermute | solution.py:259
  33.3 3.0 %collective-permute-done.8.refs_5_ = bf16[256,128]{1,0:T(8,128)(2,1)S(1)} collective-permute-done((bf16[256,128]{1,0:T(8,128)(2,1)S(1)}, bf16[256,128]{1,0:T(8,128)(2,1)S(1)}, u32[]{:S(2)}, u32[]{:S(2)}) %collective-permute-start.8) | collective-permute-done | bytes 65568 | tf_op jit(solution)/shard_map/ppermute | solution.py:365
  36.2 0.5 %collective-permute-done.9.refs_6_ = bf16[256,128]{1,0:T(8,128)(2,1)S(1)} collective-permute-done((bf16[256,128]{1,0:T(8,128)(2,1)S(1)}, bf16[256,128]{1,0:T(8,128)(2,1)S(1)}, u32[]{:S(2)}, u32[]{:S(2)}) %collective-permute-start.9) | collective-permute-done | bytes 65568 | tf_op jit(solution)/shard_map/ppermute | solution.py:259
  36.7 0.8 %shard_map.77.refs_6_ = f32[128,128]{1,0:T(8,128)S(1)} custom-call(bf16[16,128,256]{2,1,0:T(8,128)(2,1)S(1)} %get-tuple-element.24.refs_0_, bf16[32,128,256]{2,1,0:T(8,128)(2,1)S(1)} %shard_map.75.refs_1_.refs_0_, bf16[256,128]{1,0:T(8,128)(2,1)S(1)} %slice.42.refs_2_, bf16[256,128]{1,0:T(8,128)(2,1)S(1)} %collective-permute-done.7.refs_3_, ...), custom_call_target="tpu_custom_call" | custom-call | tf_op jit(solution)/shard_map/pallas_call | solution.py:36
  37.5 1.1 %final.1 = bf16[4,64,128]{2,1,0:T(8,128)(2,1)} custom-call(bf16[32,128,256]{2,1,0:T(8,128)(2,1)S(1)} %shard_map.75.refs_1_.refs_0_, bf16[320,128]{1,0:T(8,128)(2,1)S(1)} %collective-permute-done.2.refs_1_, bf16[1088,128]{1,0:T(8,128)(2,1)S(1)} %collective-permute-done.6.refs_4_.refs_2_, bf16[64,128]{1,0:T(8,128)(2,1)S(1)} %get-tuple-element.30.refs_3_, ...), custom_call_target="tpu_custom_call" | custom-call | tf_op jit(solution)/shard_map/final/pallas_call | solution.py:390
  (31 shorter events, 0.1 us)
Async XLA Ops:
  1.8 7.8 %copy-start.2 = (bf16[4,64,128]{2,1,0:T(8,128)(2,1)}, bf16[4,64,128]{2,1,0:T(8,128)(2,1)S(1)}, u32[]{:S(2)}) copy-start(bf16[4,64,128]{2,1,0:T(8,128)(2,1)S(1)} %get-tuple-element.25.signal_ref) | copy-start | bytes 196612
  1.8 7.8 %copy-start.4 = (bf16[4,64,128]{2,1,0:T(8,128)(2,1)}, bf16[4,64,128]{2,1,0:T(8,128)(2,1)S(1)}, u32[]{:S(2)}) copy-start(bf16[4,64,128]{2,1,0:T(8,128)(2,1)S(1)} %get-tuple-element.26.basis_ref) | copy-start | bytes 196612
  1.8 9.6 %copy-start.6 = (s32[1,192]{1,0:T(1,128)}, s32[1,192]{1,0:T(1,128)S(1)}, u32[]{:S(2)}) copy-start(s32[1,192]{1,0:T(1,128)S(1)} %get-tuple-element.17.cols_ref) | copy-start | bytes 2308
  1.8 9.6 %copy-start.8 = (s32[1,192]{1,0:T(1,128)}, s32[1,192]{1,0:T(1,128)S(1)}, u32[]{:S(2)}) copy-start(s32[1,192]{1,0:T(1,128)S(1)} %get-tuple-element.18.rows_ref) | copy-start | bytes 2308
  1.8 9.6 %copy-start.10 = (s32[1,192]{1,0:T(1,128)}, s32[1,192]{1,0:T(1,128)S(1)}, u32[]{:S(2)}) copy-start(s32[1,192]{1,0:T(1,128)S(1)} %get-tuple-element.19.live_ref) | copy-start | bytes 2308
  1.8 14.7 %collective-permute-start.3 = (bf16[128,128]{1,0:T(8,128)(2,1)}, bf16[128,128]{1,0:T(8,128)(2,1)}, u32[]{:S(2)}, u32[]{:S(2)}) collective-permute-start(bf16[128,128]{1,0:T(8,128)(2,1)} %get-tuple-element.21), channel_id=1, source_target_pairs={{0,4},{1,5},{2,6},{3,7},{4,0},{5,1},{6,2},{7,3},{8,12},{9,13},{10,... | collective-permute-start | bytes 98312 | tf_op jit(solution)/shard_map/ppermute | solution.py:259
  8.0 11.7 %collective-permute-start = (bf16[192,128]{1,0:T(8,128)(2,1)}, bf16[192,128]{1,0:T(8,128)(2,1)}, u32[]{:S(2)}, u32[]{:S(2)}) collective-permute-start(bf16[192,128]{1,0:T(8,128)(2,1)} %constant_dynamic-update-slice_fusion), channel_id=1, source_target_pairs={{0,2},{1,3},{2,0},{3,1},{4,6},{5,7},{6,4},{7,5},{8,10},{9,11},{10,... | collective-permute-start | bytes 147464 | tf_op jit(solution)/shard_map/ppermute | solution.py:259
  9.6 10.1 %collective-permute-start.1 = (bf16[192,128]{1,0:T(8,128)(2,1)}, bf16[192,128]{1,0:T(8,128)(2,1)}, u32[]{:S(2)}, u32[]{:S(2)}) collective-permute-start(bf16[192,128]{1,0:T(8,128)(2,1)} %constant_dynamic-update-slice_fusion), channel_id=1, source_target_pairs={{0,6},{1,7},{2,4},{3,5},{4,2},{5,3},{6,0},{7,1},{8,14},{9,15},{10,... | collective-permute-start | bytes 147464 | tf_op jit(solution)/shard_map/ppermute | solution.py:259
  9.6 4.9 %copy-start = (bf16[4,3,128,128]{3,2,1,0:T(8,128)(2,1)S(1)}, bf16[4,3,128,128]{3,2,1,0:T(8,128)(2,1)}, u32[]{:S(2)}) copy-start(bf16[4,3,128,128]{3,2,1,0:T(8,128)(2,1)} %refs_5_.1) | copy-start | bytes 1179652
  11.4 0.6 %copy-start.7 = (s32[1,192]{1,0:T(1,128)S(1)}, s32[1,192]{1,0:T(1,128)}, u32[]{:S(2)}) copy-start(s32[1,192]{1,0:T(1,128)} %copy-done.6) | copy-start | bytes 2308
  12.1 0.7 %copy-start.9 = (s32[1,192]{1,0:T(1,128)S(1)}, s32[1,192]{1,0:T(1,128)}, u32[]{:S(2)}) copy-start(s32[1,192]{1,0:T(1,128)} %copy-done.8) | copy-start | bytes 2308
  12.7 0.7 %copy-start.11 = (s32[1,192]{1,0:T(1,128)S(1)}, s32[1,192]{1,0:T(1,128)}, u32[]{:S(2)}) copy-start(s32[1,192]{1,0:T(1,128)} %copy-done.10) | copy-start | bytes 2308
  14.5 0.8 %copy-start.3 = (bf16[4,64,128]{2,1,0:T(8,128)(2,1)S(1)}, bf16[4,64,128]{2,1,0:T(8,128)(2,1)}, u32[]{:S(2)}) copy-start(bf16[4,64,128]{2,1,0:T(8,128)(2,1)} %copy-done.2) | copy-start | bytes 196612
  15.3 0.8 %copy-start.5 = (bf16[4,64,128]{2,1,0:T(8,128)(2,1)S(1)}, bf16[4,64,128]{2,1,0:T(8,128)(2,1)}, u32[]{:S(2)}) copy-start(bf16[4,64,128]{2,1,0:T(8,128)(2,1)} %copy-done.4) | copy-start | bytes 196612
  18.0 5.8 %collective-permute-start.4 = (bf16[256,128]{1,0:T(8,128)(2,1)}, bf16[256,128]{1,0:T(8,128)(2,1)S(1)}, u32[]{:S(2)}, u32[]{:S(2)}) collective-permute-start(bf16[256,128]{1,0:T(8,128)(2,1)} %get-tuple-element.41), channel_id=1, source_target_pairs={{0,1},{1,0},{2,3},{3,2},{4,5},{5,4},{6,7},{7,6},{8,9},{9,8},{10,11... | collective-permute-start | bytes 196616 | tf_op jit(solution)/shard_map/ppermute | solution.py:259
  19.7 12.8 %collective-permute-start.7 = (bf16[256,128]{1,0:T(8,128)(2,1)}, bf16[256,128]{1,0:T(8,128)(2,1)S(1)}, u32[]{:S(2)}, u32[]{:S(2)}) collective-permute-start(bf16[256,128]{1,0:T(8,128)(2,1)} %get-tuple-element.41), channel_id=1, source_target_pairs={{0,24},{8,16},{16,8},{24,0},{1,25},{9,17},{17,9},{25,1},{2,26},{10... | collective-permute-start | bytes 196616 | tf_op jit(solution)/shard_map/ppermute | solution.py:350
  23.3 5.1 %collective-permute-start.5 = (bf16[384,128]{1,0:T(8,128)(2,1)S(1)}, bf16[384,128]{1,0:T(8,128)(2,1)S(1)}, u32[]{:S(2)}, u32[]{:S(2)}) collective-permute-start(bf16[384,128]{1,0:T(8,128)(2,1)S(1)} %pad_maximum_fusion), channel_id=1, source_target_pairs={{0,1},{1,0},{2,3},{3,2},{4,5},{5,4},{6,7},{7,6},{8,9},{9,8},{10,11... | collective-permute-start | bytes 294920 | tf_op jit(solution)/shard_map/ppermute | solution.py:259
  29.0 7.7 %collective-permute-start.6 = (bf16[1088,128]{1,0:T(8,128)(2,1)}, bf16[1088,128]{1,0:T(8,128)(2,1)S(1)}, u32[]{:S(2)}, u32[]{:S(2)}) collective-permute-start(bf16[1088,128]{1,0:T(8,128)(2,1)} %slice_dynamic-update-slice_fusion), channel_id=1, source_target_pairs={{0,8},{8,0},{16,24},{24,16},{1,9},{9,1},{17,25},{25,17},{2,10},{10... | collective-permute-start | bytes 835592 | tf_op jit(solution)/shard_map/ppermute | solution.py:373
  29.5 8.1 %collective-permute-start.2 = (bf16[320,128]{1,0:T(8,128)(2,1)S(1)}, bf16[320,128]{1,0:T(8,128)(2,1)S(1)}, u32[]{:S(2)}, u32[]{:S(2)}) collective-permute-start(bf16[320,128]{1,0:T(8,128)(2,1)S(1)} %pad_maximum_fusion.1), channel_id=1, source_target_pairs={{0,25},{1,24},{2,27},{3,26},{4,29},{5,28},{6,31},{7,30},{8,17},{9,... | collective-permute-start | bytes 245768 | tf_op jit(solution)/shard_map/ppermute | solution.py:360
  30.7 0.9 %copy-start.1 = (bf16[768,128]{1,0:T(8,128)(2,1)S(1)}, bf16[768,128]{1,0:T(8,128)(2,1)}, u32[]{:S(2)}) copy-start(bf16[768,128]{1,0:T(8,128)(2,1)} %get-tuple-element.31.refs_1_) | copy-start | bytes 589828
  32.0 4.2 %collective-permute-start.8 = (bf16[256,128]{1,0:T(8,128)(2,1)S(1)}, bf16[256,128]{1,0:T(8,128)(2,1)S(1)}, u32[]{:S(2)}, u32[]{:S(2)}) collective-permute-start(bf16[256,128]{1,0:T(8,128)(2,1)S(1)} %collective-permute-done.4), channel_id=1, source_target_pairs={{0,24},{8,16},{16,8},{24,0},{1,25},{9,17},{17,9},{25,1},{2,26},{10... | collective-permute-start | bytes 196616 | tf_op jit(solution)/shard_map/ppermute | solution.py:365
  32.5 4.3 %collective-permute-start.9 = (bf16[256,128]{1,0:T(8,128)(2,1)S(1)}, bf16[256,128]{1,0:T(8,128)(2,1)S(1)}, u32[]{:S(2)}, u32[]{:S(2)}) collective-permute-start(bf16[256,128]{1,0:T(8,128)(2,1)S(1)} %collective-permute-done.7.refs_3_), channel_id=1, source_target_pairs={{0,2},{1,3},{2,0},{3,1},{4,6},{5,7},{6,4},{7,5},{8,10},{9,11},{10,... | collective-permute-start | bytes 196616 | tf_op jit(solution)/shard_map/ppermute | solution.py:259

commit v5 on v4

--- a/solution.py
+++ b/solution.py
@@ -346,19 +346,20 @@
     places = places + [p ^ 4 for p in places]
     places = places + [p ^ 2 for p in places]
     first_half = packed(panel, got)
-    over_ya = across_row(first_half, 1)
+    got = across_row(packed(first_half, for_across), 1)
+    over_ya, across = got[: 2 * size], got[2 * size :]
     other_a = lax.ppermute(first_half, "grp", others)
     panel = packed(first_half, near_z[:size], far_z[:size])
     along = jnp.where((row % 4 == 1) | (row % 4 == 2), far_z[size:], near_z[size:])
     size = panel.shape[0] // 2
     places_y = [p ^ 1 for p in places]
     half = len(places) // 2
-    got = across_row(packed(panel[size:], along, for_across), 1)
+    got = across_row(packed(panel[size:], along), 1)
     leaps = [
         (g * n_row + r, h * n_row + (r ^ 1)) for g, h in others for r in range(n_row)
     ]
     other_b = lax.ppermute(packed(panel[size:], along), ("grp", "row"), leaps)
-    over_yb, along, across = got[:size], got[size : size + R], got[size + R :]
+    over_yb, along = got[:size], got[size:]
     early_part = packed(panel, over_ya)
     early_places = places + places_y[:half]
     late_places = places_y[half:]

time: 39.3 us -> 28.8 us (0.73); the launches traced: 38.7 us -> 28.6 us
  local copies, waits for them, and re-layouts: 12.1 us -> 0.13 us
  starting transfers between devices: 10.8 us -> 13.5 us
  other arithmetic: 0.76 us -> 0.03 us
  waiting for transfers between devices: 7.45 us -> 8.1 us
  Pallas kernels: 7.31 us -> 6.71 us
    unnamed x28 -> x6, local copies, waits for them, and re-layouts: 10.3 us -> 0.06 us
    ppermute x1, waiting for transfers between devices: 2.95 us -> 0.01 us  [per_device(): other_c = lax.ppermute(over_ya, 'grp', others)]
    ppermute x6, waiting for transfers between devices: 4.49 us -> 7 us  [across_row(): return lax.ppermute(value, 'row', [(i, i ^ bit) for i in range(n_row)])]
    concatenate x3, local copies, waits for them, and re-layouts: 1.89 us -> 0.05 us  [packed(): return jnp.concatenate(values, axis=0)]
    ppermute x1, starting transfers between devices: 0.01 us -> 1.59 us  [per_device(): other_a = lax.ppermute(first_half, 'grp', others)]
    ppermute x1, starting transfers between devices: 0.44 us -> 1.52 us  [per_device(): other_c = lax.ppermute(over_ya, 'grp', others)]
    ppermute x1, waiting for transfers between devices: 0.01 us -> 1.09 us  [per_device(): other_a = lax.ppermute(first_half, 'grp', others)]
    select_n x1, other arithmetic: 0.75 us -> 0.01 us  [per_device(): jnp.where((row % 4 == 1) | (row % 4 == 2), far_z[size:], near_z[size:])]
  transfers between devices with their start and end apart: 10 -> 10, of which waited for: 3 -> 5; matrix products, arithmetic and copies ran while one was open for 22% -> 0% of each run, Pallas kernels for 11% -> 16%
where the time goes in v5:
time: 28.8 us; the launch traced here: 28.6 us
  starting transfers between devices  13.5 us (47%)
  waiting for transfers between devices  8.1 us (28%)
  Pallas kernels  6.71 us (23%)
    ppermute x6, starting transfers between devices, across_row(): return lax.ppermute(value, 'row', [(i, i ^ bit) for i in range(n_row)])  9.11 us
    ppermute x6, waiting for transfers between devices, across_row(): return lax.ppermute(value, 'row', [(i, i ^ bit) for i in range(n_row)])  7 us
    pallas_call x6, Pallas kernels, call(): pl.pallas_call(kernel, out_shape=shapes[0] if single else shapes, in_spec...  5.59 us
    ppermute x1, starting transfers between devices, per_device(): other_a = lax.ppermute(first_half, 'grp', others)  1.59 us
    ppermute x1, starting transfers between devices, per_device(): other_c = lax.ppermute(over_ya, 'grp', others)  1.52 us
    ppermute x1, starting transfers between devices, per_device(): other_b = lax.ppermute(packed(panel[size:], along), ('grp', 'row'), leaps)  1.18 us
    pallas_call x1, Pallas kernels, per_device(): pl.pallas_call(functools.partial(final_kernel, [(0, pairs_kind, 1, late_p...  1.12 us
    ppermute x1, waiting for transfers between devices, per_device(): other_a = lax.ppermute(first_half, 'grp', others)  1.09 us
  transfers between devices with their start and end apart: 10, of which 5 were waited for; matrix products, arithmetic and copies ran while one was open for 0% of the time, Pallas kernels for 16%

profile of v5, /device:TPU:0, one launch (start us, length us, event | category | flops | bytes accessed | tf_op | source)
XLA Modules:
  0.0 28.6 jit_solution(8991663722278990559)
XLA Ops:
  0.0 1.2 %shard_map.73 = (bf16[4,64,128]{2,1,0:T(8,128)(2,1)S(1)}, bf16[4,64,128]{2,1,0:T(8,128)(2,1)S(1)}, s32[1,192]{1,0:T(1,128)S(1)}, s32[1,192]{1,0:T(1,128)S(1)}, s...) custom-call(bf16[4,64,128]{2,1,0:T(8,128)(2,1)} %refs_0_.1, ...), custom_call_target="tpu_custom_call" | custom-call | tf_op jit(solution)/shard_map/pallas_call | solution.py:36
  1.2 4.1 %collective-permute-start.3 = (bf16[128,128]{1,0:T(8,128)(2,1)S(1)}, bf16[128,128]{1,0:T(8,128)(2,1)S(1)}, u32[]{:S(2)}, u32[]{:S(2)}) collective-permute-start(bf16[128,128]{1,0:T(8,128)(2,1)S(1)} %get-tuple-element.21), channel_id=1, source_target_pairs={{0,4},{1,5},{2,6},{3,7},{4,0},{5,1},{6,2},{7,3},{8,12},{9,13},{10,... | collective-permute-start | bytes 98312 | tf_op jit(solution)/shard_map/ppermute | solution.py:259
  5.3 1.6 %collective-permute-start = (bf16[192,128]{1,0:T(8,128)(2,1)S(1)}, bf16[192,128]{1,0:T(8,128)(2,1)S(1)}, u32[]{:S(2)}, u32[]{:S(2)}) collective-permute-start(bf16[192,128]{1,0:T(8,128)(2,1)S(1)} %constant_dynamic-update-slice_fusion), channel_id=1, source_target_pairs={{0,2},{1,3},{2,0},{3,1},{4,6},{5,7},{6,4},{7,5},{8,10},{9,11},{10,... | collective-permute-start | bytes 147464 | tf_op jit(solution)/shard_map/ppermute | solution.py:259
  7.0 0.0 collective-permute-start.1
  7.0 0.6 %collective-permute-done.3 = bf16[128,128]{1,0:T(8,128)(2,1)S(1)} collective-permute-done((bf16[128,128]{1,0:T(8,128)(2,1)S(1)}, bf16[128,128]{1,0:T(8,128)(2,1)S(1)}, u32[]{:S(2)}, u32[]{:S(2)}) %collective-permute-start.3) | collective-permute-done | bytes 32800 | tf_op jit(solution)/shard_map/ppermute | solution.py:259
  7.5 1.7 %collective-permute-start.4 = (bf16[320,128]{1,0:T(8,128)(2,1)S(1)}, bf16[320,128]{1,0:T(8,128)(2,1)S(1)}, u32[]{:S(2)}, u32[]{:S(2)}) collective-permute-start(bf16[320,128]{1,0:T(8,128)(2,1)S(1)} %pad_maximum_fusion.1), channel_id=1, source_target_pairs={{0,1},{1,0},{2,3},{3,2},{4,5},{5,4},{6,7},{7,6},{8,9},{9,8},{10,11... | collective-permute-start | bytes 245768 | tf_op jit(solution)/shard_map/ppermute | solution.py:259
  9.3 0.2 collective-permute-done
  9.5 3.4 %collective-permute-done.1 = bf16[192,128]{1,0:T(8,128)(2,1)S(1)} collective-permute-done((bf16[192,128]{1,0:T(8,128)(2,1)S(1)}, bf16[192,128]{1,0:T(8,128)(2,1)S(1)}, u32[]{:S(2)}, u32[]{:S(2)}) %collective-permute-start.1) | collective-permute-done | bytes 49184 | tf_op jit(solution)/shard_map/ppermute | solution.py:259
  12.9 1.6 %collective-permute-start.5 = (bf16[320,128]{1,0:T(8,128)(2,1)S(1)}, bf16[320,128]{1,0:T(8,128)(2,1)S(1)}, u32[]{:S(2)}, u32[]{:S(2)}) collective-permute-start(bf16[320,128]{1,0:T(8,128)(2,1)S(1)} %pad_maximum_fusion), channel_id=1, source_target_pairs={{0,1},{1,0},{2,3},{3,2},{4,5},{5,4},{6,7},{7,6},{8,9},{9,8},{10,11... | collective-permute-start | bytes 245768 | tf_op jit(solution)/shard_map/ppermute | solution.py:259
  14.5 0.0 collective-permute-done.4
  14.5 2.9 %collective-permute-done.5 = bf16[320,128]{1,0:T(8,128)(2,1)S(1)} collective-permute-done((bf16[320,128]{1,0:T(8,128)(2,1)S(1)}, bf16[320,128]{1,0:T(8,128)(2,1)S(1)}, u32[]{:S(2)}, u32[]{:S(2)}) %collective-permute-start.5) | collective-permute-done | bytes 81952 | tf_op jit(solution)/shard_map/ppermute | solution.py:259
  17.4 0.1 collective-permute-start.6
  17.5 1.6 %collective-permute-start.7 = (bf16[256,128]{1,0:T(8,128)(2,1)S(1)}, bf16[256,128]{1,0:T(8,128)(2,1)S(1)}, u32[]{:S(2)}, u32[]{:S(2)}) collective-permute-start(bf16[256,128]{1,0:T(8,128)(2,1)S(1)} %pad_maximum_fusion.2), channel_id=1, source_target_pairs={{0,24},{8,16},{16,8},{24,0},{1,25},{9,17},{17,9},{25,1},{2,26},{10... | collective-permute-start | bytes 196616 | tf_op jit(solution)/shard_map/ppermute | solution.py:351
  19.1 1.2 %collective-permute-start.2 = (bf16[320,128]{1,0:T(8,128)(2,1)S(1)}, bf16[320,128]{1,0:T(8,128)(2,1)S(1)}, u32[]{:S(2)}, u32[]{:S(2)}) collective-permute-start(bf16[320,128]{1,0:T(8,128)(2,1)S(1)} %pad_maximum_fusion), channel_id=1, source_target_pairs={{0,25},{1,24},{2,27},{3,26},{4,29},{5,28},{6,31},{7,30},{8,17},{9,... | collective-permute-start | bytes 245768 | tf_op jit(solution)/shard_map/ppermute | solution.py:361
  20.3 1.1 %collective-permute-done.7.refs_3_ = bf16[256,128]{1,0:T(8,128)(2,1)S(1)} collective-permute-done((bf16[256,128]{1,0:T(8,128)(2,1)S(1)}, bf16[256,128]{1,0:T(8,128)(2,1)S(1)}, u32[]{:S(2)}, u32[]{:S(2)}) %collective-permute-start.7) | collective-permute-done | bytes 65568 | tf_op jit(solution)/shard_map/ppermute | solution.py:351
  21.4 0.0 collective-permute-start.9
  21.4 1.5 %collective-permute-start.8 = (bf16[256,128]{1,0:T(8,128)(2,1)S(1)}, bf16[256,128]{1,0:T(8,128)(2,1)S(1)}, u32[]{:S(2)}, u32[]{:S(2)}) collective-permute-start(bf16[256,128]{1,0:T(8,128)(2,1)S(1)} %get-tuple-element.31), channel_id=1, source_target_pairs={{0,24},{8,16},{16,8},{24,0},{1,25},{9,17},{17,9},{25,1},{2,26},{10... | collective-permute-start | bytes 196616 | tf_op jit(solution)/shard_map/ppermute | solution.py:366
  22.9 0.0 copy-start
  22.9 1.8 %shard_map.74 = (bf16[16,128,256]{2,1,0:T(8,128)(2,1)S(1)}, bf16[128,4096]{1,0:T(8,128)(2,1)S(1)}) custom-call(s32[1,192]{1,0:T(1,128)S(1)} %get-tuple-element.17.cols_ref, s32[1,192]{1,0:T(1,128)S(1)} %get-tuple-element.18.rows_ref, s32[1,192]{1,0:T(1,128)S(1)} %get-tuple-element.19.live_ref, bf16[192,4096]{1,0:T(8,128)(2,1)} %coupling_ref.1), custom_call_target="tpu_custom_call" | custom-call | tf_op jit(solution)/shard_map/pallas_call | solution.py:36
  24.7 1.1 %shard_map.75.refs_1_.refs_0_ = bf16[32,128,256]{2,1,0:T(8,128)(2,1)S(1)} custom-call(s32[1,192]{1,0:T(1,128)S(1)} %get-tuple-element.17.cols_ref, s32[1,192]{1,0:T(1,128)S(1)} %get-tuple-element.18.rows_ref, s32[1,192]{1,0:T(1,128)S(1)} %get-tuple-element.19.live_ref, bf16[128,4096]{1,0:T(8,128)(2,1)S(1)} %get-tuple-element.20.rest_ref), custom_call_target="tpu_custom_call" | custom-call | tf_op jit(solution)/shard_map/pallas_call | solution.py:36
  25.8 0.0 copy-done
  25.8 0.4 %shard_map.78 = (f32[64,512]{1,0:T(8,128)S(1)}, bf16[256,512]{1,0:T(8,128)(2,1)S(1)}) custom-call(bf16[4,64,128]{2,1,0:T(8,128)(2,1)S(1)} %get-tuple-element.25.signal_ref, bf16[4,3,128,128]{3,2,1,0:T(8,128)(2,1)S(1)} %copy-done, bf16[4,64,128]{2,1,0:T(8,128)(2,1)S(1)} %get-tuple-element.26.basis_ref), custom_call_target="tpu_custom_call" | custom-call | tf_op jit(solution)/shard_map/pallas_call | solution.py:36
  26.2 0.4 %shard_map.76.refs_7_ = f32[128,128]{1,0:T(8,128)S(1)} custom-call(bf16[16,128,256]{2,1,0:T(8,128)(2,1)S(1)} %get-tuple-element.24.refs_0_, bf16[768,128]{1,0:T(8,128)(2,1)S(1)} %get-tuple-element.29.refs_1_), custom_call_target="tpu_custom_call" | custom-call | tf_op jit(solution)/shard_map/pallas_call | solution.py:36
  26.6 0.0 collective-permute-done.9.refs_6_
  26.7 0.0 collective-permute-done.8.refs_5_
  26.7 0.0 collective-permute-done.6.refs_4_.refs_2_
  26.7 0.8 %shard_map.77.refs_6_ = f32[128,128]{1,0:T(8,128)S(1)} custom-call(bf16[16,128,256]{2,1,0:T(8,128)(2,1)S(1)} %get-tuple-element.24.refs_0_, bf16[32,128,256]{2,1,0:T(8,128)(2,1)S(1)} %shard_map.75.refs_1_.refs_0_, bf16[256,128]{1,0:T(8,128)(2,1)S(1)} %slice.43.refs_2_, bf16[256,128]{1,0:T(8,128)(2,1)S(1)} %collective-permute-done.7.refs_3_, ...), custom_call_target="tpu_custom_call" | custom-call | tf_op jit(solution)/shard_map/pallas_call | solution.py:36
  27.5 0.0 collective-permute-done.2.refs_1_
  27.5 1.1 %final.1 = bf16[4,64,128]{2,1,0:T(8,128)(2,1)} custom-call(bf16[32,128,256]{2,1,0:T(8,128)(2,1)S(1)} %shard_map.75.refs_1_.refs_0_, bf16[320,128]{1,0:T(8,128)(2,1)S(1)} %collective-permute-done.2.refs_1_, bf16[1088,128]{1,0:T(8,128)(2,1)S(1)} %collective-permute-done.6.refs_4_.refs_2_, bf16[64,128]{1,0:T(8,128)(2,1)S(1)} %slice.41.refs_3_, ...), custom_call_target="tpu_custom_call" | custom-call | tf_op jit(solution)/shard_map/final/pallas_call | solution.py:391
  (14 shorter events, 0.2 us)
Async XLA Ops:
  1.2 6.4 %collective-permute-start.3 = (bf16[128,128]{1,0:T(8,128)(2,1)S(1)}, bf16[128,128]{1,0:T(8,128)(2,1)S(1)}, u32[]{:S(2)}, u32[]{:S(2)}) collective-permute-start(bf16[128,128]{1,0:T(8,128)(2,1)S(1)} %get-tuple-element.21), channel_id=1, source_target_pairs={{0,4},{1,5},{2,6},{3,7},{4,0},{5,1},{6,2},{7,3},{8,12},{9,13},{10,... | collective-permute-start | bytes 98312 | tf_op jit(solution)/shard_map/ppermute | solution.py:259
  5.3 4.2 %collective-permute-start = (bf16[192,128]{1,0:T(8,128)(2,1)S(1)}, bf16[192,128]{1,0:T(8,128)(2,1)S(1)}, u32[]{:S(2)}, u32[]{:S(2)}) collective-permute-start(bf16[192,128]{1,0:T(8,128)(2,1)S(1)} %constant_dynamic-update-slice_fusion), channel_id=1, source_target_pairs={{0,2},{1,3},{2,0},{3,1},{4,6},{5,7},{6,4},{7,5},{8,10},{9,11},{10,... | collective-permute-start | bytes 147464 | tf_op jit(solution)/shard_map/ppermute | solution.py:259
  7.0 5.9 %collective-permute-start.1 = (bf16[192,128]{1,0:T(8,128)(2,1)S(1)}, bf16[192,128]{1,0:T(8,128)(2,1)S(1)}, u32[]{:S(2)}, u32[]{:S(2)}) collective-permute-start(bf16[192,128]{1,0:T(8,128)(2,1)S(1)} %constant_dynamic-update-slice_fusion), channel_id=1, source_target_pairs={{0,6},{1,7},{2,4},{3,5},{4,2},{5,3},{6,0},{7,1},{8,14},{9,15},{10,... | collective-permute-start | bytes 147464 | tf_op jit(solution)/shard_map/ppermute | solution.py:259
  7.5 7.0 %collective-permute-start.4 = (bf16[320,128]{1,0:T(8,128)(2,1)S(1)}, bf16[320,128]{1,0:T(8,128)(2,1)S(1)}, u32[]{:S(2)}, u32[]{:S(2)}) collective-permute-start(bf16[320,128]{1,0:T(8,128)(2,1)S(1)} %pad_maximum_fusion.1), channel_id=1, source_target_pairs={{0,1},{1,0},{2,3},{3,2},{4,5},{5,4},{6,7},{7,6},{8,9},{9,8},{10,11... | collective-permute-start | bytes 245768 | tf_op jit(solution)/shard_map/ppermute | solution.py:259
  12.9 4.5 %collective-permute-start.5 = (bf16[320,128]{1,0:T(8,128)(2,1)S(1)}, bf16[320,128]{1,0:T(8,128)(2,1)S(1)}, u32[]{:S(2)}, u32[]{:S(2)}) collective-permute-start(bf16[320,128]{1,0:T(8,128)(2,1)S(1)} %pad_maximum_fusion), channel_id=1, source_target_pairs={{0,1},{1,0},{2,3},{3,2},{4,5},{5,4},{6,7},{7,6},{8,9},{9,8},{10,11... | collective-permute-start | bytes 245768 | tf_op jit(solution)/shard_map/ppermute | solution.py:259
  17.4 9.2 %collective-permute-start.6 = (bf16[1088,128]{1,0:T(8,128)(2,1)S(1)}, bf16[1088,128]{1,0:T(8,128)(2,1)S(1)}, u32[]{:S(2)}, u32[]{:S(2)}) collective-permute-start(bf16[1088,128]{1,0:T(8,128)(2,1)S(1)} %constant_dynamic-update-slice_fusion.2), channel_id=1, source_target_pairs={{0,8},{8,0},{16,24},{24,16},{1,9},{9,1},{17,25},{25,17},{2,10},{10... | collective-permute-start | bytes 835592 | tf_op jit(solution)/shard_map/ppermute | solution.py:374
  17.5 3.9 %collective-permute-start.7 = (bf16[256,128]{1,0:T(8,128)(2,1)S(1)}, bf16[256,128]{1,0:T(8,128)(2,1)S(1)}, u32[]{:S(2)}, u32[]{:S(2)}) collective-permute-start(bf16[256,128]{1,0:T(8,128)(2,1)S(1)} %pad_maximum_fusion.2), channel_id=1, source_target_pairs={{0,24},{8,16},{16,8},{24,0},{1,25},{9,17},{17,9},{25,1},{2,26},{10... | collective-permute-start | bytes 196616 | tf_op jit(solution)/shard_map/ppermute | solution.py:351
  19.1 8.4 %collective-permute-start.2 = (bf16[320,128]{1,0:T(8,128)(2,1)S(1)}, bf16[320,128]{1,0:T(8,128)(2,1)S(1)}, u32[]{:S(2)}, u32[]{:S(2)}) collective-permute-start(bf16[320,128]{1,0:T(8,128)(2,1)S(1)} %pad_maximum_fusion), channel_id=1, source_target_pairs={{0,25},{1,24},{2,27},{3,26},{4,29},{5,28},{6,31},{7,30},{8,17},{9,... | collective-permute-start | bytes 245768 | tf_op jit(solution)/shard_map/ppermute | solution.py:361
  21.4 5.3 %collective-permute-start.9 = (bf16[256,128]{1,0:T(8,128)(2,1)S(1)}, bf16[256,128]{1,0:T(8,128)(2,1)S(1)}, u32[]{:S(2)}, u32[]{:S(2)}) collective-permute-start(bf16[256,128]{1,0:T(8,128)(2,1)S(1)} %collective-permute-done.7.refs_3_), channel_id=1, source_target_pairs={{0,2},{1,3},{2,0},{3,1},{4,6},{5,7},{6,4},{7,5},{8,10},{9,11},{10,... | collective-permute-start | bytes 196616 | tf_op jit(solution)/shard_map/ppermute | solution.py:259
  21.4 5.3 %collective-permute-start.8 = (bf16[256,128]{1,0:T(8,128)(2,1)S(1)}, bf16[256,128]{1,0:T(8,128)(2,1)S(1)}, u32[]{:S(2)}, u32[]{:S(2)}) collective-permute-start(bf16[256,128]{1,0:T(8,128)(2,1)S(1)} %get-tuple-element.31), channel_id=1, source_target_pairs={{0,24},{8,16},{16,8},{24,0},{1,25},{9,17},{17,9},{25,1},{2,26},{10... | collective-permute-start | bytes 196616 | tf_op jit(solution)/shard_map/ppermute | solution.py:366
  22.9 2.9 %copy-start = (bf16[4,3,128,128]{3,2,1,0:T(8,128)(2,1)S(1)}, bf16[4,3,128,128]{3,2,1,0:T(8,128)(2,1)}, u32[]{:S(2)}) copy-start(bf16[4,3,128,128]{3,2,1,0:T(8,128)(2,1)} %refs_5_.1) | copy-start | bytes 1179652

commit v6 on v5

--- a/solution.py
+++ b/solution.py
@@ -277,7 +277,7 @@
     )
 
     def wide(n_kinds):
-        return (n_kinds * gc * (height + PAD), LANES)
+        return (n_kinds * gc * (height + PAD) + height, LANES)
 
     own_operator, rest = call(
         functools.partial(own_operator_kernel, n_grp, n_row, cl_dev),
@@ -365,27 +365,27 @@
     late_places = places_y[half:]
     other_c = lax.ppermute(over_ya, "grp", others)
     other_e = across_row(other_a, 2)
+    plan = [
+        (0, 0, 2, early_places),
+        (0, 0, 3, late_places),
+        (1, pairs_kind, 4, places[:half]),
+        (1, pairs_kind, 5, places_y[:half]),
+    ]
     own_far = call(
-        functools.partial(far_kernel, [(0, 0, 1, early_places)], pairs_piece, False),
+        functools.partial(far_kernel, plan, pairs_piece, False),
         [((height, LANES), F32)],
         own_operator,
-        *held(early_part),
+        side_operator,
+        *held(early_part, over_yb, other_a, other_c),
     )
     partner = lax.ppermute(packed(early_part, over_yb, along), "grp", partners)
 
-    plan = [
-        (0, 0, 2, late_places),
-        (1, pairs_kind, 3, places[:half]),
-        (1, 0, 4, early_places + late_places),
-        (1, pairs_kind, 5, places_y[:half]),
-        (1, pairs_kind, 6, places[half:]),
-    ]
+    plan = [(0, 0, 1, early_places + late_places), (0, pairs_kind, 2, places[half:])]
     far = call(
         functools.partial(far_kernel, plan, pairs_piece, True),
         [((height, LANES), F32)],
-        own_operator,
         side_operator,
-        *held(over_yb, other_a, partner, other_c, other_e),
+        *held(partner, other_e),
         own_far,
     )
     return pl.pallas_call(

time: 28.8 us -> 28.5 us (0.990)
  the two profiles are of different devices: /device:TPU:0 before, /device:TPU:1 now
where the time goes in v6:
time: 28.5 us; the launch traced here: 28.1 us
  starting transfers between devices  14.6 us (51%)
  Pallas kernels  6.71 us (24%)
  waiting for transfers between devices  6.52 us (23%)
    ppermute x6, starting transfers between devices, across_row(): return lax.ppermute(value, 'row', [(i, i ^ bit) for i in range(n_row)])  7.17 us
    pallas_call x6, Pallas kernels, call(): pl.pallas_call(kernel, out_shape=shapes[0] if single else shapes, in_spec...  5.59 us
    ppermute x6, waiting for transfers between devices, across_row(): return lax.ppermute(value, 'row', [(i, i ^ bit) for i in range(n_row)])  5.53 us
    ppermute x1, starting transfers between devices, per_device(): partner = lax.ppermute(packed(early_part, over_yb, along), 'grp', partners)  3.5 us
    ppermute x1, starting transfers between devices, per_device(): other_b = lax.ppermute(packed(panel[size:], along), ('grp', 'row'), leaps)  1.52 us
    ppermute x1, starting transfers between devices, per_device(): other_a = lax.ppermute(first_half, 'grp', others)  1.18 us
    ppermute x1, starting transfers between devices, per_device(): other_c = lax.ppermute(over_ya, 'grp', others)  1.18 us
    pallas_call x1, Pallas kernels, per_device(): pl.pallas_call(functools.partial(final_kernel, [(0, pairs_kind, 1, late_p...  1.12 us
  transfers between devices with their start and end apart: 10, of which 4 were waited for; matrix products, arithmetic and copies ran while one was open for 0% of the time, Pallas kernels for 16%

profile of v6, /device:TPU:1, one launch (start us, length us, event | category | flops | bytes accessed | tf_op | source)
XLA Modules:
  0.0 28.1 jit_solution(4425036420530366289)
XLA Ops:
  0.0 1.1 %shard_map.73 = (bf16[4,64,128]{2,1,0:T(8,128)(2,1)S(1)}, bf16[4,64,128]{2,1,0:T(8,128)(2,1)S(1)}, s32[1,192]{1,0:T(1,128)S(1)}, s32[1,192]{1,0:T(1,128)S(1)}, s...) custom-call(bf16[4,64,128]{2,1,0:T(8,128)(2,1)} %refs_0_.1, ...), custom_call_target="tpu_custom_call" | custom-call | tf_op jit(solution)/shard_map/pallas_call | solution.py:36
  1.2 3.2 %collective-permute-start.3 = (bf16[128,128]{1,0:T(8,128)(2,1)S(1)}, bf16[128,128]{1,0:T(8,128)(2,1)S(1)}, u32[]{:S(2)}, u32[]{:S(2)}) collective-permute-start(bf16[128,128]{1,0:T(8,128)(2,1)S(1)} %get-tuple-element.21), channel_id=1, source_target_pairs={{0,4},{1,5},{2,6},{3,7},{4,0},{5,1},{6,2},{7,3},{8,12},{9,13},{10,... | collective-permute-start | bytes 98312 | tf_op jit(solution)/shard_map/ppermute | solution.py:259
  4.4 1.4 %collective-permute-start = (bf16[192,128]{1,0:T(8,128)(2,1)S(1)}, bf16[192,128]{1,0:T(8,128)(2,1)S(1)}, u32[]{:S(2)}, u32[]{:S(2)}) collective-permute-start(bf16[192,128]{1,0:T(8,128)(2,1)S(1)} %constant_dynamic-update-slice_fusion), channel_id=1, source_target_pairs={{0,2},{1,3},{2,0},{3,1},{4,6},{5,7},{6,4},{7,5},{8,10},{9,11},{10,... | collective-permute-start | bytes 147464 | tf_op jit(solution)/shard_map/ppermute | solution.py:259
  5.7 0.0 collective-permute-start.1
  5.7 0.0 collective-permute-done.3
  5.8 1.3 %collective-permute-start.4 = (bf16[320,128]{1,0:T(8,128)(2,1)S(1)}, bf16[320,128]{1,0:T(8,128)(2,1)S(1)}, u32[]{:S(2)}, u32[]{:S(2)}) collective-permute-start(bf16[320,128]{1,0:T(8,128)(2,1)S(1)} %pad_maximum_fusion.1), channel_id=1, source_target_pairs={{0,1},{1,0},{2,3},{3,2},{4,5},{5,4},{6,7},{7,6},{8,9},{9,8},{10,11... | collective-permute-start | bytes 245768 | tf_op jit(solution)/shard_map/ppermute | solution.py:259
  7.1 0.3 %collective-permute-done = bf16[192,128]{1,0:T(8,128)(2,1)S(1)} collective-permute-done((bf16[192,128]{1,0:T(8,128)(2,1)S(1)}, bf16[192,128]{1,0:T(8,128)(2,1)S(1)}, u32[]{:S(2)}, u32[]{:S(2)}) %collective-permute-start) | collective-permute-done | bytes 49184 | tf_op jit(solution)/shard_map/ppermute | solution.py:259
  7.4 3.2 %collective-permute-done.1 = bf16[192,128]{1,0:T(8,128)(2,1)S(1)} collective-permute-done((bf16[192,128]{1,0:T(8,128)(2,1)S(1)}, bf16[192,128]{1,0:T(8,128)(2,1)S(1)}, u32[]{:S(2)}, u32[]{:S(2)}) %collective-permute-start.1) | collective-permute-done | bytes 49184 | tf_op jit(solution)/shard_map/ppermute | solution.py:259
  10.6 1.3 %collective-permute-start.5 = (bf16[320,128]{1,0:T(8,128)(2,1)S(1)}, bf16[320,128]{1,0:T(8,128)(2,1)S(1)}, u32[]{:S(2)}, u32[]{:S(2)}) collective-permute-start(bf16[320,128]{1,0:T(8,128)(2,1)S(1)} %pad_maximum_fusion), channel_id=1, source_target_pairs={{0,1},{1,0},{2,3},{3,2},{4,5},{5,4},{6,7},{7,6},{8,9},{9,8},{10,11... | collective-permute-start | bytes 245768 | tf_op jit(solution)/shard_map/ppermute | solution.py:259
  11.9 0.0 collective-permute-done.4
  12.0 2.0 %collective-permute-done.5 = bf16[320,128]{1,0:T(8,128)(2,1)S(1)} collective-permute-done((bf16[320,128]{1,0:T(8,128)(2,1)S(1)}, bf16[320,128]{1,0:T(8,128)(2,1)S(1)}, u32[]{:S(2)}, u32[]{:S(2)}) %collective-permute-start.5) | collective-permute-done | bytes 81952 | tf_op jit(solution)/shard_map/ppermute | solution.py:259
  14.0 3.5 %collective-permute-start.6 = (bf16[1088,128]{1,0:T(8,128)(2,1)S(1)}, bf16[1088,128]{1,0:T(8,128)(2,1)S(1)}, u32[]{:S(2)}, u32[]{:S(2)}) collective-permute-start(bf16[1088,128]{1,0:T(8,128)(2,1)S(1)} %constant_dynamic-update-slice_fusion.2), channel_id=1, source_target_pairs={{0,8},{8,0},{16,24},{24,16},{1,9},{9,1},{17,25},{25,17},{2,10},{10... | collective-permute-start | bytes 835592 | tf_op jit(solution)/shard_map/ppermute | solution.py:381
  17.5 1.2 %collective-permute-start.7 = (bf16[256,128]{1,0:T(8,128)(2,1)S(1)}, bf16[256,128]{1,0:T(8,128)(2,1)S(1)}, u32[]{:S(2)}, u32[]{:S(2)}) collective-permute-start(bf16[256,128]{1,0:T(8,128)(2,1)S(1)} %pad_maximum_fusion.2), channel_id=1, source_target_pairs={{0,24},{8,16},{16,8},{24,0},{1,25},{9,17},{17,9},{25,1},{2,26},{10... | collective-permute-start | bytes 196616 | tf_op jit(solution)/shard_map/ppermute | solution.py:351
  18.7 1.5 %collective-permute-start.2 = (bf16[320,128]{1,0:T(8,128)(2,1)S(1)}, bf16[320,128]{1,0:T(8,128)(2,1)S(1)}, u32[]{:S(2)}, u32[]{:S(2)}) collective-permute-start(bf16[320,128]{1,0:T(8,128)(2,1)S(1)} %pad_maximum_fusion), channel_id=1, source_target_pairs={{0,25},{1,24},{2,27},{3,26},{4,29},{5,28},{6,31},{7,30},{8,17},{9,... | collective-permute-start | bytes 245768 | tf_op jit(solution)/shard_map/ppermute | solution.py:361
  20.2 1.2 %collective-permute-start.9 = (bf16[256,128]{1,0:T(8,128)(2,1)S(1)}, bf16[256,128]{1,0:T(8,128)(2,1)S(1)}, u32[]{:S(2)}, u32[]{:S(2)}) collective-permute-start(bf16[256,128]{1,0:T(8,128)(2,1)S(1)} %get-tuple-element.29), channel_id=1, source_target_pairs={{0,24},{8,16},{16,8},{24,0},{1,25},{9,17},{17,9},{25,1},{2,26},{10... | collective-permute-start | bytes 196616 | tf_op jit(solution)/shard_map/ppermute | solution.py:366
  21.4 0.0 collective-permute-done.7.refs_4_
  21.4 0.0 collective-permute-start.8
  21.4 0.0 copy-start
  21.4 1.8 %shard_map.74 = (bf16[16,128,256]{2,1,0:T(8,128)(2,1)S(1)}, bf16[128,4096]{1,0:T(8,128)(2,1)S(1)}) custom-call(s32[1,192]{1,0:T(1,128)S(1)} %get-tuple-element.17.cols_ref, s32[1,192]{1,0:T(1,128)S(1)} %get-tuple-element.18.rows_ref, s32[1,192]{1,0:T(1,128)S(1)} %get-tuple-element.19.live_ref, bf16[192,4096]{1,0:T(8,128)(2,1)} %coupling_ref.1), custom_call_target="tpu_custom_call" | custom-call | tf_op jit(solution)/shard_map/pallas_call | solution.py:36
  23.2 1.1 %shard_map.75.refs_1_.refs_0_ = bf16[32,128,256]{2,1,0:T(8,128)(2,1)S(1)} custom-call(s32[1,192]{1,0:T(1,128)S(1)} %get-tuple-element.17.cols_ref, s32[1,192]{1,0:T(1,128)S(1)} %get-tuple-element.18.rows_ref, s32[1,192]{1,0:T(1,128)S(1)} %get-tuple-element.19.live_ref, bf16[128,4096]{1,0:T(8,128)(2,1)S(1)} %get-tuple-element.20.rest_ref), custom_call_target="tpu_custom_call" | custom-call | tf_op jit(solution)/shard_map/pallas_call | solution.py:36
  24.3 0.0 copy-done
  24.3 0.4 %shard_map.78 = (f32[64,512]{1,0:T(8,128)S(1)}, bf16[256,512]{1,0:T(8,128)(2,1)S(1)}) custom-call(bf16[4,64,128]{2,1,0:T(8,128)(2,1)S(1)} %get-tuple-element.25.signal_ref, bf16[4,3,128,128]{3,2,1,0:T(8,128)(2,1)S(1)} %copy-done, bf16[4,64,128]{2,1,0:T(8,128)(2,1)S(1)} %get-tuple-element.26.basis_ref), custom_call_target="tpu_custom_call" | custom-call | tf_op jit(solution)/shard_map/pallas_call | solution.py:36
  24.7 1.0 %collective-permute-done.9.refs_5_ = bf16[256,128]{1,0:T(8,128)(2,1)S(1)} collective-permute-done((bf16[256,128]{1,0:T(8,128)(2,1)S(1)}, bf16[256,128]{1,0:T(8,128)(2,1)S(1)}, u32[]{:S(2)}, u32[]{:S(2)}) %collective-permute-start.9) | collective-permute-done | bytes 65568 | tf_op jit(solution)/shard_map/ppermute | solution.py:366
  25.7 0.6 %shard_map.76.refs_3_ = f32[128,128]{1,0:T(8,128)S(1)} custom-call(bf16[16,128,256]{2,1,0:T(8,128)(2,1)S(1)} %get-tuple-element.24.refs_0_, bf16[32,128,256]{2,1,0:T(8,128)(2,1)S(1)} %shard_map.75.refs_1_.refs_0_, bf16[768,128]{1,0:T(8,128)(2,1)S(1)} %get-tuple-element.31.refs_2_, bf16[256,128]{1,0:T(8,128)(2,1)S(1)} %slice.43.refs_3_, ...), custom_call_target="tpu_custom_call" | custom-call | tf_op jit(solution)/shard_map/pallas_call | solution.py:36
  26.3 0.0 collective-permute-done.8.refs_2_
  26.4 0.0 collective-permute-done.6.refs_1_.refs_2_
  26.4 0.6 %shard_map.77.refs_6_ = f32[128,128]{1,0:T(8,128)S(1)} custom-call(bf16[32,128,256]{2,1,0:T(8,128)(2,1)S(1)} %shard_map.75.refs_1_.refs_0_, bf16[1088,128]{1,0:T(8,128)(2,1)S(1)} %collective-permute-done.6.refs_1_.refs_2_, bf16[256,128]{1,0:T(8,128)(2,1)S(1)} %collective-permute-done.8.refs_2_, f32[128,128]{1,0:T(8,128)S(1)} %shard_map.76.refs_3_), custom_call_target="tpu_custom_call" | custom-call | tf_op jit(solution)/shard_map/pallas_call | solution.py:36
  26.9 0.0 collective-permute-done.2.refs_1_
  27.0 1.1 %final.1 = bf16[4,64,128]{2,1,0:T(8,128)(2,1)} custom-call(bf16[32,128,256]{2,1,0:T(8,128)(2,1)S(1)} %shard_map.75.refs_1_.refs_0_, bf16[320,128]{1,0:T(8,128)(2,1)S(1)} %collective-permute-done.2.refs_1_, bf16[1088,128]{1,0:T(8,128)(2,1)S(1)} %collective-permute-done.6.refs_1_.refs_2_, bf16[64,128]{1,0:T(8,128)(2,1)S(1)} %slice.41.refs_3_, ...), custom_call_target="tpu_custom_call" | custom-call | tf_op jit(solution)/shard_map/final/pallas_call | solution.py:391
  (14 shorter events, 0.1 us)
Async XLA Ops:
  1.2 4.6 %collective-permute-start.3 = (bf16[128,128]{1,0:T(8,128)(2,1)S(1)}, bf16[128,128]{1,0:T(8,128)(2,1)S(1)}, u32[]{:S(2)}, u32[]{:S(2)}) collective-permute-start(bf16[128,128]{1,0:T(8,128)(2,1)S(1)} %get-tuple-element.21), channel_id=1, source_target_pairs={{0,4},{1,5},{2,6},{3,7},{4,0},{5,1},{6,2},{7,3},{8,12},{9,13},{10,... | collective-permute-start | bytes 98312 | tf_op jit(solution)/shard_map/ppermute | solution.py:259
  4.4 3.0 %collective-permute-start = (bf16[192,128]{1,0:T(8,128)(2,1)S(1)}, bf16[192,128]{1,0:T(8,128)(2,1)S(1)}, u32[]{:S(2)}, u32[]{:S(2)}) collective-permute-start(bf16[192,128]{1,0:T(8,128)(2,1)S(1)} %constant_dynamic-update-slice_fusion), channel_id=1, source_target_pairs={{0,2},{1,3},{2,0},{3,1},{4,6},{5,7},{6,4},{7,5},{8,10},{9,11},{10,... | collective-permute-start | bytes 147464 | tf_op jit(solution)/shard_map/ppermute | solution.py:259
  5.7 4.8 %collective-permute-start.1 = (bf16[192,128]{1,0:T(8,128)(2,1)S(1)}, bf16[192,128]{1,0:T(8,128)(2,1)S(1)}, u32[]{:S(2)}, u32[]{:S(2)}) collective-permute-start(bf16[192,128]{1,0:T(8,128)(2,1)S(1)} %constant_dynamic-update-slice_fusion), channel_id=1, source_target_pairs={{0,6},{1,7},{2,4},{3,5},{4,2},{5,3},{6,0},{7,1},{8,14},{9,15},{10,... | collective-permute-start | bytes 147464 | tf_op jit(solution)/shard_map/ppermute | solution.py:259
  5.8 6.2 %collective-permute-start.4 = (bf16[320,128]{1,0:T(8,128)(2,1)S(1)}, bf16[320,128]{1,0:T(8,128)(2,1)S(1)}, u32[]{:S(2)}, u32[]{:S(2)}) collective-permute-start(bf16[320,128]{1,0:T(8,128)(2,1)S(1)} %pad_maximum_fusion.1), channel_id=1, source_target_pairs={{0,1},{1,0},{2,3},{3,2},{4,5},{5,4},{6,7},{7,6},{8,9},{9,8},{10,11... | collective-permute-start | bytes 245768 | tf_op jit(solution)/shard_map/ppermute | solution.py:259
  10.6 3.4 %collective-permute-start.5 = (bf16[320,128]{1,0:T(8,128)(2,1)S(1)}, bf16[320,128]{1,0:T(8,128)(2,1)S(1)}, u32[]{:S(2)}, u32[]{:S(2)}) collective-permute-start(bf16[320,128]{1,0:T(8,128)(2,1)S(1)} %pad_maximum_fusion), channel_id=1, source_target_pairs={{0,1},{1,0},{2,3},{3,2},{4,5},{5,4},{6,7},{7,6},{8,9},{9,8},{10,11... | collective-permute-start | bytes 245768 | tf_op jit(solution)/shard_map/ppermute | solution.py:259
  14.0 12.3 %collective-permute-start.6 = (bf16[1088,128]{1,0:T(8,128)(2,1)S(1)}, bf16[1088,128]{1,0:T(8,128)(2,1)S(1)}, u32[]{:S(2)}, u32[]{:S(2)}) collective-permute-start(bf16[1088,128]{1,0:T(8,128)(2,1)S(1)} %constant_dynamic-update-slice_fusion.2), channel_id=1, source_target_pairs={{0,8},{8,0},{16,24},{24,16},{1,9},{9,1},{17,25},{25,17},{2,10},{10... | collective-permute-start | bytes 835592 | tf_op jit(solution)/shard_map/ppermute | solution.py:381
  17.5 3.9 %collective-permute-start.7 = (bf16[256,128]{1,0:T(8,128)(2,1)S(1)}, bf16[256,128]{1,0:T(8,128)(2,1)S(1)}, u32[]{:S(2)}, u32[]{:S(2)}) collective-permute-start(bf16[256,128]{1,0:T(8,128)(2,1)S(1)} %pad_maximum_fusion.2), channel_id=1, source_target_pairs={{0,24},{8,16},{16,8},{24,0},{1,25},{9,17},{17,9},{25,1},{2,26},{10... | collective-permute-start | bytes 196616 | tf_op jit(solution)/shard_map/ppermute | solution.py:351
  18.7 8.2 %collective-permute-start.2 = (bf16[320,128]{1,0:T(8,128)(2,1)S(1)}, bf16[320,128]{1,0:T(8,128)(2,1)S(1)}, u32[]{:S(2)}, u32[]{:S(2)}) collective-permute-start(bf16[320,128]{1,0:T(8,128)(2,1)S(1)} %pad_maximum_fusion), channel_id=1, source_target_pairs={{0,25},{1,24},{2,27},{3,26},{4,29},{5,28},{6,31},{7,30},{8,17},{9,... | collective-permute-start | bytes 245768 | tf_op jit(solution)/shard_map/ppermute | solution.py:361
  20.2 5.5 %collective-permute-start.9 = (bf16[256,128]{1,0:T(8,128)(2,1)S(1)}, bf16[256,128]{1,0:T(8,128)(2,1)S(1)}, u32[]{:S(2)}, u32[]{:S(2)}) collective-permute-start(bf16[256,128]{1,0:T(8,128)(2,1)S(1)} %get-tuple-element.29), channel_id=1, source_target_pairs={{0,24},{8,16},{16,8},{24,0},{1,25},{9,17},{17,9},{25,1},{2,26},{10... | collective-permute-start | bytes 196616 | tf_op jit(solution)/shard_map/ppermute | solution.py:366
  21.4 4.9 %collective-permute-start.8 = (bf16[256,128]{1,0:T(8,128)(2,1)S(1)}, bf16[256,128]{1,0:T(8,128)(2,1)S(1)}, u32[]{:S(2)}, u32[]{:S(2)}) collective-permute-start(bf16[256,128]{1,0:T(8,128)(2,1)S(1)} %collective-permute-done.7.refs_4_), channel_id=1, source_target_pairs={{0,2},{1,3},{2,0},{3,1},{4,6},{5,7},{6,4},{7,5},{8,10},{9,11},{10,... | collective-permute-start | bytes 196616 | tf_op jit(solution)/shard_map/ppermute | solution.py:259
  21.4 2.9 %copy-start = (bf16[4,3,128,128]{3,2,1,0:T(8,128)(2,1)S(1)}, bf16[4,3,128,128]{3,2,1,0:T(8,128)(2,1)}, u32[]{:S(2)}) copy-start(bf16[4,3,128,128]{3,2,1,0:T(8,128)(2,1)} %refs_5_.1) | copy-start | bytes 1179652
